TPU v7x, 32 devices: a whole 2x2x4 slice. The times are simulated.
32 devices in a mesh: dp: 4 (over y, x), fs: 8 (over z, core).
Axes of the slice: x: 2, y: 2, z: 4, core: 2. Of those that a mesh axis runs over, the one named last changes fastest.
Arguments:
- tokens: bfloat16 [32, 320, 1024], P(('dp', 'fs')), may hold values from -6 to 6
- image_side: int32 [32], P(('dp', 'fs')), may hold values from 16 to 32, as said below
- cotangent: bfloat16 [32, 512, 256], P(('dp', 'fs')), may hold values from -26 to 26
- query_weight: bfloat16 [102400], P(('dp', 'fs')), may hold values from -0.3125 to 0.3125
- keyval_weight: bfloat16 [204800], P(('dp', 'fs')), may hold values from -0.3125 to 0.3125
- reduce_weight: bfloat16 [409600], P(('dp', 'fs')), may hold values from -0.15625 to 0.15625
- output_weight: bfloat16 [102400], P(('dp', 'fs')), may hold values from -2.5 to 2.5
- expand_weight: bfloat16 [409600], P(('dp', 'fs')), may hold values from -0.3125 to 0.3125
- depth_weight: bfloat16 [11520], P(('dp', 'fs')), may hold values from -2 to 2
- contract_weight: bfloat16 [409600], P(('dp', 'fs')), may hold values from -0.15625 to 0.15625
- merge_weight: bfloat16 [1474560], P(('dp', 'fs')), may hold values from -0.109375 to 0.109375
- norm_gains: bfloat16 [1792], P(('dp', 'fs')), may hold values from 0.25 to 1.75
- all_biases: bfloat16 [6144], P(('dp', 'fs')), may hold values from -3 to 3
Outputs:
- section_four: bfloat16 [32, 512, 256], P(('dp', 'fs'))
- token_grad: float32 [32, 320, 1024], P(('dp', 'fs'))
- query_grad: float32 [102400], P(('dp', 'fs'))
- keyval_grad: float32 [204800], P(('dp', 'fs'))
- reduce_grad: float32 [409600], P(('dp', 'fs'))
- output_grad: float32 [102400], P(('dp', 'fs'))
- expand_grad: float32 [409600], P(('dp', 'fs'))
- depth_grad: float32 [11520], P(('dp', 'fs'))
- contract_grad: float32 [409600], P(('dp', 'fs'))
- merge_grad: float32 [1474560], P(('dp', 'fs'))
- gains_grad: float32 [1792], P(('dp', 'fs'))
- biases_grad: float32 [6144], P(('dp', 'fs'))
Inputs may be any that keep to these rules, and one draw needn't show every extreme that they name: `image_side`: each frame holds one square image in its top left corner with side 32, 16, or 0 for an empty frame; the first of each device's 1 frames always holds an image.
All inputs are finite; a program needn't handle non-finite values.
Results may differ from a plain program's by a relative error of at most 0.014.
Values may be sent and summed in bfloat16 or wider, within the bound.
No kernel may reach another device: no remote copies, remote signals or barrier semaphores. Data moves between devices by JAX's collectives and lax.ppermute only.
A program may use at most 256 MiB of HBM per device.

v0:
```python
import functools

import jax
import jax.numpy as jnp
import numpy as np
from jax import lax
from jax.experimental import pallas as pl
from jax.experimental.pallas import tpu as pltpu
from jax.sharding import PartitionSpec as P


D = 320
HEADS = 5
FF = 1280
OUT_D = 512
SIDE = 32
QUARTER = 256
TOKENS = SIDE * SIDE
MERGE_PAD = 2944
SUPER = 32
FLIPS = (2, 4, 8, 16)
EPS = 1e-06
F32, BF16, I32 = jnp.float32, jnp.bfloat16, jnp.int32

B_Q, B_R, C_R, B_O, C_1, C_2, B_1, B_DW, B_2, C_S, B_M, C_M = 0, 5, 10, 15, 20, 25, 30, 50, 70, 75, 80, 88
G_R, G_1, G_2, G_S, G_M = 96, 101, 106, 111, 116

PARTS = ((0, 1), (1, 4))
A_ROWS, B_ROWS, C_ROWS = 208, 224, 368
SMALL_ROW = 200
A_SPLIT = 104
VMEM_LIMIT = 24 * 1024 * 1024
VMEM_ALL = 60 * 1024 * 1024


def slot_of(xor):
    return (xor >> 1) | ((xor & 1) << 4)


def xor_of(slot):
    return ((slot & 15) << 1) | (slot >> 4)


def dot(a, b):
    return jnp.dot(a, b, preferred_element_type=F32)


def dot_nt(a, b):
    return lax.dot_general(a, b, (((1,), (1,)), ((), ())), preferred_element_type=F32)


def dot_tn(a, b):
    return lax.dot_general(a, b, (((0,), (0,)), ((), ())), preferred_element_type=F32)


def iota(shape, axis):
    return lax.broadcasted_iota(I32, shape, axis)


def one_hot(test):
    return jnp.where(test, 1.0, 0.0).astype(BF16)


def lanes(index, width=128):
    return pl.ds(pl.multiple_of(index * width, width), width)


def loop(count, body):
    def step(index, carry):
        body(index)
        return carry

    lax.fori_loop(0, count, step, 0)


def column(table, start, count):
    return jnp.concatenate(
        [jnp.broadcast_to(table[:, h : h + 1], (64, 128)) for h in range(start, start + count)], axis=0
    )


def put_column(table, start, values):
    for h in range(values.shape[0] // 64):
        table[:, start + h : start + h + 1] = values[64 * h : 64 * h + 64, 0:1]


def token_place(lane):
    quad = lane >> 8
    row = 2 * ((lane >> 4) & 15) + (quad >> 1)
    col = 2 * (lane & 15) + (quad & 1)
    return row, col


def token_mask(tile, side, width=128):
    row, col = token_place(iota((1, width), 1) + tile * width)
    return jnp.where((row < side) & (col < side), 1.0, 0.0)


def key_place(index):
    return index >> 4, index & 15


def select_kernel(count, bases, small, small_at, *refs):
    sources, refs = refs[:count], refs[count:]
    if small:
        scal, biases, gains = refs[:3]
        refs = refs[3:]
    low_ref, high_ref, out, rows_ref, sems = refs[:5]
    held = refs[5:]
    copies = [
        pltpu.make_async_copy(source, place, sems.at[n]) for n, (source, place) in enumerate(zip(sources, held))
    ]
    for copy in copies:
        copy.start()
    half = rows_ref.shape[0] // 2
    rows_ref[...] = jnp.zeros_like(rows_ref)
    place = iota((out.shape[0], 2 * half), 1)
    pick_low = one_hot(place == low_ref[...])
    pick_high = one_hot(place == high_ref[...])
    for copy in copies:
        copy.wait()
    for source, base in zip(held, bases):
        rows_ref[base : base + source.shape[0], :] = source[...].astype(F32)
    if small:
        rows_ref[small_at : small_at + 1, :] = biases[:, 0:128].astype(F32)
        rows_ref[small_at + 1 : small_at + 2, 0:64] = biases[:, 128:192].astype(F32)
        wide = jnp.concatenate([gains[...].astype(F32), jnp.zeros((1, 72), F32)], axis=1)
        wide = jnp.broadcast_to(wide, (8, 128))
        rows_ref[small_at + 2 : small_at + 3, :] = pltpu.roll(wide, (56 * scal[0]) & 63, 1)[0:1, :]
    rows_ref[half:, :] = pltpu.roll(rows_ref[0:half, :], 64, 1)
    total = rows_ref[...].astype(BF16)
    low, upper = dot(pick_low, total), dot(pick_high, total)
    out[...] = jnp.where(iota((out.shape[0], 128), 1) < 64, low, upper).astype(BF16)


def select(sources, table, rows, vectors=()):
    bases, at = [], 0
    for source in sources:
        bases.append(at)
        at += -(-source.shape[0] // 16) * 16
    small = len(vectors) > 0
    half = at + (16 if small else 0)
    low, high = table(bases + [at], half).astype(np.int32)[:, :, None]
    specs = [pl.BlockSpec(memory_space=pltpu.HBM)] * len(sources)
    if small:
        specs += [pl.BlockSpec(memory_space=pltpu.SMEM)] + [pl.BlockSpec(memory_space=pltpu.VMEM)] * 2
    specs += [pl.BlockSpec(memory_space=pltpu.VMEM)] * 2
    return pl.pallas_call(
        functools.partial(select_kernel, len(sources), tuple(bases), small, at),
        in_specs=specs,
        out_shape=jax.ShapeDtypeStruct((rows, 128), BF16),
        scratch_shapes=[pltpu.VMEM((2 * half, 128), F32), pltpu.SemaphoreType.DMA((len(sources),))]
        + [pltpu.VMEM(source.shape, source.dtype) for source in sources],
        compiler_params=pltpu.CompilerParams(vmem_limit_bytes=VMEM_ALL if small else VMEM_LIMIT),
        cost_estimate=cost(2),
    )(*sources, *vectors, low, high)


def pair(half, low_src, high_src):
    low = -1 if low_src is None else low_src[0] + low_src[1] // 2 + half * (low_src[1] % 2)
    high = -1 if high_src is None else high_src[0] + high_src[1] // 2 + half * (1 - high_src[1] % 2)
    return low, high


def chunk_sources(bases, row, c):
    q, o, kv = bases
    if c < 6 or c >= 8:
        base, first = ((q, 0), (kv, 0), (kv, 10), None, (o, 0))[c // 2]
        at = 5 * (first + row) + 2 * (c % 2)
        return (base, at), (base, at + 1)
    if c == 6:
        return (q, 5 * row + 4), (kv, 5 * row + 4)
    return (kv, 5 * (10 + row) + 4), (o, 5 * row + 4)


def a_place(kind, row, c):
    if row < 8:
        return 16 * c + 8 * kind + row
    return 160 + 8 * (c // 2) + 4 * kind + 2 * (c % 2) + row - 8


def b_place(row, c):
    if row < 8:
        return 8 * c + row
    return 80 + 8 * (c // 4) + 2 * (c % 4) + row - 8


def table_a(bases, half):
    q, o, kv, r, small = bases
    rows = [(-1, -1)] * A_ROWS
    for c in range(10):
        for row in range(10):
            at = 20 * row + 2 * c
            rows[a_place(0, row, c)] = pair(half, (r, at), (r, at + 1))
            rows[a_place(1, row, c)] = pair(half, *chunk_sources((q, o, kv), row, c))
    for row in range(3):
        rows[SMALL_ROW + row] = pair(half, (small, 2 * row), (small, 2 * row + 1))
    return np.array(rows).T


def table_b(bases, half):
    w2, w1, dw, _ = bases
    rows = [(-1, -1)] * B_ROWS
    for c in range(10):
        for row in range(10):
            at = 20 * row + 2 * c
            rows[b_place(row, c)] = pair(half, (w2, at), (w2, at + 1))
    for c in range(3):
        for row in range(40):
            at = 5 * row + 2 * c
            rows[104 + 40 * c + row] = pair(half, (w1, at), (w1, at + 1) if c < 2 else (dw, 2 * row + 1))
    return np.array(rows).T


def table_c(bases, half):
    m, _ = bases
    rows = []
    for c in range(23):
        for row in range(16):
            at = 45 * row + 2 * c
            rows.append(pair(half, (m, at), (m, at + 1) if c < 22 else None))
    return np.array(rows).T


def turn(rows):
    return pltpu.roll(rows, 64, 1)


def halves(low, high):
    return jnp.where(iota((1, 128), 1) < 64, low, high)


def put_rows(out, first, count, stride, rows):
    out[pl.ds(first, count, stride=stride), :] = rows


def put_320(out, first, count, load):
    even, odd = ([load(chunk, parity) for chunk in range(3)] for parity in range(2))
    turned = [turn(rows) for rows in odd]
    for at, rows in enumerate(
        (even[0], even[1], halves(even[2], turned[0]), halves(turned[0], turned[1]), halves(turned[1], turned[2]))
    ):
        put_rows(out, first + at, count // 2, 5, rows)


def every_other(ref, start, count):
    return ref[pl.ds(start, count, stride=2), :]


def out_a_kernel(scal, sums, q, o, kv, r, biases, gains):
    squares = (
        (q, 0, (0, 1, 6), False),
        (o, 0, (8, 9, 7), True),
        (kv, 0, (2, 3, 6), True),
        (kv, 25, (4, 5, 7), False),
    )
    for out, first, chunks, high in squares:
        for start, count, lane_row in ((0, 8, 0), (8, 2, 20)):

            def load(chunk, parity, chunks=chunks, high=high, start=start, count=count):
                rows = every_other(sums, a_place(1, start, chunks[chunk]) + parity, count // 2)
                return turn(rows) if chunk == 2 and high else rows

            put_320(out, first + lane_row, count, load)
    for c in range(10):
        for start, count in ((0, 8), (8, 2)):
            put_rows(r, 10 * start + c, count, 10, sums[pl.ds(a_place(0, start, c), count), :])
    small = sums[SMALL_ROW : SMALL_ROW + 8, :]
    biases[:, 0:128] = small[0:1]
    biases[:, 128:192] = small[1:2, 0:64]
    gains[...] = pltpu.roll(small, (128 - ((56 * scal[0]) & 63)) & 127, 1)[2:3, 0:56]


def out_b_kernel(scal, sums, w2, w1):
    for c in range(10):
        for start, count in ((0, 8), (8, 2)):
            put_rows(w2, 10 * start + c, count, 10, sums[pl.ds(b_place(start, c), count), :])
    put_320(w1, 0, 40, lambda chunk, parity: every_other(sums, 104 + 40 * chunk + parity, 20))


def out_c_kernel(scal, sums, m):
    even = [every_other(sums, 16 * c, 8) for c in range(23)]
    turned = [turn(every_other(sums, 16 * c + 1, 8)) for c in range(23)]
    for c in range(22):
        put_rows(m, c, 8, 45, even[c])
        put_rows(m, 23 + c, 8, 45, halves(turned[c], turned[c + 1]))
    put_rows(m, 22, 8, 45, halves(even[22], turned[0]))


def split_ten(row, per, magic):
    owner = (row * magic) >> 16
    return owner, row - per * owner


def tens(row, me):
    owner, rest = split_ten(row, 10, 6554)
    slot = slot_of(owner ^ me)
    return jnp.where(rest < 8, slot * 8 + rest, 248 + slot * 2 + rest)


def from_tens(me):
    return one_hot(iota((D, D), 1) == tens(iota((D, 1), 0), me))


def to_tens(me):
    return one_hot(iota((D, D), 0) == tens(iota((1, D), 1), me))


def keyval_tens(row, me, upper):
    owner, rest = split_ten(row, 20, 3277)
    inside = (rest >= 10) if upper else (rest < 10)
    return jnp.where(inside, tens(10 * owner + rest - (10 if upper else 0), me), -1)


def rest_row(row):
    return 64 * ((row & 7) >> 1) + 2 * (row >> 3) + (row & 1)


def norm(values, gain, shift):
    mean = jnp.mean(values, axis=0, keepdims=True)
    centred = values - mean
    rstd = lax.rsqrt(jnp.mean(centred * centred, axis=0, keepdims=True) + EPS)
    return centred * rstd * gain + shift, mean, rstd


def norm_back(grad, hat, rstd, gain):
    scaled = grad * gain
    return rstd * (
        scaled
        - jnp.mean(scaled, axis=0, keepdims=True)
        - hat * jnp.mean(scaled * hat, axis=0, keepdims=True)
    )


def stat_rows(mean, rstd):
    row = iota((8, mean.shape[1]), 0)
    return jnp.where(row == 0, mean, jnp.where(row == 1, rstd, 0.0))


def entry_kernel(scal, tokens, entry, stats):
    side = scal[1]
    for quad in range(4):
        lane = iota((1, 256), 1) + quad * 256
        row, col = token_place(lane)
        natural = row * SIDE + col
        pick = one_hot(iota((TOKENS, 256), 0) == natural)
        mask = jnp.where((row < side) & (col < side), 1.0, 0.0)
        entry[:, quad * 256 : quad * 256 + 256] = (dot(tokens[...], pick) * mask).astype(BF16)

    def body(tile):
        values = entry[:, lanes(tile)].astype(F32)
        mean = jnp.mean(values, axis=0, keepdims=True)
        centred = values - mean
        rstd = lax.rsqrt(jnp.mean(centred * centred, axis=0, keepdims=True) + EPS)
        stats[:, lanes(tile)] = stat_rows(mean, rstd)

    loop(8, body)


def small_table(me, low, high):
    gathered = jnp.concatenate(
        [half[:, SMALL_ROW : SMALL_ROW + 8, :].astype(F32).reshape(128, 128) for half in (low, high)], axis=0
    ).astype(BF16)
    vector = iota((128, 256), 0)
    place = iota((128, 256), 1)
    row = place & 7
    owner = xor_of(place >> 3) ^ me
    first = (7 * owner) >> 3
    straight = (
        ((row == 0) & (vector == 3 * owner))
        | ((row == 1) & (vector == 3 * owner + 2))
        | ((row == 2) & (vector == 96 + first))
    )
    turned = ((row == 0) & (vector == 3 * owner + 1)) | ((row == 2) & (vector == 97 + first))
    rows = dot(one_hot(straight), gathered) + pltpu.roll(dot(one_hot(turned), gathered), 64, 1)
    return jnp.transpose(rows)[0:64, :]


def project_kernel(scal, low, high, entry, stats, wq, wkv, wrs, wo, first, qs, raw, stat_r, red, kv, kt, vt, bt, square, rest, redin):
    me = scal[0]
    bt[...] = small_table(me, low, high)
    for half, source in enumerate((low, high)):

        def chunk(c, half=half, source=source):
            block = source[:, pl.ds(pl.multiple_of(16 * c, 16), 16), :].astype(F32)
            rows = slice(128 * half, 128 * half + 128)
            wrs[rows, lanes(c)] = block[:, 0:8].reshape(128, 128).astype(BF16)
            square[rows, lanes(c)] = block[:, 8:16].reshape(128, 128).astype(BF16)

        loop(10, chunk)
        block = source[:, 160:208, :].astype(F32)
        for c in range(5):
            part = block[:, 8 * c : 8 * c + 8].reshape(128, 128).astype(BF16)
            rest[128 * half : 128 * half + 128, 128 * c : 128 * c + 128] = part
    spread = one_hot(iota((256, 256), 0) == rest_row(iota((1, 256), 1)))

    def last_two(p):
        part = dot(spread, rest[:, lanes(p)]).astype(BF16)
        wrs[256:320, lanes(p, 256)] = jnp.concatenate([part[0:64], part[64:128]], axis=1)
        square[256:320, lanes(p, 256)] = jnp.concatenate([part[128:192], part[192:256]], axis=1)

    loop(5, last_two)
    order = from_tens(me)
    wq[:, 0:256] = dot(order, square[:, 0:256]).astype(BF16)
    wo[:, 0:256] = dot(order, square[:, 1024:1280]).astype(BF16)
    tails = dot(order, square[:, 768:1024])
    wq[:, 256:320] = tails[:, 0:64].astype(BF16)
    wo[:, 256:320] = pltpu.roll(tails, 64, 1)[:, 0:64].astype(BF16)
    row = iota((2 * D, 1), 0)
    place = iota((2 * D, D), 1)
    lower = one_hot(place == keyval_tens(row, me, False))
    upper = one_hot(place == keyval_tens(row, me, True))
    wkv[:, 0:256] = (dot(lower, square[:, 256:512]) + dot(upper, square[:, 512:768])).astype(BF16)
    tail = pltpu.roll(dot(lower, square[:, 768:896]), 64, 1) + dot(upper, square[:, 896:1024])
    wkv[:, 256:320] = tail[:, 0:64].astype(BF16)

    gain, shift = column(bt, G_1, 5), column(bt, C_1, 5)

    def body(tile):
        centred = entry[:, lanes(tile)].astype(F32) - stats[0:1, lanes(tile)]
        first[:, lanes(tile)] = (centred * stats[1:2, lanes(tile)] * gain + shift).astype(BF16)

    loop(8, body)
    for quad in range(4):
        redin[D * quad : D * quad + D, :] = first[:, 256 * quad : 256 * quad + 256]
    bias = column(bt, B_R, 5)
    bias = jnp.concatenate([bias, bias], axis=1)
    mixed = dot(wrs[...], redin[...])
    total = bias
    for part in range(3):
        piece = mixed.astype(BF16)
        total = total + dot(order, piece)
        mixed = mixed - piece.astype(F32)
    raw[...] = total
    gain, shift = column(bt, G_R, 5), column(bt, C_R, 5)
    for tile in range(2):
        at = slice(128 * tile, 128 * tile + 128)
        values, mean, rstd = norm(raw[:, at], gain, shift)
        red[:, at] = values.astype(BF16)
        stat_r[:, at] = stat_rows(mean, rstd)
    keyval = dot(wkv[...], red[...])
    kv[...] = keyval.astype(BF16)
    turned = jnp.transpose(keyval)
    for h in range(HEADS):
        kt[h] = turned[:, 64 * h : 64 * h + 64].astype(BF16)
        vt[h] = turned[:, D + 64 * h : D + 64 * h + 64].astype(BF16)
    bias = column(bt, B_Q, 5)
    bias = jnp.concatenate([bias, bias], axis=1)

    def query(quad):
        at = lanes(quad, 256)
        qs[:, at] = (dot(wq[...], first[:, at]) + bias).astype(BF16) * BF16(0.125)

    loop(4, query)


def key_bias(side):
    i, j = key_place(iota((QUARTER, 1), 0))
    return jnp.where((i < (side >> 1)) & (j < (side >> 1)), 0.0, -10000.0)


def attend_kernel(scal, kt, qs, kv, att, lse, scores, probs):
    bias = key_bias(scal[1])

    def score(h, slot):
        scores[slot] = dot(kt[h], qs[pl.ds(pl.multiple_of(64 * h, 64), 64), :])

    score(0, 0)

    def head(h):
        score(jnp.minimum(h + 1, HEADS - 1), 1 - (h & 1))
        rows = pl.ds(pl.multiple_of(64 * h, 64), 64)
        values = kv[pl.ds(pl.multiple_of(D + 64 * h, 64), 64), :]
        for tile in range(8):
            at = slice(128 * tile, 128 * tile + 128)
            part = scores[h & 1, :, at] + bias
            top = jnp.max(part, axis=0, keepdims=True)
            weights = jnp.exp(part - top)
            total = jnp.sum(weights, axis=0, keepdims=True)
            lse[h, :, at] = top + jnp.log(total)
            probs[:, at] = (weights * (1.0 / total)).astype(BF16)
        att[rows, :] = dot(values, probs[...]).astype(BF16)

    loop(HEADS, head)


def middle_kernel(scal, bt, wo, att, entry, mid, sec, stats, work):
    side = scal[1]
    work[...] = dot(wo[...], att[...])
    bias, gain, shift = column(bt, B_O, 5), column(bt, G_2, 5), column(bt, C_2, 5)

    def body(tile):
        at = lanes(tile)
        mask = token_mask(tile, side)
        values = entry[:, at].astype(F32) + mask * (work[:, at] + bias)
        mid[:, at] = values
        normed, mean, rstd = norm(values, gain, shift)
        stats[:, at] = stat_rows(mean, rstd)
        sec[0:D, at] = (normed.astype(BF16).astype(F32) * mask).astype(BF16)
        sec[D : D + 64, at] = jnp.where(iota((64, 128), 0) == 9, mask, 0.0).astype(BF16)

    loop(8, body)


def ffn_weights_kernel(scal, bt, low, high, w1, w1t, w2, w2t, taps, main, rest, wide):
    me = scal[0]
    for half, source in enumerate((low, high)):
        def chunks(p, half=half, source=source):
            block = source[:, pl.ds(pl.multiple_of(16 * p, 16), 16), :].astype(F32)
            both = jnp.concatenate([block[:, 0:8].reshape(128, 128), block[:, 8:16].reshape(128, 128)], axis=1)
            main[128 * half : 128 * half + 128, lanes(p, 256)] = both.astype(BF16)

        loop(5, chunks)
        block = source[:, 80:112, :].astype(F32)
        for c in range(3):
            part = block[:, 8 * c : 8 * c + 8].reshape(128, 128).astype(BF16)
            rest[128 * half : 128 * half + 128, 128 * c : 128 * c + 128] = part

        def expansion(slot, half=half, source=source):
            owner = ((slot << 1) | half) ^ me
            block = source[slot, 80:224, :].astype(F32)
            rows = pl.ds(pl.multiple_of(40 * owner, 8), 40)
            for c in range(3):
                wide[rows, 128 * c : 128 * c + 128] = block[24 + 40 * c : 64 + 40 * c]

        loop(16, expansion)
    spread = one_hot(iota((256, 256), 0) == rest_row(iota((1, 256), 1)))
    for j in range(3):
        part = dot(spread, rest[:, 128 * j : 128 * j + 128]).astype(BF16)
        for k in range(4 if j < 2 else 2):
            c = 4 * j + k
            main[256:320, 128 * c : 128 * c + 128] = part[64 * k : 64 * k + 64]
    order = from_tens(me)

    def contraction(p):
        block = dot(order, main[:, lanes(p, 256)])
        w2[:, lanes(p, 256)] = block.astype(BF16)
        w2t[pl.ds(pl.multiple_of(256 * p, 256), 256), :] = jnp.transpose(block).astype(BF16)

    loop(5, contraction)
    bias = column(bt, B_1, 20)
    lane = iota((FF, 128), 1)
    tail = wide[:, 256:384]
    low_tail = tail.astype(BF16)

    def spread(tap):
        taps[tap] = dot(low_tail, one_hot(iota((128, 128), 0) == 64 + tap))

    loop(9, spread)
    taps[9] = column(bt, B_DW, 20)
    w1[:, 0:256] = wide[:, 0:256].astype(BF16)
    w1[:, 256:384] = jnp.where(lane < 64, tail, jnp.where(lane == 73, bias, 0.0)).astype(BF16)

    def turn(p):
        rows = pl.ds(pl.multiple_of(256 * p, 256), 256)
        w1t[:, lanes(p, 256)] = jnp.transpose(wide[rows, :])[0:D].astype(BF16)

    loop(5, turn)


def edge_masks():
    lane = iota((1, 128), 1)
    j = lane & 15
    return jnp.where(j != 0, 1.0, 0.0), jnp.where(j != 15, 1.0, 0.0), lane >= 16, lane < 112


def left_of(tiles):
    return [pltpu.roll(tile, 1, 1) for tile in tiles]


def right_of(tiles):
    return [pltpu.roll(tile, 127, 1) for tile in tiles]


def above(tiles, inside):
    turned = [pltpu.roll(tile, 16, 1) for tile in tiles]
    return [jnp.where(inside, turned[0], 0.0), jnp.where(inside, turned[1], turned[0])]


def below(tiles, inside):
    turned = [pltpu.roll(tile, 112, 1) for tile in tiles]
    return [jnp.where(inside, turned[0], turned[1]), jnp.where(inside, turned[1], 0.0)]


def times(tiles, factor):
    return [tile * factor for tile in tiles]


def plus(*many):
    return [functools.reduce(lambda a, b: a + b, tiles) for tiles in zip(*many)]


def tile_at(a, e, half):
    start = 256 * (2 * a + e) + 128 * half
    return slice(start, start + 128)


def quads(ref, rows):
    return [[[ref[rows, tile_at(a, e, half)] for half in range(2)] for e in range(2)] for a in range(2)]


LOG2E = float(np.log2(np.e))


def gelu_parts(x):
    y = x * np.float32(0.5**0.5)
    cdf = lax.erf(y) * 0.5 + 0.5
    bell = jnp.exp2(y * y * np.float32(-LOG2E) + np.float32(-0.5 * np.log2(2.0 * np.pi)))
    return x * cdf, cdf + x * bell


def ffn_kernel(scal, w1, taps, sec, act, slope, hid_a, hid_b):
    j_first, j_last, i_first, i_last = edge_masks()

    def fill(hid, step):
        rows = pl.ds(pl.multiple_of(jnp.minimum(step, FF // 64 - 1) * 64, 64), 64)
        hid[...] = dot(w1[rows, :], sec[...])

    def group(hid, step, index):
        rows = slice(16 * index, 16 * index + 16)
        out_rows = pl.ds(pl.multiple_of(64 * step + 16 * index, 16), 16)
        k = [taps[n, out_rows, :] for n in range(10)]
        first = [k[3 * r] * j_first for r in range(3)]
        last = [k[3 * r + 2] * j_last for r in range(3)]
        quad = quads(hid, rows)
        left = [left_of(quad[a][1]) for a in range(2)]
        right = [right_of(quad[a][0]) for a in range(2)]

        def across(a, e, r):
            if e == 0:
                parts = zip(left[a], quad[a][0], quad[a][1])
                return [first[r] * x + k[3 * r + 1] * y + k[3 * r + 2] * z for x, y, z in parts]
            parts = zip(quad[a][0], quad[a][1], right[a])
            return [k[3 * r] * x + k[3 * r + 1] * y + last[r] * z for x, y, z in parts]

        for e in range(2):
            up = above(across(1, e, 0), i_first)
            down = below(across(0, e, 2), i_last)
            outs = (plus(across(0, e, 1), across(1, e, 2), up), plus(across(0, e, 0), across(1, e, 1), down))
            for a in range(2):
                for half in range(2):
                    value, grad = gelu_parts(outs[a][half] + k[9])
                    act[out_rows, tile_at(a, e, half)] = value.astype(BF16)
                    slope[out_rows, tile_at(a, e, half)] = grad.astype(BF16)

    fill(hid_a, 0)

    def two(index):
        fill(hid_b, 2 * index + 1)
        for n in range(4):
            group(hid_a, 2 * index, n)
        fill(hid_a, 2 * index + 2)
        for n in range(4):
            group(hid_b, 2 * index + 1, n)

    loop(FF // 128, two)


def ending_kernel(scal, bt, w2, act, mid, end, sect, stats, work):
    side = scal[1]
    work[...] = dot(w2[...], act[...])
    bias, gain, shift = column(bt, B_2, 5), column(bt, G_S, 5), column(bt, C_S, 5)

    def body(tile):
        at = lanes(tile)
        mask = token_mask(tile, side)
        values = mid[:, at] + mask * (work[:, at] + bias)
        end[:, at] = values
        normed, mean, rstd = norm(values, gain, shift)
        stats[:, at] = stat_rows(mean, rstd)
        sect[:, at] = (normed.astype(BF16).astype(F32) * mask).astype(BF16)

    loop(8, body)


def lane_sum(values):
    return jnp.sum(values, axis=1, keepdims=True)


def merge_kernel(scal, bt, c_low, c_high, sect, end, stats, cot, four, keep, send, end_grad, branch, grads, wm, patch, mg, back, work, natural):
    me, side = scal[0], scal[1]
    grads[...] = jnp.zeros_like(grads)
    for half, source in enumerate((c_low, c_high)):

        def place(c, half=half, source=source):
            block = source[:, pl.ds(pl.multiple_of(16 * c, 16), 16), :].reshape(256, 128)
            wm[256 * half : 256 * half + 256, lanes(c)] = block

        loop(23, place)

    def reorder(to_owner):
        def one(slot):
            at = pl.ds(pl.multiple_of(16 * slot, 16), 16)
            owner = pl.ds(pl.multiple_of((xor_of(slot) ^ me) * 16, 16), 16)
            to_owner(at, owner)

        loop(32, one)

    j_first, j_last, i_first, i_last = edge_masks()
    quad = [[[t.astype(F32) for t in pair] for pair in row] for row in quads(sect, slice(None))]
    left = [times(left_of(quad[a][1]), j_first) for a in range(2)]
    pieces = (
        above(left[1], i_first),
        above(quad[1][0], i_first),
        above(quad[1][1], i_first),
        left[0],
        quad[0][0],
        quad[0][1],
        left[1],
        quad[1][0],
        quad[1][1],
    )
    for n, piece in enumerate(pieces):
        for half in range(2):
            patch[D * n : D * n + D, 128 * half : 128 * half + 128] = piece[half].astype(BF16)
    patch[9 * D :, :] = jnp.zeros((MERGE_PAD - 9 * D, 256), BF16)
    bias, gain, shift = column(bt, B_M, 8), column(bt, G_M, 8), column(bt, C_M, 8)
    work[...] = dot(wm[...], patch[...])

    def from_slots(at, owner):
        natural[owner, :] = work[at, :]

    reorder(from_slots)
    half_side = side >> 1
    for tile in range(2):
        at = slice(128 * tile, 128 * tile + 128)
        i, j = key_place(iota((1, 128), 1) + 128 * tile)
        mask = jnp.where((i < half_side) & (j < half_side), 1.0, 0.0)
        values = natural[:, at] + bias
        mean = jnp.mean(values, axis=0, keepdims=True)
        centred = values - mean
        rstd = lax.rsqrt(jnp.mean(centred * centred, axis=0, keepdims=True) + EPS)
        hat = centred * rstd
        four[:, at] = ((hat * gain + shift) * mask).astype(BF16)
        grad = cot[:, at].astype(F32) * mask
        low = norm_back(grad, hat, rstd, gain).astype(BF16)
        natural[:, at] = low.astype(F32)
        parts = (grad * hat, grad, low.astype(F32))
        sums = parts if tile == 0 else [s + v for s, v in zip(sums, parts)]
    put_column(grads, G_M, lane_sum(sums[0]))
    put_column(grads, C_M, lane_sum(sums[1]))
    put_column(grads, B_M, lane_sum(sums[2]))

    def to_slots(at, owner):
        mg[at, :] = natural[owner, :].astype(BF16)

    reorder(to_slots)

    def widths(body):
        loop(11, lambda c: body(pl.multiple_of(c * 256, 256), 256))
        body(11 * 256, 128)

    def patch_grad(start, width):
        back[pl.ds(start, width), :] = dot_tn(wm[:, pl.ds(start, width)], mg[...])

    widths(patch_grad)

    def piece(n):
        return [back[D * n : D * n + D, 128 * half : 128 * half + 128] for half in range(2)]

    results = (
        piece(4),
        plus(piece(5), times(right_of(piece(3)), j_last)),
        plus(piece(7), below(piece(1), i_last)),
        plus(
            piece(8),
            times(right_of(piece(6)), j_last),
            below(plus(piece(2), times(right_of(piece(0)), j_last)), i_last),
        ),
    )
    for n, values in enumerate(results):
        for half in range(2):
            end_grad[:, 256 * n + 128 * half : 256 * n + 128 * half + 128] = values[half]
    gain = column(bt, G_S, 5)
    zeros = jnp.zeros((D, 128), F32)

    def body(tile, carry):
        at = lanes(tile)
        mask = token_mask(tile, side)
        grad = end_grad[:, at] * mask
        hat = (end[:, at] - stats[0:1, at]) * stats[1:2, at]
        result = norm_back(grad, hat, stats[1:2, at], gain)
        end_grad[:, at] = result
        low = (result * mask).astype(BF16)
        branch[:, at] = low
        return carry[0] + grad * hat, carry[1] + grad, carry[2] + low.astype(F32)

    sums = lax.fori_loop(0, 8, body, (zeros, zeros, zeros))
    put_column(grads, G_S, lane_sum(sums[0]))
    put_column(grads, C_S, lane_sum(sums[1]))
    put_column(grads, B_2, lane_sum(sums[2]))

    def give(start, width):
        block = dot_nt(mg[...], patch[pl.ds(start, width), :]).astype(BF16)
        for c in range(width // 128):
            to = pl.ds(pl.multiple_of((start >> 3) + 16 * c, 16), 16)
            part = block[:, 128 * c : 128 * c + 128].reshape(32, 16, 128)
            keep[:, to, :] = part[0:16]
            send[:, to, :] = part[16:32]

    widths(give)


def ffn_back_kernel(first_part, count, scal, w1, w2t, taps, sec, slope, branch, hg, dkx, hid_a, hid_b, cg_a, cg_b):
    start, steps = 256 * first_part, 4 * count
    j_first, j_last, i_first, i_last = edge_masks()
    lane = iota((16, 128), 1)

    def fill(hid, cg, step):
        rows = pl.ds(pl.multiple_of(start + jnp.minimum(step, steps - 1) * 64, 64), 64)
        cg[...] = dot(w2t[rows, :], branch[...]) * slope[rows, :].astype(F32)
        hid[...] = dot(w1[rows, :], sec[...])

    def group(hid, cg, step, index):
        rows = slice(16 * index, 16 * index + 16)
        from_rows = pl.ds(pl.multiple_of(start + 64 * step + 16 * index, 16), 16)
        to_rows = pl.ds(pl.multiple_of(64 * step + 16 * index, 16), 16)
        k = [taps[n, from_rows, :] for n in range(9)]
        quad = quads(cg, rows)
        bias = functools.reduce(lambda x, y: x + y, [t for row in quad for pair in row for t in pair])
        across = [
            (
                (times(left_of(quad[a][1]), j_first), quad[a][0], quad[a][1]),
                (quad[a][0], quad[a][1], times(right_of(quad[a][0]), j_last)),
            )
            for a in range(2)
        ]
        sums = [None] * 9
        for e in range(2):
            upper = [above(tiles, i_first) for tiles in across[1][e]]
            lower = [below(tiles, i_last) for tiles in across[0][e]]
            for a, near in ((0, (upper, across[0][e], across[1][e])), (1, (across[0][e], across[1][e], lower))):
                for half in range(2):
                    value = hid[rows, tile_at(a, e, half)]
                    total = None
                    for r in range(3):
                        for c in range(3):
                            tap = 3 * (2 - r) + (2 - c)
                            term = k[tap] * near[r][c][half]
                            total = term if total is None else total + term
                            term = value * near[r][c][half]
                            sums[tap] = term if sums[tap] is None else sums[tap] + term
                    hg[to_rows, tile_at(a, e, half)] = total.astype(BF16)
        table = jnp.where(lane == 9, lane_sum(bias), 0.0)
        for n in range(9):
            table = jnp.where(lane == n, lane_sum(sums[n]), table)
        dkx[to_rows, :] = table

    fill(hid_a, cg_a, 0)

    def two(index):
        fill(hid_b, cg_b, 2 * index + 1)
        for n in range(4):
            group(hid_a, cg_a, 2 * index, n)
        fill(hid_a, cg_a, 2 * index + 2)
        for n in range(4):
            group(hid_b, cg_b, 2 * index + 1, n)

    loop(steps // 2, two)


def middle_back_kernel(scal, bt, w1t, hg0, hg1, end_grad, mid, stats, mid_grad, low_grad, grads, work):
    side = scal[1]
    work[...] = sum(
        dot(w1t[:, 256 * at : 256 * (at + count)], hg[...]) for hg, (at, count) in zip((hg0, hg1), PARTS)
    )
    grads[...] = jnp.zeros_like(grads)
    gain = column(bt, G_2, 5)
    zeros = jnp.zeros((D, 128), F32)

    def body(tile, carry):
        at = lanes(tile)
        mask = token_mask(tile, side)
        grad = work[:, at] * mask
        hat = (mid[:, at] - stats[0:1, at]) * stats[1:2, at]
        result = end_grad[:, at] + norm_back(grad, hat, stats[1:2, at], gain)
        mid_grad[:, at] = result
        low = (result * mask).astype(BF16)
        low_grad[:, at] = low
        return carry[0] + grad * hat, carry[1] + grad, carry[2] + low.astype(F32)

    sums = lax.fori_loop(0, 8, body, (zeros, zeros, zeros))
    put_column(grads, G_2, lane_sum(sums[0]))
    put_column(grads, C_2, lane_sum(sums[1]))
    put_column(grads, B_O, lane_sum(sums[2]))


def pack_b_kernel(scal, hg0, hg1, dk0, dk1, sec, branch, act, keep, send, grads, dw1, gather, mixed):
    me = scal[0]
    grads[...] = jnp.zeros_like(grads)
    lane = iota((256, 128), 1)
    for hg, dkx, (at, count) in zip((hg0, hg1), (dk0, dk1), PARTS):

        def outer(n, hg=hg, dkx=dkx, at=at):
            rows = pl.ds(pl.multiple_of(256 * n, 256), 256)
            to = pl.ds(pl.multiple_of(256 * (n + at), 256), 256)
            part = dot_nt(hg[rows, :], sec[...])
            dw1[to, 0:256] = part[:, 0:256]
            turned = pltpu.roll(dkx[rows, :], 64, 1)
            dw1[to, 256:384] = jnp.where(lane < 64, part[:, 256:384], jnp.where(lane < 73, turned, 0.0))
            table = grads[...]
            for m in range(4):
                here = slice(64 * m, 64 * m + 64)
                number = 4 * (n + at) + m
                table = jnp.where(lane[here] == B_1 + number, part[here, 329:330], table)
                table = jnp.where(lane[here] == B_DW + number, dkx[rows, :][here, 9:10], table)
            grads[...] = table

        loop(count, outer)
    mixed[...] = dot(to_tens(me), branch[...]).astype(BF16)
    gather[:, 0:24, :] = jnp.zeros((32, 24, 128), F32)

    def contraction(p):
        block = dot_nt(mixed[...], act[pl.ds(pl.multiple_of(256 * p, 256), 256), :])
        parts = [block[0:256, 128 * e : 128 * e + 128].reshape(32, 1, 8, 128) for e in range(2)]
        full = jnp.concatenate(parts, axis=1).reshape(32, 16, 128).astype(BF16)
        to = pl.ds(pl.multiple_of(16 * p, 16), 16)
        keep[:, to, :] = full[0:16]
        send[:, to, :] = full[16:32]
        tail = jnp.concatenate([block[256:320, 0:128], block[256:320, 128:256]], axis=0).astype(BF16)
        place = rest_row(iota((256, 1), 0)) - 128 * (p & 1)
        to = pl.ds(pl.multiple_of(8 * (p >> 1), 8), 8)
        gather[:, to, :] += dot(one_hot(iota((256, 128), 1) == place), tail).reshape(32, 8, 128)

    loop(5, contraction)

    def expansion(owner):
        slot = slot_of(owner ^ me)
        rows = pl.ds(pl.multiple_of(40 * owner, 8), 40)
        for c in range(3):
            gather[slot, 24 + 40 * c : 64 + 40 * c, :] = dw1[rows, 128 * c : 128 * c + 128]

    loop(32, expansion)
    keep[:, 80:224, :] = gather[0:16].astype(BF16)
    send[:, 80:224, :] = gather[16:32].astype(BF16)


def attend_back_kernel(scal, kt, vt, qs, kv, wo, low_grad, lse, dq, dkv, og):
    bias = key_bias(scal[1])
    og[...] = dot_tn(wo[...], low_grad[...]).astype(BF16)

    def head(h):
        rows = pl.ds(pl.multiple_of(64 * h, 64), 64)
        more = pl.ds(pl.multiple_of(D + 64 * h, 64), 64)
        dk = jnp.zeros((64, 256), F32)
        dv = jnp.zeros((64, 256), F32)
        for quad in range(4):
            at = slice(256 * quad, 256 * quad + 256)
            probs = jnp.exp(dot(kt[h], qs[rows, at]) + bias - lse[h, :, at])
            grad = dot(vt[h], og[rows, at])
            mean = jnp.sum(probs * grad, axis=0, keepdims=True)
            score = (probs * (grad - mean)).astype(BF16)
            dq[rows, at] = (dot(kv[rows, :], score) * 0.125).astype(BF16)
            dk += dot_nt(qs[rows, at], score)
            dv += dot_nt(og[rows, at], probs.astype(BF16))
        dkv[rows, :] = dk.astype(BF16)
        dkv[more, :] = dv.astype(BF16)

    loop(HEADS, head)


def first_kernel(scal, bt, wq, wkv, wrs, first, red, raw, stat_r, dq, dkv, low_grad, att, entry, stats, g_one, g_two, g_three, keep, send, work, grads, wide, redin, stack_r, stack_z, tails_of):
    me = scal[0]
    grads[...] = g_one[...] + g_two[...] + g_three[...]
    for quad in range(4):
        redin[D * quad : D * quad + D, :] = first[:, 256 * quad : 256 * quad + 256]
    dred = dot_tn(wkv[...], dkv[...])
    gain = column(bt, G_R, 5)
    lows = []
    for tile in range(2):
        at = slice(128 * tile, 128 * tile + 128)
        grad = dred[:, at]
        hat = (raw[:, at] - stat_r[0:1, at]) * stat_r[1:2, at]
        low = norm_back(grad, hat, stat_r[1:2, at], gain).astype(BF16)
        lows.append(low)
        parts = (grad * hat, grad, low.astype(F32))
        sums = parts if tile == 0 else [s + v for s, v in zip(sums, parts)]
    put_column(grads, G_R, lane_sum(sums[0]))
    put_column(grads, C_R, lane_sum(sums[1]))
    put_column(grads, B_R, lane_sum(sums[2]))
    low = jnp.concatenate(lows, axis=1)
    order = to_tens(me)
    low = dot(order, low).astype(BF16)
    wide[...] = dot_tn(wrs[...], low)
    straight = dot_tn(wq[...], dq[...])
    for quad in range(4):
        at = slice(256 * quad, 256 * quad + 256)
        work[:, at] = straight[:, at] + wide[D * quad : D * quad + D, :]
    zeros = jnp.zeros((D, 128), F32)

    def body(tile, carry):
        at = lanes(tile)
        grad = work[:, at]
        hat = (entry[:, at].astype(F32) - stats[0:1, at]) * stats[1:2, at]
        return carry[0] + grad * hat, carry[1] + grad, carry[2] + dq[:, at].astype(F32)

    sums = lax.fori_loop(0, 8, body, (zeros, zeros, zeros))
    put_column(grads, G_1, lane_sum(sums[0]))
    put_column(grads, C_1, lane_sum(sums[1]))
    put_column(grads, B_Q, lane_sum(sums[2]))
    stack_r[...] = dot_nt(low, redin[...])

    def outer(pick, grad, value):
        return dot_nt(dot(pick, grad[...]).astype(BF16), value[...])

    row = iota((1, 2 * D), 1)
    place = iota((D, 2 * D), 0)
    parts = (
        outer(order, dq, first),
        outer(one_hot(place == keyval_tens(row, me, False)), dkv, red),
        outer(one_hot(place == keyval_tens(row, me, True)), dkv, red),
        outer(order, low_grad, att),
    )
    for part, at in zip(parts, (0, 256, 512, 1024)):
        stack_z[:, at : at + 256] = part[:, 0:256]
    stack_z[:, 768:1024] = jnp.concatenate([part[:, 256:320] for part in parts], axis=1)
    spread = one_hot(iota((256, 256), 1) == rest_row(iota((256, 1), 0)))

    def pack(p):
        at = lanes(p, 256)
        both = stack_r[:, at], stack_z[:, at]
        for e in range(2):
            pieces = [block[0:256, 128 * e : 128 * e + 128].reshape(32, 1, 8, 128) for block in both]
            full = jnp.concatenate(pieces, axis=1).reshape(32, 16, 128).astype(BF16)
            to = pl.ds(pl.multiple_of(32 * p + 16 * e, 16), 16)
            keep[:, to, :] = full[0:16]
            send[:, to, :] = full[16:32]
        tail = jnp.concatenate(
            [block[256:320, 128 * e : 128 * e + 128] for block in both for e in range(2)], axis=0
        ).astype(BF16)
        to = pl.ds(pl.multiple_of(8 * p, 8), 8)
        tails_of[:, to, :] = dot(spread, tail).reshape(32, 8, 128)

    loop(5, pack)
    rows = jnp.transpose(jnp.concatenate([grads[...], jnp.zeros((64, 128), F32)], axis=0)).astype(BF16)
    place = iota((256, 128), 0)
    vector = iota((256, 128), 1)
    line = place & 7
    owner = xor_of(place >> 3) ^ me
    start = (7 * owner) >> 3
    straight = (
        ((line == 0) & (vector == 3 * owner))
        | ((line == 1) & (vector == 3 * owner + 2))
        | ((line == 2) & (vector == 96 + start))
    )
    turned = ((line == 0) & (vector == 3 * owner + 1)) | ((line == 2) & (vector == 97 + start))
    small = dot(one_hot(straight), rows) + pltpu.roll(dot(one_hot(turned), rows), 64, 1)
    tails_of[:, 40:48, :] = small.reshape(32, 8, 128)
    keep[:, 160:208, :] = tails_of[0:16].astype(BF16)
    send[:, 160:208, :] = tails_of[16:32].astype(BF16)


def token_kernel(scal, bt, grad_in, mid_grad, entry, stats, tok, high, rest):
    side = scal[1]
    gain = column(bt, G_1, 5)

    def body(tile):
        at = lanes(tile)
        hat = (entry[:, at].astype(F32) - stats[0:1, at]) * stats[1:2, at]
        result = mid_grad[:, at] + norm_back(grad_in[:, at], hat, stats[1:2, at], gain)
        result = result * token_mask(tile, side)
        upper = result.astype(BF16)
        high[:, at] = upper
        rest[:, at] = (result - upper.astype(F32)).astype(BF16)

    loop(8, body)
    row, col = token_place(iota((TOKENS, 1), 0))
    natural = row * SIDE + col

    def quad(index):
        at = lanes(index, 256)
        pick = one_hot(iota((TOKENS, 256), 1) + 256 * index == natural)
        tok[:, at] = dot(high[...], pick) + dot(rest[...], pick)

    loop(4, quad)


def cost(micros):
    return pl.CostEstimate(flops=int(micros * 1e9), bytes_accessed=1000, transcendentals=0)


def call(kernel, args, outs, scratch=(), micros=5):
    return pl.pallas_call(
        kernel,
        in_specs=[pl.BlockSpec(memory_space=pltpu.SMEM if arg.dtype == I32 else pltpu.VMEM) for arg in args],
        out_shape=[jax.ShapeDtypeStruct(shape, dtype) for shape, dtype in outs],
        scratch_shapes=[pltpu.VMEM(shape, dtype) for shape, dtype in scratch],
        compiler_params=pltpu.CompilerParams(vmem_limit_bytes=VMEM_LIMIT),
        cost_estimate=cost(micros),
    )(*args)


def local(group, axes, *arrays):
    return step_of(group, axes, *arrays)


def step_of(group, axes, tokens, image_side, cotangent, *shards):
    index = lax.axis_index(axes[0]) * lax.axis_size(axes[1]) + lax.axis_index(axes[1])
    me = index // group
    devices = SUPER * group

    def flip(values, mask):
        pairs = [(i, ((i // group) ^ mask) * group + i % group) for i in range(devices)]
        return lax.ppermute(values, axes, pairs)

    def gather(block, split=0):
        held = block[None]
        for mask in FLIPS[:2]:
            held = jnp.concatenate([held, flip(held, mask)], axis=0)
        if split:
            one, two = held[:, :split], held[:, split:]
            one, two = (jnp.concatenate([one, flip(one, 8)], axis=0), jnp.concatenate([two, flip(two, 16)], axis=0))
            far, near = flip(one, 16), flip(two, 8)
            two = jnp.concatenate([two[:4], near[:4], two[4:], near[4:]], axis=0)
            held = jnp.concatenate([jnp.concatenate([one, far], axis=0), two], axis=1)
        else:
            for mask in FLIPS[2:]:
                held = jnp.concatenate([held, flip(held, mask)], axis=0)
        return held, flip(held, 1)

    def scatter(keep, send, split=0):
        def step(held, mask):
            return flip(held, mask).astype(F32)

        def halve(held, mask):
            half = held.shape[0] // 2
            return held[:half].astype(F32) + step(held[half:], mask)

        held = (keep.astype(F32) + step(send, 1)).astype(BF16)
        if split:
            one, two = held[:, :split], held[:, split:].reshape(2, 2, 4, -1, 128)
            one, two = (
                halve(one, 16).astype(BF16),
                (two[:, 0].astype(F32) + step(two[:, 1], 8)).astype(BF16).reshape(8, -1, 128),
            )
            held = jnp.concatenate([halve(one, 8), halve(two, 16)], axis=1).astype(BF16)
        else:
            held = halve(held, 16).astype(BF16)
            held = halve(held, 8).astype(BF16)
        held = halve(held, 4).astype(BF16)
        return halve(held, 2)[0]

    if group > 1:
        per = lax.axis_size(axes[1])
        start = (index % per) // group * group

        def join(shard):
            full = lax.all_gather(shard, axes[1], axis=0)
            return lax.dynamic_slice_in_dim(full, start, group, axis=0).reshape(-1)

        shards = [join(shard) for shard in shards]
    query, keyval, reduce_w, output, expand, depth, contract, merge, gains, biases = shards

    def rows(flat):
        return flat.reshape(-1, 128)

    scal = jnp.stack([me.astype(I32), image_side[0].astype(I32)])
    taps = jnp.pad(depth.reshape(40, 9), ((0, 0), (64, 55)))
    block_a = select(
        [rows(query), rows(output), rows(keyval), rows(reduce_w)],
        table_a, A_ROWS, (scal, biases[None], gains[None]),
    )
    block_b = select([rows(contract), rows(expand), taps], table_b, B_ROWS)
    block_c = select([rows(merge)], table_c, C_ROWS)
    a_low, a_high = gather(block_a, A_SPLIT)
    b_low, b_high = gather(block_b)
    c_low, c_high = gather(block_c, C_ROWS // 2)

    big, narrow = (D, TOKENS), (D, QUARTER)
    entry, stats_1 = call(entry_kernel, (scal, tokens[0]), [(big, BF16), ((8, TOKENS), F32)], micros=3.5)
    wq, wkv, wr, wo, first, qs, raw, stat_r, red, kv, kt, vt, bt = call(
        project_kernel,
        (scal, a_low, a_high, entry, stats_1),
        [
            ((D, D), BF16), ((2 * D, D), BF16), ((D, 4 * D), BF16), ((D, D), BF16), (big, BF16), (big, BF16),
            (narrow, F32), ((8, QUARTER), F32), (narrow, BF16), ((2 * D, QUARTER), BF16),
            ((HEADS, QUARTER, 64), BF16), ((HEADS, QUARTER, 64), BF16), ((64, 128), F32),
        ],
        [((D, 1280), BF16), ((256, 640), BF16), ((4 * D, QUARTER), BF16)],
        micros=8,
    )
    att, lse = call(attend_kernel, (scal, kt, qs, kv), [(big, BF16), ((HEADS, 1, TOKENS), F32)],
        [((2, QUARTER, TOKENS), F32), ((QUARTER, TOKENS), BF16)], micros=8.5)
    mid, sec, stats_2 = call(
        middle_kernel, (scal, bt, wo, att, entry), [(big, F32), ((384, TOKENS), BF16), ((8, TOKENS), F32)], [(big, F32)],
        micros=5,
    )
    w1, w1t, w2, w2t, taps = call(
        ffn_weights_kernel,
        (scal, bt, b_low, b_high),
        [((FF, 384), BF16), ((D, FF), BF16), ((D, FF), BF16), ((FF, D), BF16), ((10, FF, 128), F32)],
        [((D, FF), BF16), ((256, 384), BF16), ((FF, 384), F32)],
        micros=8,
    )
    act, slope = call(
        ffn_kernel,
        (scal, w1, taps, sec),
        [((FF, TOKENS), BF16), ((FF, TOKENS), BF16)],
        [((64, TOKENS), F32), ((64, TOKENS), F32)],
        micros=17,
    )
    end, sect, stats_s = call(
        ending_kernel, (scal, bt, w2, act, mid), [(big, F32), (big, BF16), ((8, TOKENS), F32)], [(big, F32)], micros=5
    )
    four, c_keep, c_send, end_grad, branch, g_one = call(
        merge_kernel,
        (scal, bt, c_low, c_high, sect, end, stats_s, cotangent[0]),
        [
            ((OUT_D, QUARTER), BF16), ((16, C_ROWS, 128), BF16), ((16, C_ROWS, 128), BF16), (big, F32), (big, BF16),
            ((64, 128), F32),
        ],
        [
            ((OUT_D, MERGE_PAD), BF16), ((MERGE_PAD, QUARTER), BF16), ((OUT_D, QUARTER), BF16),
            ((MERGE_PAD, QUARTER), F32), ((OUT_D, QUARTER), F32), ((OUT_D, QUARTER), F32),
        ],
        micros=20,
    )
    sum_c = scatter(c_keep, c_send, C_ROWS // 2)
    hgs, dks = [], []
    for at, count in PARTS:
        hg, dk = call(
            functools.partial(ffn_back_kernel, at, count),
            (scal, w1, w2t, taps, sec, slope, branch),
            [((256 * count, TOKENS), BF16), ((256 * count, 128), F32)],
            [((64, TOKENS), F32)] * 4,
            micros=6 * count,
        )
        hgs.append(hg)
        dks.append(dk)
    b_keep, b_send, g_three = call(
        pack_b_kernel,
        (scal, *hgs, *dks, sec, branch, act),
        [((16, B_ROWS, 128), BF16), ((16, B_ROWS, 128), BF16), ((64, 128), F32)],
        [((FF, 384), F32), ((32, 144, 128), F32), (big, BF16)],
        micros=9,
    )
    sum_b = scatter(b_keep, b_send)
    mid_grad, low_grad, g_two = call(
        middle_back_kernel,
        (scal, bt, w1t, *hgs, end_grad, mid, stats_2),
        [(big, F32), (big, BF16), ((64, 128), F32)],
        [(big, F32)],
        micros=6,
    )
    dq, dkv = call(
        attend_back_kernel,
        (scal, kt, vt, qs, kv, wo, low_grad, lse),
        [(big, BF16), ((2 * D, QUARTER), BF16)],
        [(big, BF16)],
        micros=9,
    )
    a_keep, a_send, first_grad = call(
        first_kernel,
        (
            scal, bt, wq, wkv, wr, first, red, raw, stat_r, dq, dkv, low_grad, att, entry, stats_1, g_one, g_two, g_three,
        ),
        [((16, A_ROWS, 128), BF16), ((16, A_ROWS, 128), BF16), (big, F32)],
        [
            ((64, 128), F32), ((4 * D, QUARTER), F32), ((4 * D, QUARTER), BF16), ((D, 1280), F32), ((D, 1280), F32),
            ((32, 48, 128), F32),
        ],
        micros=11,
    )
    sum_a = scatter(a_keep, a_send, A_SPLIT)
    (token_grad,) = call(
        token_kernel,
        (scal, bt, first_grad, mid_grad, entry, stats_1),
        [(big, F32)],
        [(big, BF16), (big, BF16)],
        micros=5,
    )
    if group > 1:

        def total(part):
            full = lax.all_gather(part, axes[1], axis=0)
            return jnp.sum(lax.dynamic_slice_in_dim(full, start, group, axis=0), axis=0)

        sum_a, sum_b, sum_c = total(sum_a), total(sum_b), total(sum_c)

    def flat(count):
        return (count, 128), F32

    query_g, output_g, keyval_g, reduce_g, biases_g, gains_g = call(
        out_a_kernel,
        (scal, sum_a),
        [flat(25), flat(25), flat(50), flat(100), ((1, 192), F32), ((1, 56), F32)],
        micros=1,
    )
    contract_g, expand_g = call(out_b_kernel, (scal, sum_b), [flat(100), flat(100)], micros=1)
    (merge_g,) = call(out_c_kernel, (scal, sum_c), [flat(360)], micros=1)
    depth_g = sum_b[184:224, 64:73]
    grads = [query_g, keyval_g, reduce_g, output_g, expand_g, depth_g, contract_g, merge_g, gains_g, biases_g]
    grads = [grad.reshape(-1) for grad in grads]
    if group > 1:
        mine = index % group
        grads = [lax.dynamic_index_in_dim(grad.reshape(group, -1), mine, keepdims=False) for grad in grads]
    return (four[None], token_grad[None], *grads)


def solution(mesh):
    axes = ("dp", "fs")
    devices = mesh.shape["dp"] * mesh.shape["fs"]
    group = devices // SUPER
    if devices != SUPER * group or mesh.shape["fs"] % group:
        raise ValueError("unsupported mesh")
    one, three = P(axes), P(axes, None, None)
    return jax.shard_map(
        functools.partial(local, group, axes),
        mesh=mesh,
        in_specs=(three, one, three) + (one,) * 10,
        out_specs=(three, three) + (one,) * 10,
        check_vma=False,
    )
```

profile of v0, /device:TPU:0, one launch (start us, length us, event | category | flops | bytes accessed | tf_op | source)
XLA Modules:
  0.0 228.9 jit_solution(5409631248205642498)
XLA Ops:
  6.0 3.1 %collective-permute-start = (bf16[1,208,128]{2,1,0:T(8,128)(2,1)}, bf16[1,208,128]{2,1,0:T(8,128)(2,1)S(1)}, u32[]{:S(2)}, u32[]{:S(2)}) collective-permute-start(bf16[1,208,128]{2,1,0:T(8,128)(2,1)} %bitcast.86), channel_id=1, source_target_pairs={{0,2},{1,3},{2,0},{3,1},{4,6},{5,7},{6,4},{7,5},{8,10},{9,11},{10,... | collective-permute-start | bytes 159752 | tf_op jit(solution)/shard_map/ppermute | solution.py:1104
  21.3 8.3 %collective-permute-done.1 = bf16[2,208,128]{2,1,0:T(8,128)(2,1)S(1)} collective-permute-done((bf16[2,208,128]{2,1,0:T(8,128)(2,1)S(1)}, bf16[2,208,128]{2,1,0:T(8,128)(2,1)S(1)}, u32[]{:S(2)}, u32[]{:S(2)}) %collective-permute-start.1) | collective-permute-done | bytes 106528 | tf_op jit(solution)/shard_map/ppermute | solution.py:1104
  40.0 3.3 %collective-permute-done.11 = bf16[4,184,128]{2,1,0:T(8,128)(2,1)S(1)} collective-permute-done((bf16[4,184,128]{2,1,0:T(8,128)(2,1)S(1)}, bf16[4,184,128]{2,1,0:T(8,128)(2,1)S(1)}, u32[]{:S(2)}, u32[]{:S(2)}) %collective-permute-start.11) | collective-permute-done | bytes 188448 | tf_op jit(solution)/shard_map/ppermute | solution.py:1104
  51.8 4.3 %collective-permute-done.12 = bf16[8,184,128]{2,1,0:T(8,128)(2,1)S(1)} collective-permute-done((bf16[8,184,128]{2,1,0:T(8,128)(2,1)S(1)}, bf16[8,184,128]{2,1,0:T(8,128)(2,1)S(1)}, u32[]{:S(2)}, u32[]{:S(2)}) %collective-permute-start.12) | collective-permute-done | bytes 376864 | tf_op jit(solution)/shard_map/ppermute | solution.py:1104
  56.1 5.2 %collective-permute-done.10 = bf16[8,184,128]{2,1,0:T(8,128)(2,1)S(1)} collective-permute-done((bf16[8,184,128]{2,1,0:T(8,128)(2,1)S(1)}, bf16[8,184,128]{2,1,0:T(8,128)(2,1)S(1)}, u32[]{:S(2)}, u32[]{:S(2)}) %collective-permute-start.10) | collective-permute-done | bytes 376864 | tf_op jit(solution)/shard_map/ppermute | solution.py:1104
  61.5 6.3 %collective-permute-done.17 = bf16[8,224,128]{2,1,0:T(8,128)(2,1)S(1)} collective-permute-done((bf16[8,224,128]{2,1,0:T(8,128)(2,1)S(1)}, bf16[8,224,128]{2,1,0:T(8,128)(2,1)S(1)}, u32[]{:S(2)}, u32[]{:S(2)}) %collective-permute-start.17) | collective-permute-done | bytes 458784 | tf_op jit(solution)/shard_map/ppermute | solution.py:1104
  67.9 7.1 %shard_map.276 = (bf16[320,320]{1,0:T(8,128)(2,1)S(1)}, bf16[640,320]{1,0:T(8,128)(2,1)S(1)}, bf16[320,1280]{1,0:T(8,128)(2,1)S(1)}, bf16[320,320]{1,0:T(8,128)(...) custom-call(s32[2]{0:T(128)S(1)} %copy-done.9, ...), custom_call_target="tpu_custom_call" | custom-call | flops 8000000000 | bytes 1000 | tf_op jit(solution)/shard_map/pallas_call | solution.py:1083
  75.0 4.8 %shard_map.280 = (bf16[320,1024]{1,0:T(8,128)(2,1)S(1)}, f32[5,1,1024]{2,1,0:T(1,128)S(1)}) custom-call(s32[2]{0:T(128)S(1)} %copy-done.9, bf16[5,256,64]{2,1,0:T(8,128)(2,1)S(1)} %get-tuple-element.78.kt, bf16[320,1024]{1,0:T(8,128)(2,1)S(1)} %get-tuple-element.79.qs, bf16[640,256]{1,0:T(8,128)(2,1)S(1)} %get-tuple-element.80.kv), custom_call_target="tpu_custom_call" | custom-call | flops 8499999744 | bytes 1000 | tf_op jit(solution)/shard_map/pallas_call | solution.py:1083
  82.7 6.3 %shard_map.279 = (bf16[1280,384]{1,0:T(8,128)(2,1)S(1)}, bf16[320,1280]{1,0:T(8,128)(2,1)S(1)}, bf16[320,1280]{1,0:T(8,128)(2,1)S(1)}, bf16[1280,320]{1,0:T(8,128)(2,1)S(1)}, f32[10,1280,128]{2,1,0:T(8,128)S(1)}) custom-call(s32[2]{0:T(128)S(1)} %copy-done.9, f32[64,128]{1,0:T(8,128)S(1)} %get-tuple-element.73.bt, ...), custom_call_target="tpu_custom_call" | custom-call | flops 8000000000 | bytes 1000 | tf_op jit(solution)/shard_map/pallas_call | solution.py:1083
  89.0 10.0 %shard_map.282 = (bf16[1280,1024]{1,0:T(8,128)(2,1)S(1)}, bf16[1280,1024]{1,0:T(8,128)(2,1)S(1)}) custom-call(s32[2]{0:T(128)S(1)} %copy-done.9, bf16[1280,384]{1,0:T(8,128)(2,1)S(1)} %get-tuple-element.75.w1, f32[10,1280,128]{2,1,0:T(8,128)S(1)} %get-tuple-element.76.taps, bf16[384,1024]{1,0:T(8,128)(2,1)S(1)} %get-tuple-element.82.sec), custom_call_target="tpu_custom_call" | custom-call | flops 16999999488 | bytes 1000 | tf_op jit(solution)/shard_map/pallas_call | solution.py:1083
  99.0 3.2 %shard_map.283 = (f32[320,1024]{1,0:T(8,128)S(1)}, bf16[320,1024]{1,0:T(8,128)(2,1)S(1)}, f32[8,1024]{1,0:T(8,128)S(1)}) custom-call(s32[2]{0:T(128)S(1)} %copy-done.9, f32[64,128]{1,0:T(8,128)S(1)} %get-tuple-element.73.bt, bf16[320,1280]{1,0:T(8,128)(2,1)S(1)} %get-tuple-element.74.w2, bf16[1280,1024]{1,0:T(8,128)(2,1)S(1)} %get-tuple-element.83.act, ...), custom_call_target="tpu_custom_call" | custom-call | flops 5000000000 | bytes 1000 | tf_op jit(solution)/shard_map/pallas_call | solution.py:1083
  102.2 13.1 %shard_map.284 = (bf16[512,256]{1,0:T(8,128)(2,1)}, bf16[16,368,128]{2,1,0:T(8,128)(2,1)S(1)}, bf16[16,368,128]{2,1,0:T(8,128)(2,1)S(1)}, f32[320,1024]{1,0:T(8,...) custom-call(s32[2]{0:T(128)S(1)} %copy-done.9, f32[64,128]{1,0:T(8,128)S(1)} %get-tuple-element.73.bt, ...), custom_call_target="tpu_custom_call" | custom-call | flops 20000000000 | bytes 1000 | tf_op jit(solution)/shard_map/pallas_call | solution.py:1083
  115.3 4.6 %shard_map.285 = (bf16[256,1024]{1,0:T(8,128)(2,1)S(1)}, f32[256,128]{1,0:T(8,128)S(1)}) custom-call(s32[2]{0:T(128)S(1)} %copy-done.9, bf16[1280,384]{1,0:T(8,128)(2,1)S(1)} %get-tuple-element.75.w1, bf16[1280,320]{1,0:T(8,128)(2,1)S(1)} %get-tuple-element.98.w2t, f32[10,1280,128]{2,1,0:T(8,128)S(1)} %get-tuple-element.76.taps, ...), custom_call_target="tpu_custom_call" | custom-call | flops 6000000000 | bytes 1000 | tf_op jit(solution)/shard_map/pallas_call | solution.py:1083
  119.9 15.4 %shard_map.286 = (bf16[1024,1024]{1,0:T(8,128)(2,1)S(1)}, f32[1024,128]{1,0:T(8,128)S(1)}) custom-call(s32[2]{0:T(128)S(1)} %copy-done.9, bf16[1280,384]{1,0:T(8,128)(2,1)S(1)} %get-tuple-element.75.w1, bf16[1280,320]{1,0:T(8,128)(2,1)S(1)} %get-tuple-element.98.w2t, f32[10,1280,128]{2,1,0:T(8,128)S(1)} %get-tuple-element.76.taps, ...), custom_call_target="tpu_custom_call" | custom-call | flops 24000000000 | bytes 1000 | tf_op jit(solution)/shard_map/pallas_call | solution.py:1083
  135.3 6.6 %shard_map.289 = (bf16[16,224,128]{2,1,0:T(8,128)(2,1)S(1)}, bf16[16,224,128]{2,1,0:T(8,128)(2,1)S(1)}, f32[64,128]{1,0:T(8,128)S(1)}) custom-call(s32[2]{0:T(128)S(1)} %copy-done.9, bf16[256,1024]{1,0:T(8,128)(2,1)S(1)} %get-tuple-element.101.hg0, bf16[1024,1024]{1,0:T(8,128)(2,1)S(1)} %get-tuple-element.102.hg1, f32[256,128]{1,0:T(8,128)S(1)} %get-tuple-element.111.dk0, ...), custom_call_target="tpu_custom_call" | custom-call | flops 8999999488 | bytes 1000 | tf_op jit(solution)/shard_map/pallas_call | solution.py:1083
  141.9 3.7 %shard_map.287 = (f32[320,1024]{1,0:T(8,128)S(1)}, bf16[320,1024]{1,0:T(8,128)(2,1)S(1)}, f32[64,128]{1,0:T(8,128)S(1)}) custom-call(s32[2]{0:T(128)S(1)} %copy-done.9, f32[64,128]{1,0:T(8,128)S(1)} %get-tuple-element.73.bt, bf16[320,1280]{1,0:T(8,128)(2,1)S(1)} %get-tuple-element.97.w1t, bf16[256,1024]{1,0:T(8,128)(2,1)S(1)} %get-tuple-element.101.hg0, ...), custom_call_target="tpu_custom_call" | custom-call | flops 6000000000 | bytes 1000 | tf_op jit(solution)/shard_map/pallas_call | solution.py:1083
  145.6 8.9 %shard_map.288 = (bf16[320,1024]{1,0:T(8,128)(2,1)S(1)}, bf16[640,256]{1,0:T(8,128)(2,1)S(1)}) custom-call(s32[2]{0:T(128)S(1)} %copy-done.9, bf16[5,256,64]{2,1,0:T(8,128)(2,1)S(1)} %get-tuple-element.78.kt, bf16[5,256,64]{2,1,0:T(8,128)(2,1)S(1)} %get-tuple-element.96.vt, bf16[320,1024]{1,0:T(8,128)(2,1)S(1)} %get-tuple-element.79.qs, ...), custom_call_target="tpu_custom_call" | custom-call | flops 8999999488 | bytes 1000 | tf_op jit(solution)/shard_map/pallas_call | solution.py:1083
  154.5 8.8 %shard_map.290 = (bf16[16,208,128]{2,1,0:T(8,128)(2,1)S(1)}, bf16[16,208,128]{2,1,0:T(8,128)(2,1)S(1)}, f32[320,1024]{1,0:T(8,128)S(1)}) custom-call(s32[2]{0:T(128)S(1)} %copy-done.9, f32[64,128]{1,0:T(8,128)S(1)} %get-tuple-element.73.bt, bf16[320,320]{1,0:T(8,128)(2,1)S(1)} %get-tuple-element.89.wq, bf16[640,320]{1,0:T(8,128)(2,1)S(1)} %get-tuple-element.90.wkv, ...), custom_call_target="tpu_custom_call" | custom-call | flops 11000000512 | bytes 1000 | tf_op jit(solution)/shard_map/pallas_call | solution.py:1083
  169.1 4.7 %collective-permute-done.20 = bf16[8,104,128]{2,1,0:T(8,128)(2,1)S(1)} collective-permute-done((bf16[8,104,128]{2,1,0:T(8,128)(2,1)S(1)}, bf16[8,104,128]{2,1,0:T(8,128)(2,1)S(1)}, u32[]{:S(2)}, u32[]{:S(2)}) %collective-permute-start.20) | collective-permute-done | bytes 213024 | tf_op jit(solution)/shard_map/ppermute | solution.py:1104
  182.1 4.3 %collective-permute-done.24 = bf16[2,208,128]{2,1,0:T(8,128)(2,1)S(1)} collective-permute-done((bf16[2,208,128]{2,1,0:T(8,128)(2,1)S(1)}, bf16[2,208,128]{2,1,0:T(8,128)(2,1)S(1)}, u32[]{:S(2)}, u32[]{:S(2)}) %collective-permute-start.24) | collective-permute-done | bytes 106528 | tf_op jit(solution)/shard_map/ppermute | solution.py:1104
  186.5 5.2 %shard_map.291 = f32[320,1024]{1,0:T(8,128)} custom-call(s32[2]{0:T(128)S(1)} %copy-done.9, f32[64,128]{1,0:T(8,128)S(1)} %get-tuple-element.73.bt, f32[320,1024]{1,0:T(8,128)S(1)} %get-tuple-element.114.grad_in, f32[320,1024]{1,0:T(8,128)S(1)} %get-tuple-element.115.mid_grad, bf16[320,1024]{1,0:T(8,128)(2,1)S(1)} %get-tuple-element.71.entry, ...), custom_call_target="tpu_custom_call" | custom-call | flops 5000000000 | bytes 1000 | tf_op jit(solution)/shard_map/pallas_call | solution.py:1083
  197.5 4.3 %collective-permute-done.28 = bf16[4,224,128]{2,1,0:T(8,128)(2,1)S(1)} collective-permute-done((bf16[4,224,128]{2,1,0:T(8,128)(2,1)S(1)}, bf16[4,224,128]{2,1,0:T(8,128)(2,1)S(1)}, u32[]{:S(2)}, u32[]{:S(2)}) %collective-permute-start.28) | collective-permute-done | bytes 229408 | tf_op jit(solution)/shard_map/ppermute | solution.py:1104
  210.5 3.7 %collective-permute-done.35 = bf16[4,184,128]{2,1,0:T(8,128)(2,1)S(1)} collective-permute-done((bf16[4,184,128]{2,1,0:T(8,128)(2,1)S(1)}, bf16[4,184,128]{2,1,0:T(8,128)(2,1)S(1)}, u32[]{:S(2)}, u32[]{:S(2)}) %collective-permute-start.35) | collective-permute-done | bytes 188448 | tf_op jit(solution)/shard_map/ppermute | solution.py:1104
  216.5 6.3 %collective-permute-done.36 = bf16[2,368,128]{2,1,0:T(8,128)(2,1)S(1)} collective-permute-done((bf16[2,368,128]{2,1,0:T(8,128)(2,1)S(1)}, bf16[2,368,128]{2,1,0:T(8,128)(2,1)S(1)}, u32[]{:S(2)}, u32[]{:S(2)}) %collective-permute-start.36) | collective-permute-done | bytes 188448 | tf_op jit(solution)/shard_map/ppermute | solution.py:1104
  (162 shorter events, 75.4 us)
Async XLA Ops:
  6.0 9.5 %collective-permute-start = (bf16[1,208,128]{2,1,0:T(8,128)(2,1)}, bf16[1,208,128]{2,1,0:T(8,128)(2,1)S(1)}, u32[]{:S(2)}, u32[]{:S(2)}) collective-permute-start(bf16[1,208,128]{2,1,0:T(8,128)(2,1)} %bitcast.86), channel_id=1, source_target_pairs={{0,2},{1,3},{2,0},{3,1},{4,6},{5,7},{6,4},{7,5},{8,10},{9,11},{10,... | collective-permute-start | bytes 159752 | tf_op jit(solution)/shard_map/ppermute | solution.py:1104
  10.1 8.1 %collective-permute-start.14 = (bf16[1,224,128]{2,1,0:T(8,128)(2,1)S(1)}, bf16[1,224,128]{2,1,0:T(8,128)(2,1)S(1)}, u32[]{:S(2)}, u32[]{:S(2)}) collective-permute-start(bf16[1,224,128]{2,1,0:T(8,128)(2,1)S(1)} %bitcast.70), channel_id=1, source_target_pairs={{0,2},{1,3},{2,0},{3,1},{4,6},{5,7},{6,4},{7,5},{8,10},{9,11},{10,... | collective-permute-start | bytes 172040 | tf_op jit(solution)/shard_map/ppermute | solution.py:1104
  15.6 14.1 %collective-permute-start.1 = (bf16[2,208,128]{2,1,0:T(8,128)(2,1)S(1)}, bf16[2,208,128]{2,1,0:T(8,128)(2,1)S(1)}, u32[]{:S(2)}, u32[]{:S(2)}) collective-permute-start(bf16[2,208,128]{2,1,0:T(8,128)(2,1)S(1)} %pad_maximum_fusion.12), channel_id=1, source_target_pairs={{0,4},{1,5},{2,6},{3,7},{4,0},{5,1},{6,2},{7,3},{8,12},{9,13},{10,... | collective-permute-start | bytes 319496 | tf_op jit(solution)/shard_map/ppermute | solution.py:1104
  18.2 14.9 %collective-permute-start.15 = (bf16[2,224,128]{2,1,0:T(8,128)(2,1)S(1)}, bf16[2,224,128]{2,1,0:T(8,128)(2,1)S(1)}, u32[]{:S(2)}, u32[]{:S(2)}) collective-permute-start(bf16[2,224,128]{2,1,0:T(8,128)(2,1)S(1)} %pad_maximum_fusion.10), channel_id=1, source_target_pairs={{0,4},{1,5},{2,6},{3,7},{4,0},{5,1},{6,2},{7,3},{8,12},{9,13},{10,... | collective-permute-start | bytes 344072 | tf_op jit(solution)/shard_map/ppermute | solution.py:1104
  18.7 16.9 %collective-permute-start.8 = (bf16[2,368,128]{2,1,0:T(8,128)(2,1)S(1)}, bf16[2,368,128]{2,1,0:T(8,128)(2,1)S(1)}, u32[]{:S(2)}, u32[]{:S(2)}) collective-permute-start(bf16[2,368,128]{2,1,0:T(8,128)(2,1)S(1)} %pad_maximum_fusion.9), channel_id=1, source_target_pairs={{0,4},{1,5},{2,6},{3,7},{4,0},{5,1},{6,2},{7,3},{8,12},{9,13},{10,... | collective-permute-start | bytes 565256 | tf_op jit(solution)/shard_map/ppermute | solution.py:1104
  29.7 9.2 %collective-permute-start.2 = (bf16[4,104,128]{2,1,0:T(8,128)(2,1)S(1)}, bf16[4,104,128]{2,1,0:T(8,128)(2,1)S(1)}, u32[]{:S(2)}, u32[]{:S(2)}) collective-permute-start(bf16[4,104,128]{2,1,0:T(8,128)(2,1)S(1)} %get-tuple-element.134), channel_id=1, source_target_pairs={{0,8},{1,9},{2,10},{3,11},{4,12},{5,13},{6,14},{7,15},{8,0},{9,1},... | collective-permute-start | bytes 319496 | tf_op jit(solution)/shard_map/ppermute | solution.py:1104
  33.1 18.0 %collective-permute-start.16 = (bf16[4,224,128]{2,1,0:T(8,128)(2,1)S(1)}, bf16[4,224,128]{2,1,0:T(8,128)(2,1)S(1)}, u32[]{:S(2)}, u32[]{:S(2)}) collective-permute-start(bf16[4,224,128]{2,1,0:T(8,128)(2,1)S(1)} %pad_maximum_fusion.4), channel_id=1, source_target_pairs={{0,8},{1,9},{2,10},{3,11},{4,12},{5,13},{6,14},{7,15},{8,0},{9,1},... | collective-permute-start | bytes 688136 | tf_op jit(solution)/shard_map/ppermute | solution.py:1104
  35.7 7.7 %collective-permute-start.11 = (bf16[4,184,128]{2,1,0:T(8,128)(2,1)S(1)}, bf16[4,184,128]{2,1,0:T(8,128)(2,1)S(1)}, u32[]{:S(2)}, u32[]{:S(2)}) collective-permute-start(bf16[4,184,128]{2,1,0:T(8,128)(2,1)S(1)} %get-tuple-element.131), channel_id=1, source_target_pairs={{0,16},{1,17},{2,18},{3,19},{4,20},{5,21},{6,22},{7,23},{8,24},{9,... | collective-permute-start | bytes 565256 | tf_op jit(solution)/shard_map/ppermute | solution.py:1104
  37.3 8.2 %collective-permute-start.5 = (bf16[8,104,128]{2,1,0:T(8,128)(2,1)S(1)}, bf16[8,104,128]{2,1,0:T(8,128)(2,1)S(1)}, u32[]{:S(2)}, u32[]{:S(2)}) collective-permute-start(bf16[8,104,128]{2,1,0:T(8,128)(2,1)S(1)} %pad_maximum_fusion.7), channel_id=1, source_target_pairs={{0,8},{1,9},{2,10},{3,11},{4,12},{5,13},{6,14},{7,15},{8,0},{9,1},... | collective-permute-start | bytes 638984 | tf_op jit(solution)/shard_map/ppermute | solution.py:1104
  39.5 10.1 %collective-permute-start.9 = (bf16[4,184,128]{2,1,0:T(8,128)(2,1)S(1)}, bf16[4,184,128]{2,1,0:T(8,128)(2,1)S(1)}, u32[]{:S(2)}, u32[]{:S(2)}) collective-permute-start(bf16[4,184,128]{2,1,0:T(8,128)(2,1)S(1)} %get-tuple-element.130), channel_id=1, source_target_pairs={{0,8},{1,9},{2,10},{3,11},{4,12},{5,13},{6,14},{7,15},{8,0},{9,1},... | collective-permute-start | bytes 565256 | tf_op jit(solution)/shard_map/ppermute | solution.py:1104
  43.4 12.7 %collective-permute-start.12 = (bf16[8,184,128]{2,1,0:T(8,128)(2,1)S(1)}, bf16[8,184,128]{2,1,0:T(8,128)(2,1)S(1)}, u32[]{:S(2)}, u32[]{:S(2)}) collective-permute-start(bf16[8,184,128]{2,1,0:T(8,128)(2,1)S(1)} %pad_maximum_fusion.3), channel_id=1, source_target_pairs={{0,8},{1,9},{2,10},{3,11},{4,12},{5,13},{6,14},{7,15},{8,0},{9,1},... | collective-permute-start | bytes 1130504 | tf_op jit(solution)/shard_map/ppermute | solution.py:1104
  46.6 21.3 %collective-permute-start.6 = (bf16[16,208,128]{2,1,0:T(8,128)(2,1)S(1)}, bf16[16,208,128]{2,1,0:T(8,128)(2,1)S(1)}, u32[]{:S(2)}, u32[]{:S(2)}) collective-permute-start(bf16[16,208,128]{2,1,0:T(8,128)(2,1)S(1)} %maximum_maximum_fusion.1.low), channel_id=1, source_target_pairs={{0,1},{1,0},{2,3},{3,2},{4,5},{5,4},{6,7},{7,6},{8,9},{9,8},{10,11... | collective-permute-start | bytes 2555912 | tf_op jit(solution)/shard_map/ppermute | solution.py:1104
  49.6 11.7 %collective-permute-start.10 = (bf16[8,184,128]{2,1,0:T(8,128)(2,1)S(1)}, bf16[8,184,128]{2,1,0:T(8,128)(2,1)S(1)}, u32[]{:S(2)}, u32[]{:S(2)}) collective-permute-start(bf16[8,184,128]{2,1,0:T(8,128)(2,1)S(1)} %pad_maximum_fusion.2), channel_id=1, source_target_pairs={{0,16},{1,17},{2,18},{3,19},{4,20},{5,21},{6,22},{7,23},{8,24},{9,... | collective-permute-start | bytes 1130504 | tf_op jit(solution)/shard_map/ppermute | solution.py:1104
  51.2 16.6 %collective-permute-start.17 = (bf16[8,224,128]{2,1,0:T(8,128)(2,1)S(1)}, bf16[8,224,128]{2,1,0:T(8,128)(2,1)S(1)}, u32[]{:S(2)}, u32[]{:S(2)}) collective-permute-start(bf16[8,224,128]{2,1,0:T(8,128)(2,1)S(1)} %pad_maximum_fusion), channel_id=1, source_target_pairs={{0,16},{1,17},{2,18},{3,19},{4,20},{5,21},{6,22},{7,23},{8,24},{9,... | collective-permute-start | bytes 1376264 | tf_op jit(solution)/shard_map/ppermute | solution.py:1104
  61.4 40.8 %collective-permute-start.13 = (bf16[16,368,128]{2,1,0:T(8,128)(2,1)S(1)}, bf16[16,368,128]{2,1,0:T(8,128)(2,1)S(1)}, u32[]{:S(2)}, u32[]{:S(2)}) collective-permute-start(bf16[16,368,128]{2,1,0:T(8,128)(2,1)S(1)} %maximum_maximum_fusion.c_low), channel_id=1, source_target_pairs={{0,1},{1,0},{2,3},{3,2},{4,5},{5,4},{6,7},{7,6},{8,9},{9,8},{10,11... | collective-permute-start | bytes 4521992 | tf_op jit(solution)/shard_map/ppermute | solution.py:1104
  67.8 14.8 %collective-permute-start.18 = (bf16[16,224,128]{2,1,0:T(8,128)(2,1)S(1)}, bf16[16,224,128]{2,1,0:T(8,128)(2,1)S(1)}, u32[]{:S(2)}, u32[]{:S(2)}) collective-permute-start(bf16[16,224,128]{2,1,0:T(8,128)(2,1)S(1)} %constant_dynamic-update-slice_fusion.low), channel_id=1, source_target_pairs={{0,1},{1,0},{2,3},{3,2},{4,5},{5,4},{6,7},{7,6},{8,9},{9,8},{10,11... | collective-permute-start | bytes 2752520 | tf_op jit(solution)/shard_map/ppermute | solution.py:1104
  163.9 16.3 %collective-permute-start.26 = (bf16[16,224,128]{2,1,0:T(8,128)(2,1)S(1)}, bf16[16,224,128]{2,1,0:T(8,128)(2,1)S(1)}, u32[]{:S(2)}, u32[]{:S(2)}) collective-permute-start(bf16[16,224,128]{2,1,0:T(8,128)(2,1)S(1)} %get-tuple-element.123), channel_id=1, source_target_pairs={{0,1},{1,0},{2,3},{3,2},{4,5},{5,4},{6,7},{7,6},{8,9},{9,8},{10,11... | collective-permute-start | bytes 2752520 | tf_op jit(solution)/shard_map/ppermute | solution.py:1104
  164.0 30.5 %collective-permute-start.31 = (bf16[16,368,128]{2,1,0:T(8,128)(2,1)S(1)}, bf16[16,368,128]{2,1,0:T(8,128)(2,1)S(1)}, u32[]{:S(2)}, u32[]{:S(2)}) collective-permute-start(bf16[16,368,128]{2,1,0:T(8,128)(2,1)S(1)} %get-tuple-element.127), channel_id=1, source_target_pairs={{0,1},{1,0},{2,3},{3,2},{4,5},{5,4},{6,7},{7,6},{8,9},{9,8},{10,11... | collective-permute-start | bytes 4521992 | tf_op jit(solution)/shard_map/ppermute | solution.py:1104
  180.5 12.5 %collective-permute-start.27 = (bf16[8,224,128]{2,1,0:T(8,128)(2,1)S(1)}, bf16[8,224,128]{2,1,0:T(8,128)(2,1)S(1)}, u32[]{:S(2)}, u32[]{:S(2)}) collective-permute-start(bf16[8,224,128]{2,1,0:T(8,128)(2,1)S(1)} %slice.210), channel_id=1, source_target_pairs={{0,16},{1,17},{2,18},{3,19},{4,20},{5,21},{6,22},{7,23},{8,24},{9,... | collective-permute-start | bytes 1376264 | tf_op jit(solution)/shard_map/ppermute | solution.py:1104
  193.2 8.5 %collective-permute-start.28 = (bf16[4,224,128]{2,1,0:T(8,128)(2,1)S(1)}, bf16[4,224,128]{2,1,0:T(8,128)(2,1)S(1)}, u32[]{:S(2)}, u32[]{:S(2)}) collective-permute-start(bf16[4,224,128]{2,1,0:T(8,128)(2,1)S(1)} %slice.212), channel_id=1, source_target_pairs={{0,8},{1,9},{2,10},{3,11},{4,12},{5,13},{6,14},{7,15},{8,0},{9,1},... | collective-permute-start | bytes 688136 | tf_op jit(solution)/shard_map/ppermute | solution.py:1104
  194.9 9.3 %collective-permute-start.32 = (bf16[8,184,128]{2,1,0:T(8,128)(2,1)S(1)}, bf16[8,184,128]{2,1,0:T(8,128)(2,1)S(1)}, u32[]{:S(2)}, u32[]{:S(2)}) collective-permute-start(bf16[8,184,128]{2,1,0:T(8,128)(2,1)S(1)} %slice.219), channel_id=1, source_target_pairs={{0,16},{1,17},{2,18},{3,19},{4,20},{5,21},{6,22},{7,23},{8,24},{9,... | collective-permute-start | bytes 1130504 | tf_op jit(solution)/shard_map/ppermute | solution.py:1104
  195.9 12.5 %collective-permute-start.34 = (bf16[2,4,184,128]{3,2,1,0:T(8,128)(2,1)S(1)}, bf16[2,4,184,128]{3,2,1,0:T(8,128)(2,1)S(1)}, u32[]{:S(2)}, u32[]{:S(2)}) collective-permute-start(bf16[2,4,184,128]{3,2,1,0:T(8,128)(2,1)S(1)} %slice_bitcast_fusion), channel_id=1, source_target_pairs={{0,8},{1,9},{2,10},{3,11},{4,12},{5,13},{6,14},{7,15},{8,0},{9,1},... | collective-permute-start | bytes 1130504 | tf_op jit(solution)/shard_map/ppermute | solution.py:1104
  201.8 14.3 %collective-permute-start.29 = (bf16[2,224,128]{2,1,0:T(8,128)(2,1)S(1)}, bf16[2,224,128]{2,1,0:T(8,128)(2,1)S(1)}, u32[]{:S(2)}, u32[]{:S(2)}) collective-permute-start(bf16[2,224,128]{2,1,0:T(8,128)(2,1)S(1)} %slice.214), channel_id=1, source_target_pairs={{0,4},{1,5},{2,6},{3,7},{4,0},{5,1},{6,2},{7,3},{8,12},{9,13},{10,... | collective-permute-start | bytes 344072 | tf_op jit(solution)/shard_map/ppermute | solution.py:1104
  214.2 8.6 %collective-permute-start.36 = (bf16[2,368,128]{2,1,0:T(8,128)(2,1)S(1)}, bf16[2,368,128]{2,1,0:T(8,128)(2,1)S(1)}, u32[]{:S(2)}, u32[]{:S(2)}) collective-permute-start(bf16[2,368,128]{2,1,0:T(8,128)(2,1)S(1)} %pad_maximum_fusion.8), channel_id=1, source_target_pairs={{0,4},{1,5},{2,6},{3,7},{4,0},{5,1},{6,2},{7,3},{8,12},{9,13},{10,... | collective-permute-start | bytes 565256 | tf_op jit(solution)/shard_map/ppermute | solution.py:1104
  (26 other events, 127.6 us)
where the time goes:
time: 229 us
  Pallas kernels  111 us (48%)
  waiting for transfers between devices  67 us (29%)
  starting transfers between devices  43 us (19%)
  local copies, waits for them, and re-layouts  3.02 us (1%)
  other arithmetic  2.83 us (1%)
    pallas_call x18, Pallas kernels, call(): pl.pallas_call(kernel, in_specs=[pl.BlockSpec(memory_space=pltpu.SMEM if...  107 us
    ppermute x38, waiting for transfers between devices, flip(): return lax.ppermute(values, axes, pairs)  67 us
    ppermute x38, starting transfers between devices, flip(): return lax.ppermute(values, axes, pairs)  43 us
  transfers between devices with their start and end apart: 38, of which 20 were waited for; matrix products, arithmetic and copies ran while one was open for 2% of the time, Pallas kernels for 20%

commit v1 on v0

--- a/solution.py
+++ b/solution.py
@@ -1103,10 +1103,13 @@
         pairs = [(i, ((i // group) ^ mask) * group + i % group) for i in range(devices)]
         return lax.ppermute(values, axes, pairs)
 
-    def gather(block, split=0):
+    def gather(block, split=0, direct=False):
         held = block[None]
-        for mask in FLIPS[:2]:
-            held = jnp.concatenate([held, flip(held, mask)], axis=0)
+        if direct:
+            held = jnp.concatenate([held, flip(held, 2), flip(held, 4), flip(held, 6)], axis=0)
+        else:
+            for mask in FLIPS[:2]:
+                held = jnp.concatenate([held, flip(held, mask)], axis=0)
         if split:
             one, two = held[:, :split], held[:, split:]
             one, two = (jnp.concatenate([one, flip(one, 8)], axis=0), jnp.concatenate([two, flip(two, 16)], axis=0))
@@ -1118,7 +1121,7 @@
                 held = jnp.concatenate([held, flip(held, mask)], axis=0)
         return held, flip(held, 1)
 
-    def scatter(keep, send, split=0):
+    def scatter(keep, send, split=0, direct=False):
         def step(held, mask):
             return flip(held, mask).astype(F32)
 
@@ -1137,6 +1140,9 @@
         else:
             held = halve(held, 16).astype(BF16)
             held = halve(held, 8).astype(BF16)
+        if direct:
+            far = step(held[2:3], 4), step(held[3:4], 6), step(held[1:2], 2)
+            return (held[0:1].astype(F32) + far[2] + far[0] + far[1])[0]
         held = halve(held, 4).astype(BF16)
         return halve(held, 2)[0]
 
@@ -1162,8 +1168,8 @@
     )
     block_b = select([rows(contract), rows(expand), taps], table_b, B_ROWS)
     block_c = select([rows(merge)], table_c, C_ROWS)
-    a_low, a_high = gather(block_a, A_SPLIT)
-    b_low, b_high = gather(block_b)
+    a_low, a_high = gather(block_a, A_SPLIT, True)
+    b_low, b_high = gather(block_b, B_ROWS // 2, True)
     c_low, c_high = gather(block_c, C_ROWS // 2)
 
     big, narrow = (D, TOKENS), (D, QUARTER)
@@ -1234,7 +1240,7 @@
         [((FF, 384), F32), ((32, 144, 128), F32), (big, BF16)],
         micros=9,
     )
-    sum_b = scatter(b_keep, b_send)
+    sum_b = scatter(b_keep, b_send, 0, True)
     mid_grad, low_grad, g_two = call(
         middle_back_kernel,
         (scal, bt, w1t, *hgs, end_grad, mid, stats_2),
@@ -1261,7 +1267,7 @@
         ],
         micros=11,
     )
-    sum_a = scatter(a_keep, a_send, A_SPLIT)
+    sum_a = scatter(a_keep, a_send, A_SPLIT, True)
     (token_grad,) = call(
         token_kernel,
         (scal, bt, first_grad, mid_grad, entry, stats_1),

time: 229 us -> 223 us (0.974)
  waiting for transfers between devices: 67 us -> 52.3 us
  starting transfers between devices: 43 us -> 51.3 us
    ppermute x38 -> x44, waiting for transfers between devices: 67 us -> 52.3 us  [flip(): return lax.ppermute(values, axes, pairs)]
    ppermute x38 -> x44, starting transfers between devices: 43 us -> 51.3 us  [flip(): return lax.ppermute(values, axes, pairs)]
  transfers between devices with their start and end apart: 38 -> 44, of which waited for: 20 -> 18; matrix products, arithmetic and copies ran while one was open for 2% -> 2% of each run, Pallas kernels for 20% -> 21%
where the time goes in v1:
time: 223 us; the launch traced here: 222 us
  Pallas kernels  111 us (50%)
  waiting for transfers between devices  52.3 us (23%)
  starting transfers between devices  51.3 us (23%)
  other arithmetic  2.85 us (1%)
  local copies, waits for them, and re-layouts  2.68 us (1%)
    pallas_call x18, Pallas kernels, call(): pl.pallas_call(kernel, in_specs=[pl.BlockSpec(memory_space=pltpu.SMEM if...  107 us
    ppermute x44, waiting for transfers between devices, flip(): return lax.ppermute(values, axes, pairs)  52.3 us
    ppermute x44, starting transfers between devices, flip(): return lax.ppermute(values, axes, pairs)  51.3 us
  transfers between devices with their start and end apart: 44, of which 18 were waited for; matrix products, arithmetic and copies ran while one was open for 2% of the time, Pallas kernels for 21%

profile of v1, /device:TPU:0, one launch (start us, length us, event | category | flops | bytes accessed | tf_op | source)
XLA Modules:
  0.0 222.3 jit_solution(8257712815623355662)
XLA Ops:
  3.1 2.9 %shard_map.274 = bf16[208,128]{1,0:T(8,128)(2,1)} custom-call(bf16[25,128]{1,0:T(8,128)(2,1)} %bitcast.91, bf16[25,128]{1,0:T(8,128)(2,1)} %bitcast.92, bf16[50,128]{1,0:T(8,128)(2,1)} %bitcast.90, bf16[100,128]{1,0:T(8,128)(2,1)} %bitcast.89, s32[2]{0:T(128)} %pad_add_fusion.refs_4_.scal, bf16[1,192]{1,0:T(2,128)(2,1)} %broadcast_in_dim.21.refs_5_, ...), custom_call_target="tpu_custom_call" | custom-call | flops 2000000000 | bytes 1000 | tf_op jit(solution)/shard_map/pallas_call | solution.py:148
  6.0 5.1 %collective-permute-start.2 = (bf16[1,208,128]{2,1,0:T(8,128)(2,1)}, bf16[1,208,128]{2,1,0:T(8,128)(2,1)S(1)}, u32[]{:S(2)}, u32[]{:S(2)}) collective-permute-start(bf16[1,208,128]{2,1,0:T(8,128)(2,1)} %bitcast.85), channel_id=1, source_target_pairs={{0,6},{1,7},{2,4},{3,5},{4,2},{5,3},{6,0},{7,1},{8,14},{9,15},{10,... | collective-permute-start | bytes 159752 | tf_op jit(solution)/shard_map/ppermute | solution.py:1104
  12.7 3.8 %collective-permute-start.17 = (bf16[1,224,128]{2,1,0:T(8,128)(2,1)S(1)}, bf16[1,224,128]{2,1,0:T(8,128)(2,1)S(1)}, u32[]{:S(2)}, u32[]{:S(2)}) collective-permute-start(bf16[1,224,128]{2,1,0:T(8,128)(2,1)S(1)} %bitcast.72), channel_id=1, source_target_pairs={{0,6},{1,7},{2,4},{3,5},{4,2},{5,3},{6,0},{7,1},{8,14},{9,15},{10,... | collective-permute-start | bytes 172040 | tf_op jit(solution)/shard_map/ppermute | solution.py:1104
  27.3 3.0 %collective-permute-start.9 = (bf16[2,368,128]{2,1,0:T(8,128)(2,1)S(1)}, bf16[2,368,128]{2,1,0:T(8,128)(2,1)S(1)}, u32[]{:S(2)}, u32[]{:S(2)}) collective-permute-start(bf16[2,368,128]{2,1,0:T(8,128)(2,1)S(1)} %pad_maximum_fusion.10), channel_id=1, source_target_pairs={{0,4},{1,5},{2,6},{3,7},{4,0},{5,1},{6,2},{7,3},{8,12},{9,13},{10,... | collective-permute-start | bytes 565256 | tf_op jit(solution)/shard_map/ppermute | solution.py:1104
  38.7 5.3 %collective-permute-done.12 = bf16[4,184,128]{2,1,0:T(8,128)(2,1)S(1)} collective-permute-done((bf16[4,184,128]{2,1,0:T(8,128)(2,1)S(1)}, bf16[4,184,128]{2,1,0:T(8,128)(2,1)S(1)}, u32[]{:S(2)}, u32[]{:S(2)}) %collective-permute-start.12) | collective-permute-done | bytes 188448 | tf_op jit(solution)/shard_map/ppermute | solution.py:1104
  46.5 6.3 %collective-permute-done.13 = bf16[8,184,128]{2,1,0:T(8,128)(2,1)S(1)} collective-permute-done((bf16[8,184,128]{2,1,0:T(8,128)(2,1)S(1)}, bf16[8,184,128]{2,1,0:T(8,128)(2,1)S(1)}, u32[]{:S(2)}, u32[]{:S(2)}) %collective-permute-start.13) | collective-permute-done | bytes 376864 | tf_op jit(solution)/shard_map/ppermute | solution.py:1104
  53.2 7.1 %shard_map.276 = (bf16[320,320]{1,0:T(8,128)(2,1)S(1)}, bf16[640,320]{1,0:T(8,128)(2,1)S(1)}, bf16[320,1280]{1,0:T(8,128)(2,1)S(1)}, bf16[320,320]{1,0:T(8,128)(...) custom-call(s32[2]{0:T(128)S(1)} %copy-done.9, ...), custom_call_target="tpu_custom_call" | custom-call | flops 8000000000 | bytes 1000 | tf_op jit(solution)/shard_map/pallas_call | solution.py:1083
  60.3 4.8 %shard_map.280 = (bf16[320,1024]{1,0:T(8,128)(2,1)S(1)}, f32[5,1,1024]{2,1,0:T(1,128)S(1)}) custom-call(s32[2]{0:T(128)S(1)} %copy-done.9, bf16[5,256,64]{2,1,0:T(8,128)(2,1)S(1)} %get-tuple-element.78.kt, bf16[320,1024]{1,0:T(8,128)(2,1)S(1)} %get-tuple-element.79.qs, bf16[640,256]{1,0:T(8,128)(2,1)S(1)} %get-tuple-element.80.kv), custom_call_target="tpu_custom_call" | custom-call | flops 8499999744 | bytes 1000 | tf_op jit(solution)/shard_map/pallas_call | solution.py:1083
  68.0 6.3 %shard_map.279 = (bf16[1280,384]{1,0:T(8,128)(2,1)S(1)}, bf16[320,1280]{1,0:T(8,128)(2,1)S(1)}, bf16[320,1280]{1,0:T(8,128)(2,1)S(1)}, bf16[1280,320]{1,0:T(8,128)(2,1)S(1)}, f32[10,1280,128]{2,1,0:T(8,128)S(1)}) custom-call(s32[2]{0:T(128)S(1)} %copy-done.9, f32[64,128]{1,0:T(8,128)S(1)} %get-tuple-element.73.bt, ...), custom_call_target="tpu_custom_call" | custom-call | flops 8000000000 | bytes 1000 | tf_op jit(solution)/shard_map/pallas_call | solution.py:1083
  74.3 10.0 %shard_map.282 = (bf16[1280,1024]{1,0:T(8,128)(2,1)S(1)}, bf16[1280,1024]{1,0:T(8,128)(2,1)S(1)}) custom-call(s32[2]{0:T(128)S(1)} %copy-done.9, bf16[1280,384]{1,0:T(8,128)(2,1)S(1)} %get-tuple-element.75.w1, f32[10,1280,128]{2,1,0:T(8,128)S(1)} %get-tuple-element.76.taps, bf16[384,1024]{1,0:T(8,128)(2,1)S(1)} %get-tuple-element.82.sec), custom_call_target="tpu_custom_call" | custom-call | flops 16999999488 | bytes 1000 | tf_op jit(solution)/shard_map/pallas_call | solution.py:1083
  84.3 3.3 %shard_map.283 = (f32[320,1024]{1,0:T(8,128)S(1)}, bf16[320,1024]{1,0:T(8,128)(2,1)S(1)}, f32[8,1024]{1,0:T(8,128)S(1)}) custom-call(s32[2]{0:T(128)S(1)} %copy-done.9, f32[64,128]{1,0:T(8,128)S(1)} %get-tuple-element.73.bt, bf16[320,1280]{1,0:T(8,128)(2,1)S(1)} %get-tuple-element.74.w2, bf16[1280,1024]{1,0:T(8,128)(2,1)S(1)} %get-tuple-element.83.act, ...), custom_call_target="tpu_custom_call" | custom-call | flops 5000000000 | bytes 1000 | tf_op jit(solution)/shard_map/pallas_call | solution.py:1083
  87.7 12.9 %shard_map.284 = (bf16[512,256]{1,0:T(8,128)(2,1)}, bf16[16,368,128]{2,1,0:T(8,128)(2,1)S(1)}, bf16[16,368,128]{2,1,0:T(8,128)(2,1)S(1)}, f32[320,1024]{1,0:T(8,...) custom-call(s32[2]{0:T(128)S(1)} %copy-done.9, f32[64,128]{1,0:T(8,128)S(1)} %get-tuple-element.73.bt, ...), custom_call_target="tpu_custom_call" | custom-call | flops 20000000000 | bytes 1000 | tf_op jit(solution)/shard_map/pallas_call | solution.py:1083
  100.6 4.6 %shard_map.285 = (bf16[256,1024]{1,0:T(8,128)(2,1)S(1)}, f32[256,128]{1,0:T(8,128)S(1)}) custom-call(s32[2]{0:T(128)S(1)} %copy-done.9, bf16[1280,384]{1,0:T(8,128)(2,1)S(1)} %get-tuple-element.75.w1, bf16[1280,320]{1,0:T(8,128)(2,1)S(1)} %get-tuple-element.98.w2t, f32[10,1280,128]{2,1,0:T(8,128)S(1)} %get-tuple-element.76.taps, ...), custom_call_target="tpu_custom_call" | custom-call | flops 6000000000 | bytes 1000 | tf_op jit(solution)/shard_map/pallas_call | solution.py:1083
  105.2 15.4 %shard_map.286 = (bf16[1024,1024]{1,0:T(8,128)(2,1)S(1)}, f32[1024,128]{1,0:T(8,128)S(1)}) custom-call(s32[2]{0:T(128)S(1)} %copy-done.9, bf16[1280,384]{1,0:T(8,128)(2,1)S(1)} %get-tuple-element.75.w1, bf16[1280,320]{1,0:T(8,128)(2,1)S(1)} %get-tuple-element.98.w2t, f32[10,1280,128]{2,1,0:T(8,128)S(1)} %get-tuple-element.76.taps, ...), custom_call_target="tpu_custom_call" | custom-call | flops 24000000000 | bytes 1000 | tf_op jit(solution)/shard_map/pallas_call | solution.py:1083
  120.6 6.6 %shard_map.289 = (bf16[16,224,128]{2,1,0:T(8,128)(2,1)S(1)}, bf16[16,224,128]{2,1,0:T(8,128)(2,1)S(1)}, f32[64,128]{1,0:T(8,128)S(1)}) custom-call(s32[2]{0:T(128)S(1)} %copy-done.9, bf16[256,1024]{1,0:T(8,128)(2,1)S(1)} %get-tuple-element.101.hg0, bf16[1024,1024]{1,0:T(8,128)(2,1)S(1)} %get-tuple-element.102.hg1, f32[256,128]{1,0:T(8,128)S(1)} %get-tuple-element.111.dk0, ...), custom_call_target="tpu_custom_call" | custom-call | flops 8999999488 | bytes 1000 | tf_op jit(solution)/shard_map/pallas_call | solution.py:1083
  127.2 3.7 %shard_map.287 = (f32[320,1024]{1,0:T(8,128)S(1)}, bf16[320,1024]{1,0:T(8,128)(2,1)S(1)}, f32[64,128]{1,0:T(8,128)S(1)}) custom-call(s32[2]{0:T(128)S(1)} %copy-done.9, f32[64,128]{1,0:T(8,128)S(1)} %get-tuple-element.73.bt, bf16[320,1280]{1,0:T(8,128)(2,1)S(1)} %get-tuple-element.97.w1t, bf16[256,1024]{1,0:T(8,128)(2,1)S(1)} %get-tuple-element.101.hg0, ...), custom_call_target="tpu_custom_call" | custom-call | flops 6000000000 | bytes 1000 | tf_op jit(solution)/shard_map/pallas_call | solution.py:1083
  130.9 8.9 %shard_map.288 = (bf16[320,1024]{1,0:T(8,128)(2,1)S(1)}, bf16[640,256]{1,0:T(8,128)(2,1)S(1)}) custom-call(s32[2]{0:T(128)S(1)} %copy-done.9, bf16[5,256,64]{2,1,0:T(8,128)(2,1)S(1)} %get-tuple-element.78.kt, bf16[5,256,64]{2,1,0:T(8,128)(2,1)S(1)} %get-tuple-element.96.vt, bf16[320,1024]{1,0:T(8,128)(2,1)S(1)} %get-tuple-element.79.qs, ...), custom_call_target="tpu_custom_call" | custom-call | flops 8999999488 | bytes 1000 | tf_op jit(solution)/shard_map/pallas_call | solution.py:1083
  139.8 8.8 %shard_map.290 = (bf16[16,208,128]{2,1,0:T(8,128)(2,1)S(1)}, bf16[16,208,128]{2,1,0:T(8,128)(2,1)S(1)}, f32[320,1024]{1,0:T(8,128)S(1)}) custom-call(s32[2]{0:T(128)S(1)} %copy-done.9, f32[64,128]{1,0:T(8,128)S(1)} %get-tuple-element.73.bt, bf16[320,320]{1,0:T(8,128)(2,1)S(1)} %get-tuple-element.89.wq, bf16[640,320]{1,0:T(8,128)(2,1)S(1)} %get-tuple-element.90.wkv, ...), custom_call_target="tpu_custom_call" | custom-call | flops 11000000512 | bytes 1000 | tf_op jit(solution)/shard_map/pallas_call | solution.py:1083
  155.7 4.0 %collective-permute-done.24 = bf16[8,104,128]{2,1,0:T(8,128)(2,1)S(1)} collective-permute-done((bf16[8,104,128]{2,1,0:T(8,128)(2,1)S(1)}, bf16[8,104,128]{2,1,0:T(8,128)(2,1)S(1)}, u32[]{:S(2)}, u32[]{:S(2)}) %collective-permute-start.24) | collective-permute-done | bytes 213024 | tf_op jit(solution)/shard_map/ppermute | solution.py:1104
  164.6 6.6 %collective-permute-done.27 = bf16[4,104,128]{2,1,0:T(8,128)(2,1)S(1)} collective-permute-done((bf16[4,104,128]{2,1,0:T(8,128)(2,1)S(1)}, bf16[4,104,128]{2,1,0:T(8,128)(2,1)S(1)}, u32[]{:S(2)}, u32[]{:S(2)}) %collective-permute-start.27) | collective-permute-done | bytes 106528 | tf_op jit(solution)/shard_map/ppermute | solution.py:1104
  174.8 5.2 %shard_map.291 = f32[320,1024]{1,0:T(8,128)} custom-call(s32[2]{0:T(128)S(1)} %copy-done.9, f32[64,128]{1,0:T(8,128)S(1)} %get-tuple-element.73.bt, f32[320,1024]{1,0:T(8,128)S(1)} %get-tuple-element.114.grad_in, f32[320,1024]{1,0:T(8,128)S(1)} %get-tuple-element.115.mid_grad, bf16[320,1024]{1,0:T(8,128)(2,1)S(1)} %get-tuple-element.71.entry, ...), custom_call_target="tpu_custom_call" | custom-call | flops 5000000000 | bytes 1000 | tf_op jit(solution)/shard_map/pallas_call | solution.py:1083
  185.9 4.5 %collective-permute-done.33 = bf16[4,224,128]{2,1,0:T(8,128)(2,1)S(1)} collective-permute-done((bf16[4,224,128]{2,1,0:T(8,128)(2,1)S(1)}, bf16[4,224,128]{2,1,0:T(8,128)(2,1)S(1)}, u32[]{:S(2)}, u32[]{:S(2)}) %collective-permute-start.33) | collective-permute-done | bytes 229408 | tf_op jit(solution)/shard_map/ppermute | solution.py:1104
  195.0 3.5 %collective-permute-done.40 = bf16[2,4,184,128]{3,2,1,0:T(8,128)(2,1)S(1)} collective-permute-done((bf16[2,4,184,128]{3,2,1,0:T(8,128)(2,1)S(1)}, bf16[2,4,184,128]{3,2,1,0:T(8,128)(2,1)S(1)}, u32[]{:S(2)}, u32[]{:S(2)}) %collective-permute-start.40) | collective-permute-done | bytes 376864 | tf_op jit(solution)/shard_map/ppermute | solution.py:1104
  210.2 6.1 %collective-permute-done.42 = bf16[2,368,128]{2,1,0:T(8,128)(2,1)S(1)} collective-permute-done((bf16[2,368,128]{2,1,0:T(8,128)(2,1)S(1)}, bf16[2,368,128]{2,1,0:T(8,128)(2,1)S(1)}, u32[]{:S(2)}, u32[]{:S(2)}) %collective-permute-start.42) | collective-permute-done | bytes 188448 | tf_op jit(solution)/shard_map/ppermute | solution.py:1104
  (167 shorter events, 71.5 us)
Async XLA Ops:
  6.0 13.8 %collective-permute-start.2 = (bf16[1,208,128]{2,1,0:T(8,128)(2,1)}, bf16[1,208,128]{2,1,0:T(8,128)(2,1)S(1)}, u32[]{:S(2)}, u32[]{:S(2)}) collective-permute-start(bf16[1,208,128]{2,1,0:T(8,128)(2,1)} %bitcast.85), channel_id=1, source_target_pairs={{0,6},{1,7},{2,4},{3,5},{4,2},{5,3},{6,0},{7,1},{8,14},{9,15},{10,... | collective-permute-start | bytes 159752 | tf_op jit(solution)/shard_map/ppermute | solution.py:1104
  11.2 9.4 %collective-permute-start.1 = (bf16[1,208,128]{2,1,0:T(8,128)(2,1)}, bf16[1,208,128]{2,1,0:T(8,128)(2,1)S(1)}, u32[]{:S(2)}, u32[]{:S(2)}) collective-permute-start(bf16[1,208,128]{2,1,0:T(8,128)(2,1)} %bitcast.86), channel_id=1, source_target_pairs={{0,4},{1,5},{2,6},{3,7},{4,0},{5,1},{6,2},{7,3},{8,12},{9,13},{10,... | collective-permute-start | bytes 159752 | tf_op jit(solution)/shard_map/ppermute | solution.py:1104
  11.2 10.8 %collective-permute-start = (bf16[1,208,128]{2,1,0:T(8,128)(2,1)}, bf16[1,208,128]{2,1,0:T(8,128)(2,1)S(1)}, u32[]{:S(2)}, u32[]{:S(2)}) collective-permute-start(bf16[1,208,128]{2,1,0:T(8,128)(2,1)} %bitcast.87), channel_id=1, source_target_pairs={{0,2},{1,3},{2,0},{3,1},{4,6},{5,7},{6,4},{7,5},{8,10},{9,11},{10,... | collective-permute-start | bytes 159752 | tf_op jit(solution)/shard_map/ppermute | solution.py:1104
  12.7 10.8 %collective-permute-start.17 = (bf16[1,224,128]{2,1,0:T(8,128)(2,1)S(1)}, bf16[1,224,128]{2,1,0:T(8,128)(2,1)S(1)}, u32[]{:S(2)}, u32[]{:S(2)}) collective-permute-start(bf16[1,224,128]{2,1,0:T(8,128)(2,1)S(1)} %bitcast.72), channel_id=1, source_target_pairs={{0,6},{1,7},{2,4},{3,5},{4,2},{5,3},{6,0},{7,1},{8,14},{9,15},{10,... | collective-permute-start | bytes 172040 | tf_op jit(solution)/shard_map/ppermute | solution.py:1104
  16.6 8.5 %collective-permute-start.16 = (bf16[1,224,128]{2,1,0:T(8,128)(2,1)S(1)}, bf16[1,224,128]{2,1,0:T(8,128)(2,1)S(1)}, u32[]{:S(2)}, u32[]{:S(2)}) collective-permute-start(bf16[1,224,128]{2,1,0:T(8,128)(2,1)S(1)} %bitcast.73), channel_id=1, source_target_pairs={{0,4},{1,5},{2,6},{3,7},{4,0},{5,1},{6,2},{7,3},{8,12},{9,13},{10,... | collective-permute-start | bytes 172040 | tf_op jit(solution)/shard_map/ppermute | solution.py:1104
  27.3 8.7 %collective-permute-start.9 = (bf16[2,368,128]{2,1,0:T(8,128)(2,1)S(1)}, bf16[2,368,128]{2,1,0:T(8,128)(2,1)S(1)}, u32[]{:S(2)}, u32[]{:S(2)}) collective-permute-start(bf16[2,368,128]{2,1,0:T(8,128)(2,1)S(1)} %pad_maximum_fusion.10), channel_id=1, source_target_pairs={{0,4},{1,5},{2,6},{3,7},{4,0},{5,1},{6,2},{7,3},{8,12},{9,13},{10,... | collective-permute-start | bytes 565256 | tf_op jit(solution)/shard_map/ppermute | solution.py:1104
  32.5 13.8 %collective-permute-start.19 = (bf16[8,112,128]{2,1,0:T(8,128)(2,1)S(1)}, bf16[8,112,128]{2,1,0:T(8,128)(2,1)S(1)}, u32[]{:S(2)}, u32[]{:S(2)}) collective-permute-start(bf16[8,112,128]{2,1,0:T(8,128)(2,1)S(1)} %pad_maximum_fusion.4), channel_id=1, source_target_pairs={{0,16},{1,17},{2,18},{3,19},{4,20},{5,21},{6,22},{7,23},{8,24},{9,... | collective-permute-start | bytes 688136 | tf_op jit(solution)/shard_map/ppermute | solution.py:1104
  33.1 11.7 %collective-permute-start.21 = (bf16[8,112,128]{2,1,0:T(8,128)(2,1)S(1)}, bf16[8,112,128]{2,1,0:T(8,128)(2,1)S(1)}, u32[]{:S(2)}, u32[]{:S(2)}) collective-permute-start(bf16[8,112,128]{2,1,0:T(8,128)(2,1)S(1)} %pad_maximum_fusion.5), channel_id=1, source_target_pairs={{0,8},{1,9},{2,10},{3,11},{4,12},{5,13},{6,14},{7,15},{8,0},{9,1},... | collective-permute-start | bytes 688136 | tf_op jit(solution)/shard_map/ppermute | solution.py:1104
  36.1 8.7 %collective-permute-start.10 = (bf16[4,184,128]{2,1,0:T(8,128)(2,1)S(1)}, bf16[4,184,128]{2,1,0:T(8,128)(2,1)S(1)}, u32[]{:S(2)}, u32[]{:S(2)}) collective-permute-start(bf16[4,184,128]{2,1,0:T(8,128)(2,1)S(1)} %get-tuple-element.130), channel_id=1, source_target_pairs={{0,8},{1,9},{2,10},{3,11},{4,12},{5,13},{6,14},{7,15},{8,0},{9,1},... | collective-permute-start | bytes 565256 | tf_op jit(solution)/shard_map/ppermute | solution.py:1104
  38.7 14.5 %collective-permute-start.7 = (bf16[16,208,128]{2,1,0:T(8,128)(2,1)S(1)}, bf16[16,208,128]{2,1,0:T(8,128)(2,1)S(1)}, u32[]{:S(2)}, u32[]{:S(2)}) collective-permute-start(bf16[16,208,128]{2,1,0:T(8,128)(2,1)S(1)} %maximum_maximum_fusion.2.low), channel_id=1, source_target_pairs={{0,1},{1,0},{2,3},{3,2},{4,5},{5,4},{6,7},{7,6},{8,9},{9,8},{10,11... | collective-permute-start | bytes 2555912 | tf_op jit(solution)/shard_map/ppermute | solution.py:1104
  44.1 8.6 %collective-permute-start.13 = (bf16[8,184,128]{2,1,0:T(8,128)(2,1)S(1)}, bf16[8,184,128]{2,1,0:T(8,128)(2,1)S(1)}, u32[]{:S(2)}, u32[]{:S(2)}) collective-permute-start(bf16[8,184,128]{2,1,0:T(8,128)(2,1)S(1)} %pad_maximum_fusion.2), channel_id=1, source_target_pairs={{0,8},{1,9},{2,10},{3,11},{4,12},{5,13},{6,14},{7,15},{8,0},{9,1},... | collective-permute-start | bytes 1130504 | tf_op jit(solution)/shard_map/ppermute | solution.py:1104
  46.4 21.5 %collective-permute-start.22 = (bf16[16,224,128]{2,1,0:T(8,128)(2,1)S(1)}, bf16[16,224,128]{2,1,0:T(8,128)(2,1)S(1)}, u32[]{:S(2)}, u32[]{:S(2)}) collective-permute-start(bf16[16,224,128]{2,1,0:T(8,128)(2,1)S(1)} %maximum_maximum_fusion.1.low), channel_id=1, source_target_pairs={{0,1},{1,0},{2,3},{3,2},{4,5},{5,4},{6,7},{7,6},{8,9},{9,8},{10,11... | collective-permute-start | bytes 2752520 | tf_op jit(solution)/shard_map/ppermute | solution.py:1104
  53.1 34.6 %collective-permute-start.14 = (bf16[16,368,128]{2,1,0:T(8,128)(2,1)S(1)}, bf16[16,368,128]{2,1,0:T(8,128)(2,1)S(1)}, u32[]{:S(2)}, u32[]{:S(2)}) collective-permute-start(bf16[16,368,128]{2,1,0:T(8,128)(2,1)S(1)} %maximum_maximum_fusion.c_low), channel_id=1, source_target_pairs={{0,1},{1,0},{2,3},{3,2},{4,5},{5,4},{6,7},{7,6},{8,9},{9,8},{10,11... | collective-permute-start | bytes 4521992 | tf_op jit(solution)/shard_map/ppermute | solution.py:1104
  149.3 34.0 %collective-permute-start.37 = (bf16[16,368,128]{2,1,0:T(8,128)(2,1)S(1)}, bf16[16,368,128]{2,1,0:T(8,128)(2,1)S(1)}, u32[]{:S(2)}, u32[]{:S(2)}) collective-permute-start(bf16[16,368,128]{2,1,0:T(8,128)(2,1)S(1)} %get-tuple-element.127), channel_id=1, source_target_pairs={{0,1},{1,0},{2,3},{3,2},{4,5},{5,4},{6,7},{7,6},{8,9},{9,8},{10,11... | collective-permute-start | bytes 4521992 | tf_op jit(solution)/shard_map/ppermute | solution.py:1104
  153.9 27.8 %collective-permute-start.32 = (bf16[8,224,128]{2,1,0:T(8,128)(2,1)S(1)}, bf16[8,224,128]{2,1,0:T(8,128)(2,1)S(1)}, u32[]{:S(2)}, u32[]{:S(2)}) collective-permute-start(bf16[8,224,128]{2,1,0:T(8,128)(2,1)S(1)} %slice.232), channel_id=1, source_target_pairs={{0,16},{1,17},{2,18},{3,19},{4,20},{5,21},{6,22},{7,23},{8,24},{9,... | collective-permute-start | bytes 1376264 | tf_op jit(solution)/shard_map/ppermute | solution.py:1104
  161.6 9.6 %collective-permute-start.27 = (bf16[4,104,128]{2,1,0:T(8,128)(2,1)S(1)}, bf16[4,104,128]{2,1,0:T(8,128)(2,1)S(1)}, u32[]{:S(2)}, u32[]{:S(2)}) collective-permute-start(bf16[4,104,128]{2,1,0:T(8,128)(2,1)S(1)} %slice_bitcast_fusion.6), channel_id=1, source_target_pairs={{0,16},{1,17},{2,18},{3,19},{4,20},{5,21},{6,22},{7,23},{8,24},{9,... | collective-permute-start | bytes 319496 | tf_op jit(solution)/shard_map/ppermute | solution.py:1104
  171.3 8.8 %collective-permute-start.28 = (bf16[1,208,128]{2,1,0:T(8,128)(2,1)S(1)}, bf16[1,208,128]{2,1,0:T(8,128)(2,1)S(1)}, u32[]{:S(2)}, u32[]{:S(2)}) collective-permute-start(bf16[1,208,128]{2,1,0:T(8,128)(2,1)S(1)} %get-tuple-element.141), channel_id=1, source_target_pairs={{0,2},{1,3},{2,0},{3,1},{4,6},{5,7},{6,4},{7,5},{8,10},{9,11},{10,... | collective-permute-start | bytes 159752 | tf_op jit(solution)/shard_map/ppermute | solution.py:1104
  181.9 8.5 %collective-permute-start.33 = (bf16[4,224,128]{2,1,0:T(8,128)(2,1)S(1)}, bf16[4,224,128]{2,1,0:T(8,128)(2,1)S(1)}, u32[]{:S(2)}, u32[]{:S(2)}) collective-permute-start(bf16[4,224,128]{2,1,0:T(8,128)(2,1)S(1)} %slice.234), channel_id=1, source_target_pairs={{0,8},{1,9},{2,10},{3,11},{4,12},{5,13},{6,14},{7,15},{8,0},{9,1},... | collective-permute-start | bytes 688136 | tf_op jit(solution)/shard_map/ppermute | solution.py:1104
  183.8 9.3 %collective-permute-start.38 = (bf16[8,184,128]{2,1,0:T(8,128)(2,1)S(1)}, bf16[8,184,128]{2,1,0:T(8,128)(2,1)S(1)}, u32[]{:S(2)}, u32[]{:S(2)}) collective-permute-start(bf16[8,184,128]{2,1,0:T(8,128)(2,1)S(1)} %slice.241), channel_id=1, source_target_pairs={{0,16},{1,17},{2,18},{3,19},{4,20},{5,21},{6,22},{7,23},{8,24},{9,... | collective-permute-start | bytes 1130504 | tf_op jit(solution)/shard_map/ppermute | solution.py:1104
  184.7 13.7 %collective-permute-start.40 = (bf16[2,4,184,128]{3,2,1,0:T(8,128)(2,1)S(1)}, bf16[2,4,184,128]{3,2,1,0:T(8,128)(2,1)S(1)}, u32[]{:S(2)}, u32[]{:S(2)}) collective-permute-start(bf16[2,4,184,128]{3,2,1,0:T(8,128)(2,1)S(1)} %slice_bitcast_fusion), channel_id=1, source_target_pairs={{0,8},{1,9},{2,10},{3,11},{4,12},{5,13},{6,14},{7,15},{8,0},{9,1},... | collective-permute-start | bytes 1130504 | tf_op jit(solution)/shard_map/ppermute | solution.py:1104
  204.3 11.9 %collective-permute-start.42 = (bf16[2,368,128]{2,1,0:T(8,128)(2,1)S(1)}, bf16[2,368,128]{2,1,0:T(8,128)(2,1)S(1)}, u32[]{:S(2)}, u32[]{:S(2)}) collective-permute-start(bf16[2,368,128]{2,1,0:T(8,128)(2,1)S(1)} %pad_maximum_fusion.9), channel_id=1, source_target_pairs={{0,4},{1,5},{2,6},{3,7},{4,0},{5,1},{6,2},{7,3},{8,12},{9,13},{10,... | collective-permute-start | bytes 565256 | tf_op jit(solution)/shard_map/ppermute | solution.py:1104
  206.6 9.8 %collective-permute-start.34 = (bf16[1,224,128]{2,1,0:T(8,128)(2,1)S(1)}, bf16[1,224,128]{2,1,0:T(8,128)(2,1)S(1)}, u32[]{:S(2)}, u32[]{:S(2)}) collective-permute-start(bf16[1,224,128]{2,1,0:T(8,128)(2,1)S(1)} %get-tuple-element.134), channel_id=1, source_target_pairs={{0,2},{1,3},{2,0},{3,1},{4,6},{5,7},{6,4},{7,5},{8,10},{9,11},{10,... | collective-permute-start | bytes 172040 | tf_op jit(solution)/shard_map/ppermute | solution.py:1104
  206.9 9.5 %collective-permute-start.36 = (bf16[1,224,128]{2,1,0:T(8,128)(2,1)S(1)}, bf16[1,224,128]{2,1,0:T(8,128)(2,1)S(1)}, u32[]{:S(2)}, u32[]{:S(2)}) collective-permute-start(bf16[1,224,128]{2,1,0:T(8,128)(2,1)S(1)} %get-tuple-element.135), channel_id=1, source_target_pairs={{0,6},{1,7},{2,4},{3,5},{4,2},{5,3},{6,0},{7,1},{8,14},{9,15},{10,... | collective-permute-start | bytes 172040 | tf_op jit(solution)/shard_map/ppermute | solution.py:1104
  208.9 8.6 %collective-permute-start.35 = (bf16[1,224,128]{2,1,0:T(8,128)(2,1)S(1)}, bf16[1,224,128]{2,1,0:T(8,128)(2,1)S(1)}, u32[]{:S(2)}, u32[]{:S(2)}) collective-permute-start(bf16[1,224,128]{2,1,0:T(8,128)(2,1)S(1)} %get-tuple-element.136), channel_id=1, source_target_pairs={{0,4},{1,5},{2,6},{3,7},{4,0},{5,1},{6,2},{7,3},{8,12},{9,13},{10,... | collective-permute-start | bytes 172040 | tf_op jit(solution)/shard_map/ppermute | solution.py:1104
  (32 other events, 198.3 us)

commit v2 on v1

--- a/solution.py
+++ b/solution.py
@@ -298,14 +298,6 @@
     return jnp.where(rest < 8, slot * 8 + rest, 248 + slot * 2 + rest)
 
 
-def from_tens(me):
-    return one_hot(iota((D, D), 1) == tens(iota((D, 1), 0), me))
-
-
-def to_tens(me):
-    return one_hot(iota((D, D), 0) == tens(iota((1, D), 1), me))
-
-
 def keyval_tens(row, me, upper):
     owner, rest = split_ten(row, 20, 3277)
     inside = (rest >= 10) if upper else (rest < 10)
@@ -314,6 +306,17 @@
 
 def rest_row(row):
     return 64 * ((row & 7) >> 1) + 2 * (row >> 3) + (row & 1)
+
+
+def orders_kernel(scal, from_tens, to_tens, from_lower, from_upper, to_lower, to_upper, from_rest, to_rest):
+    me = scal[0]
+    from_tens[...] = one_hot(iota((D, D), 1) == tens(iota((D, 1), 0), me))
+    to_tens[...] = one_hot(iota((D, D), 0) == tens(iota((1, D), 1), me))
+    for upper, down, up in ((False, from_lower, to_lower), (True, from_upper, to_upper)):
+        down[...] = one_hot(iota((2 * D, D), 1) == keyval_tens(iota((2 * D, 1), 0), me, upper))
+        up[...] = one_hot(iota((D, 2 * D), 0) == keyval_tens(iota((1, 2 * D), 1), me, upper))
+    from_rest[...] = one_hot(iota((256, 256), 0) == rest_row(iota((1, 256), 1)))
+    to_rest[...] = one_hot(iota((256, 256), 1) == rest_row(iota((256, 1), 0)))
 
 
 def norm(values, gain, shift):
@@ -337,13 +340,14 @@
     return jnp.where(row == 0, mean, jnp.where(row == 1, rstd, 0.0))
 
 
-def entry_kernel(scal, tokens, entry, stats):
+def entry_kernel(scal, tokens, entry, stats, turned):
     side = scal[1]
     for quad in range(4):
         lane = iota((1, 256), 1) + quad * 256
         row, col = token_place(lane)
         natural = row * SIDE + col
         pick = one_hot(iota((TOKENS, 256), 0) == natural)
+        turned[:, quad * 256 : quad * 256 + 256] = pick
         mask = jnp.where((row < side) & (col < side), 1.0, 0.0)
         entry[:, quad * 256 : quad * 256 + 256] = (dot(tokens[...], pick) * mask).astype(BF16)
 
@@ -376,7 +380,7 @@
     return jnp.transpose(rows)[0:64, :]
 
 
-def project_kernel(scal, low, high, entry, stats, wq, wkv, wrs, wo, first, qs, raw, stat_r, red, kv, kt, vt, bt, square, rest, redin):
+def project_kernel(scal, from_tens, from_lower, from_upper, from_rest, low, high, entry, stats, wq, wkv, wrs, wo, first, qs, raw, stat_r, red, kv, kt, vt, bt, square, rest, redin):
     me = scal[0]
     bt[...] = small_table(me, low, high)
     for half, source in enumerate((low, high)):
@@ -392,26 +396,20 @@
         for c in range(5):
             part = block[:, 8 * c : 8 * c + 8].reshape(128, 128).astype(BF16)
             rest[128 * half : 128 * half + 128, 128 * c : 128 * c + 128] = part
-    spread = one_hot(iota((256, 256), 0) == rest_row(iota((1, 256), 1)))
 
     def last_two(p):
-        part = dot(spread, rest[:, lanes(p)]).astype(BF16)
+        part = dot(from_rest[...], rest[:, lanes(p)]).astype(BF16)
         wrs[256:320, lanes(p, 256)] = jnp.concatenate([part[0:64], part[64:128]], axis=1)
         square[256:320, lanes(p, 256)] = jnp.concatenate([part[128:192], part[192:256]], axis=1)
 
     loop(5, last_two)
-    order = from_tens(me)
-    wq[:, 0:256] = dot(order, square[:, 0:256]).astype(BF16)
-    wo[:, 0:256] = dot(order, square[:, 1024:1280]).astype(BF16)
-    tails = dot(order, square[:, 768:1024])
+    wq[:, 0:256] = dot(from_tens[...], square[:, 0:256]).astype(BF16)
+    wo[:, 0:256] = dot(from_tens[...], square[:, 1024:1280]).astype(BF16)
+    tails = dot(from_tens[...], square[:, 768:1024])
     wq[:, 256:320] = tails[:, 0:64].astype(BF16)
     wo[:, 256:320] = pltpu.roll(tails, 64, 1)[:, 0:64].astype(BF16)
-    row = iota((2 * D, 1), 0)
-    place = iota((2 * D, D), 1)
-    lower = one_hot(place == keyval_tens(row, me, False))
-    upper = one_hot(place == keyval_tens(row, me, True))
-    wkv[:, 0:256] = (dot(lower, square[:, 256:512]) + dot(upper, square[:, 512:768])).astype(BF16)
-    tail = pltpu.roll(dot(lower, square[:, 768:896]), 64, 1) + dot(upper, square[:, 896:1024])
+    wkv[:, 0:256] = (dot(from_lower[...], square[:, 256:512]) + dot(from_upper[...], square[:, 512:768])).astype(BF16)
+    tail = pltpu.roll(dot(from_lower[...], square[:, 768:896]), 64, 1) + dot(from_upper[...], square[:, 896:1024])
     wkv[:, 256:320] = tail[:, 0:64].astype(BF16)
 
     gain, shift = column(bt, G_1, 5), column(bt, C_1, 5)
@@ -429,7 +427,7 @@
     total = bias
     for part in range(3):
         piece = mixed.astype(BF16)
-        total = total + dot(order, piece)
+        total = total + dot(from_tens[...], piece)
         mixed = mixed - piece.astype(F32)
     raw[...] = total
     gain, shift = column(bt, G_R, 5), column(bt, C_R, 5)
@@ -459,27 +457,36 @@
     return jnp.where((i < (side >> 1)) & (j < (side >> 1)), 0.0, -10000.0)
 
 
-def attend_kernel(scal, kt, qs, kv, att, lse, scores, probs):
+def head_rows(h):
+    return pl.ds(pl.multiple_of(64 * h, 64), 64)
+
+
+def attend_kernel(scal, kt, qs, kv, att, lse, scores_a, scores_b, probs_a, probs_b):
     bias = key_bias(scal[1])
 
-    def score(h, slot):
-        scores[slot] = dot(kt[h], qs[pl.ds(pl.multiple_of(64 * h, 64), 64), :])
-
-    score(0, 0)
-
-    def head(h):
-        score(jnp.minimum(h + 1, HEADS - 1), 1 - (h & 1))
-        rows = pl.ds(pl.multiple_of(64 * h, 64), 64)
-        values = kv[pl.ds(pl.multiple_of(D + 64 * h, 64), 64), :]
-        for tile in range(8):
+    def score(scores, h, start):
+        scores[...] = dot(kt[h], qs[head_rows(h), start : start + 512])
+
+    def finish(scores, probs, h, start):
+        for tile in range(4):
             at = slice(128 * tile, 128 * tile + 128)
-            part = scores[h & 1, :, at] + bias
+            to = slice(start + 128 * tile, start + 128 * tile + 128)
+            part = scores[:, at] + bias
             top = jnp.max(part, axis=0, keepdims=True)
             weights = jnp.exp(part - top)
             total = jnp.sum(weights, axis=0, keepdims=True)
-            lse[h, :, at] = top + jnp.log(total)
+            lse[h, :, to] = top + jnp.log(total)
             probs[:, at] = (weights * (1.0 / total)).astype(BF16)
-        att[rows, :] = dot(values, probs[...]).astype(BF16)
+        values = kv[pl.ds(pl.multiple_of(D + 64 * h, 64), 64), :]
+        att[head_rows(h), start : start + 512] = dot(values, probs[...]).astype(BF16)
+
+    score(scores_a, 0, 0)
+
+    def head(h):
+        score(scores_b, h, 512)
+        finish(scores_a, probs_a, h, 0)
+        score(scores_a, jnp.minimum(h + 1, HEADS - 1), 0)
+        finish(scores_b, probs_b, h, 512)
 
     loop(HEADS, head)
 
@@ -502,7 +509,7 @@
     loop(8, body)
 
 
-def ffn_weights_kernel(scal, bt, low, high, w1, w1t, w2, w2t, taps, main, rest, wide):
+def ffn_weights_kernel(scal, bt, from_tens, from_rest, low, high, w1, w1t, w2, w2t, taps, main, rest, wide):
     me = scal[0]
     for half, source in enumerate((low, high)):
         def chunks(p, half=half, source=source):
@@ -524,38 +531,33 @@
                 wide[rows, 128 * c : 128 * c + 128] = block[24 + 40 * c : 64 + 40 * c]
 
         loop(16, expansion)
-    spread = one_hot(iota((256, 256), 0) == rest_row(iota((1, 256), 1)))
     for j in range(3):
-        part = dot(spread, rest[:, 128 * j : 128 * j + 128]).astype(BF16)
+        part = dot(from_rest[...], rest[:, 128 * j : 128 * j + 128]).astype(BF16)
         for k in range(4 if j < 2 else 2):
             c = 4 * j + k
             main[256:320, 128 * c : 128 * c + 128] = part[64 * k : 64 * k + 64]
-    order = from_tens(me)
-
-    def contraction(p):
-        block = dot(order, main[:, lanes(p, 256)])
-        w2[:, lanes(p, 256)] = block.astype(BF16)
-        w2t[pl.ds(pl.multiple_of(256 * p, 256), 256), :] = jnp.transpose(block).astype(BF16)
-
-    loop(5, contraction)
-    bias = column(bt, B_1, 20)
-    lane = iota((FF, 128), 1)
-    tail = wide[:, 256:384]
-    low_tail = tail.astype(BF16)
+
+    def block(p):
+        rows = pl.ds(pl.multiple_of(256 * p, 256), 256)
+        full = dot(from_tens[...], main[:, lanes(p, 256)])
+        w2[:, lanes(p, 256)] = full.astype(BF16)
+        w2t[rows, :] = jnp.transpose(full).astype(BF16)
+        w1t[:, lanes(p, 256)] = jnp.transpose(wide[rows, :])[0:D].astype(BF16)
+
+    loop(5, block)
+    low_tail = wide[:, 256:384].astype(BF16)
 
     def spread(tap):
         taps[tap] = dot(low_tail, one_hot(iota((128, 128), 0) == 64 + tap))
 
     loop(9, spread)
-    taps[9] = column(bt, B_DW, 20)
     w1[:, 0:256] = wide[:, 0:256].astype(BF16)
-    w1[:, 256:384] = jnp.where(lane < 64, tail, jnp.where(lane == 73, bias, 0.0)).astype(BF16)
-
-    def turn(p):
-        rows = pl.ds(pl.multiple_of(256 * p, 256), 256)
-        w1t[:, lanes(p, 256)] = jnp.transpose(wide[rows, :])[0:D].astype(BF16)
-
-    loop(5, turn)
+    lane = iota((64, 128), 1)
+    for h in range(20):
+        rows = slice(64 * h, 64 * h + 64)
+        taps[9, rows, :] = jnp.broadcast_to(bt[:, B_DW + h : B_DW + h + 1], (64, 128))
+        beside = jnp.where(lane == 73, bt[:, B_1 + h : B_1 + h + 1], 0.0)
+        w1[rows, 256:384] = jnp.where(lane < 64, wide[rows, 256:384], beside).astype(BF16)
 
 
 def edge_masks():
@@ -753,7 +755,20 @@
     def patch_grad(start, width):
         back[pl.ds(start, width), :] = dot_tn(wm[:, pl.ds(start, width)], mg[...])
 
-    widths(patch_grad)
+
+    def give(start, width):
+        block = dot_nt(mg[...], patch[pl.ds(start, width), :]).astype(BF16)
+        for c in range(width // 128):
+            to = pl.ds(pl.multiple_of((start >> 3) + 16 * c, 16), 16)
+            part = block[:, 128 * c : 128 * c + 128].reshape(32, 16, 128)
+            keep[:, to, :] = part[0:16]
+            send[:, to, :] = part[16:32]
+
+    def both(start, width):
+        patch_grad(start, width)
+        give(start, width)
+
+    widths(both)
 
     def piece(n):
         return [back[D * n : D * n + D, 128 * half : 128 * half + 128] for half in range(2)]
@@ -774,7 +789,7 @@
     gain = column(bt, G_S, 5)
     zeros = jnp.zeros((D, 128), F32)
 
-    def body(tile, carry):
+    def one(tile):
         at = lanes(tile)
         mask = token_mask(tile, side)
         grad = end_grad[:, at] * mask
@@ -783,22 +798,16 @@
         end_grad[:, at] = result
         low = (result * mask).astype(BF16)
         branch[:, at] = low
-        return carry[0] + grad * hat, carry[1] + grad, carry[2] + low.astype(F32)
-
-    sums = lax.fori_loop(0, 8, body, (zeros, zeros, zeros))
+        return grad * hat, grad, low.astype(F32)
+
+    def body(step, carry):
+        pairs = zip(carry, one(2 * step), one(2 * step + 1))
+        return tuple(total + (x + y) for total, x, y in pairs)
+
+    sums = lax.fori_loop(0, 4, body, (zeros, zeros, zeros))
     put_column(grads, G_S, lane_sum(sums[0]))
     put_column(grads, C_S, lane_sum(sums[1]))
     put_column(grads, B_2, lane_sum(sums[2]))
-
-    def give(start, width):
-        block = dot_nt(mg[...], patch[pl.ds(start, width), :]).astype(BF16)
-        for c in range(width // 128):
-            to = pl.ds(pl.multiple_of((start >> 3) + 16 * c, 16), 16)
-            part = block[:, 128 * c : 128 * c + 128].reshape(32, 16, 128)
-            keep[:, to, :] = part[0:16]
-            send[:, to, :] = part[16:32]
-
-    widths(give)
 
 
 def ffn_back_kernel(first_part, count, scal, w1, w2t, taps, sec, slope, branch, hg, dkx, hid_a, hid_b, cg_a, cg_b):
@@ -868,7 +877,7 @@
     gain = column(bt, G_2, 5)
     zeros = jnp.zeros((D, 128), F32)
 
-    def body(tile, carry):
+    def one(tile):
         at = lanes(tile)
         mask = token_mask(tile, side)
         grad = work[:, at] * mask
@@ -877,15 +886,19 @@
         mid_grad[:, at] = result
         low = (result * mask).astype(BF16)
         low_grad[:, at] = low
-        return carry[0] + grad * hat, carry[1] + grad, carry[2] + low.astype(F32)
-
-    sums = lax.fori_loop(0, 8, body, (zeros, zeros, zeros))
+        return grad * hat, grad, low.astype(F32)
+
+    def body(step, carry):
+        pairs = zip(carry, one(2 * step), one(2 * step + 1))
+        return tuple(total + (x + y) for total, x, y in pairs)
+
+    sums = lax.fori_loop(0, 4, body, (zeros, zeros, zeros))
     put_column(grads, G_2, lane_sum(sums[0]))
     put_column(grads, C_2, lane_sum(sums[1]))
     put_column(grads, B_O, lane_sum(sums[2]))
 
 
-def pack_b_kernel(scal, hg0, hg1, dk0, dk1, sec, branch, act, keep, send, grads, dw1, gather, mixed):
+def pack_b_kernel(scal, to_tens, hg0, hg1, dk0, dk1, sec, branch, act, keep, send, grads, dw1, gather, mixed):
     me = scal[0]
     grads[...] = jnp.zeros_like(grads)
     lane = iota((256, 128), 1)
@@ -907,7 +920,7 @@
             grads[...] = table
 
         loop(count, outer)
-    mixed[...] = dot(to_tens(me), branch[...]).astype(BF16)
+    mixed[...] = dot(to_tens[...], branch[...]).astype(BF16)
     gather[:, 0:24, :] = jnp.zeros((32, 24, 128), F32)
 
     def contraction(p):
@@ -935,31 +948,42 @@
     send[:, 80:224, :] = gather[16:32].astype(BF16)
 
 
-def attend_back_kernel(scal, kt, vt, qs, kv, wo, low_grad, lse, dq, dkv, og):
+def attend_back_kernel(scal, kt, vt, qs, kv, wo, low_grad, lse, dq, dkv, og, scores_a, scores_b, grads_a, grads_b, probs_a, probs_b, back_a, back_b):
     bias = key_bias(scal[1])
     og[...] = dot_tn(wo[...], low_grad[...]).astype(BF16)
 
+    def score(scores, grads, h, start):
+        at = slice(start, start + 512)
+        scores[...] = dot(kt[h], qs[head_rows(h), at])
+        grads[...] = dot(vt[h], og[head_rows(h), at])
+
+    def finish(scores, grads, probs, back, h, start):
+        for tile in range(4):
+            at = slice(128 * tile, 128 * tile + 128)
+            to = slice(start + 128 * tile, start + 128 * tile + 128)
+            weights = jnp.exp(scores[:, at] + bias - lse[h, :, to])
+            grad = grads[:, at]
+            mean = jnp.sum(weights * grad, axis=0, keepdims=True)
+            back[:, at] = (weights * (grad - mean)).astype(BF16)
+            probs[:, at] = weights.astype(BF16)
+        rows, at = head_rows(h), slice(start, start + 512)
+        dq[rows, at] = (dot(kv[rows, :], back[...]) * 0.125).astype(BF16)
+        return dot_nt(qs[rows, at], back[...]), dot_nt(og[rows, at], probs[...])
+
+    score(scores_a, grads_a, 0, 0)
+
     def head(h):
-        rows = pl.ds(pl.multiple_of(64 * h, 64), 64)
-        more = pl.ds(pl.multiple_of(D + 64 * h, 64), 64)
-        dk = jnp.zeros((64, 256), F32)
-        dv = jnp.zeros((64, 256), F32)
-        for quad in range(4):
-            at = slice(256 * quad, 256 * quad + 256)
-            probs = jnp.exp(dot(kt[h], qs[rows, at]) + bias - lse[h, :, at])
-            grad = dot(vt[h], og[rows, at])
-            mean = jnp.sum(probs * grad, axis=0, keepdims=True)
-            score = (probs * (grad - mean)).astype(BF16)
-            dq[rows, at] = (dot(kv[rows, :], score) * 0.125).astype(BF16)
-            dk += dot_nt(qs[rows, at], score)
-            dv += dot_nt(og[rows, at], probs.astype(BF16))
-        dkv[rows, :] = dk.astype(BF16)
-        dkv[more, :] = dv.astype(BF16)
+        score(scores_b, grads_b, h, 512)
+        one = finish(scores_a, grads_a, probs_a, back_a, h, 0)
+        score(scores_a, grads_a, jnp.minimum(h + 1, HEADS - 1), 0)
+        two = finish(scores_b, grads_b, probs_b, back_b, h, 512)
+        dkv[head_rows(h), :] = (one[0] + two[0]).astype(BF16)
+        dkv[pl.ds(pl.multiple_of(D + 64 * h, 64), 64), :] = (one[1] + two[1]).astype(BF16)
 
     loop(HEADS, head)
 
 
-def first_kernel(scal, bt, wq, wkv, wrs, first, red, raw, stat_r, dq, dkv, low_grad, att, entry, stats, g_one, g_two, g_three, keep, send, work, grads, wide, redin, stack_r, stack_z, tails_of):
+def first_kernel(scal, bt, to_tens, to_lower, to_upper, to_rest, wq, wkv, wrs, first, red, raw, stat_r, dq, dkv, low_grad, att, entry, stats, g_one, g_two, g_three, keep, send, work, grads, wide, redin, stack_r, stack_z, tails_of):
     me = scal[0]
     grads[...] = g_one[...] + g_two[...] + g_three[...]
     for quad in range(4):
@@ -979,8 +1003,7 @@
     put_column(grads, C_R, lane_sum(sums[1]))
     put_column(grads, B_R, lane_sum(sums[2]))
     low = jnp.concatenate(lows, axis=1)
-    order = to_tens(me)
-    low = dot(order, low).astype(BF16)
+    low = dot(to_tens[...], low).astype(BF16)
     wide[...] = dot_tn(wrs[...], low)
     straight = dot_tn(wq[...], dq[...])
     for quad in range(4):
@@ -988,33 +1011,34 @@
         work[:, at] = straight[:, at] + wide[D * quad : D * quad + D, :]
     zeros = jnp.zeros((D, 128), F32)
 
-    def body(tile, carry):
+    def one(tile):
         at = lanes(tile)
         grad = work[:, at]
         hat = (entry[:, at].astype(F32) - stats[0:1, at]) * stats[1:2, at]
-        return carry[0] + grad * hat, carry[1] + grad, carry[2] + dq[:, at].astype(F32)
-
-    sums = lax.fori_loop(0, 8, body, (zeros, zeros, zeros))
+        return grad * hat, grad, dq[:, at].astype(F32)
+
+    def body(step, carry):
+        pairs = zip(carry, one(2 * step), one(2 * step + 1))
+        return tuple(total + (x + y) for total, x, y in pairs)
+
+    sums = lax.fori_loop(0, 4, body, (zeros, zeros, zeros))
     put_column(grads, G_1, lane_sum(sums[0]))
     put_column(grads, C_1, lane_sum(sums[1]))
     put_column(grads, B_Q, lane_sum(sums[2]))
     stack_r[...] = dot_nt(low, redin[...])
 
     def outer(pick, grad, value):
-        return dot_nt(dot(pick, grad[...]).astype(BF16), value[...])
-
-    row = iota((1, 2 * D), 1)
-    place = iota((D, 2 * D), 0)
+        return dot_nt(dot(pick[...], grad[...]).astype(BF16), value[...])
+
     parts = (
-        outer(order, dq, first),
-        outer(one_hot(place == keyval_tens(row, me, False)), dkv, red),
-        outer(one_hot(place == keyval_tens(row, me, True)), dkv, red),
-        outer(order, low_grad, att),
+        outer(to_tens, dq, first),
+        outer(to_lower, dkv, red),
+        outer(to_upper, dkv, red),
+        outer(to_tens, low_grad, att),
     )
     for part, at in zip(parts, (0, 256, 512, 1024)):
         stack_z[:, at : at + 256] = part[:, 0:256]
     stack_z[:, 768:1024] = jnp.concatenate([part[:, 256:320] for part in parts], axis=1)
-    spread = one_hot(iota((256, 256), 1) == rest_row(iota((256, 1), 0)))
 
     def pack(p):
         at = lanes(p, 256)
@@ -1029,7 +1053,7 @@
             [block[256:320, 128 * e : 128 * e + 128] for block in both for e in range(2)], axis=0
         ).astype(BF16)
         to = pl.ds(pl.multiple_of(8 * p, 8), 8)
-        tails_of[:, to, :] = dot(spread, tail).reshape(32, 8, 128)
+        tails_of[:, to, :] = dot(to_rest[...], tail).reshape(32, 8, 128)
 
     loop(5, pack)
     rows = jnp.transpose(jnp.concatenate([grads[...], jnp.zeros((64, 128), F32)], axis=0)).astype(BF16)
@@ -1050,7 +1074,7 @@
     send[:, 160:208, :] = tails_of[16:32].astype(BF16)
 
 
-def token_kernel(scal, bt, grad_in, mid_grad, entry, stats, tok, high, rest):
+def token_kernel(scal, bt, turned, grad_in, mid_grad, entry, stats, tok, high, rest):
     side = scal[1]
     gain = column(bt, G_1, 5)
 
@@ -1064,13 +1088,10 @@
         rest[:, at] = (result - upper.astype(F32)).astype(BF16)
 
     loop(8, body)
-    row, col = token_place(iota((TOKENS, 1), 0))
-    natural = row * SIDE + col
 
     def quad(index):
-        at = lanes(index, 256)
-        pick = one_hot(iota((TOKENS, 256), 1) + 256 * index == natural)
-        tok[:, at] = dot(high[...], pick) + dot(rest[...], pick)
+        pick = turned[pl.ds(pl.multiple_of(256 * index, 256), 256), :]
+        tok[:, lanes(index, 256)] = dot_nt(high[...], pick) + dot_nt(rest[...], pick)
 
     loop(4, quad)
 
@@ -1173,10 +1194,17 @@
     c_low, c_high = gather(block_c, C_ROWS // 2)
 
     big, narrow = (D, TOKENS), (D, QUARTER)
-    entry, stats_1 = call(entry_kernel, (scal, tokens[0]), [(big, BF16), ((8, TOKENS), F32)], micros=3.5)
+    from_tens, to_tens, from_lower, from_upper, to_lower, to_upper, from_rest, to_rest = call(
+        orders_kernel,
+        (scal,),
+        [((D, D), BF16)] * 2 + [((2 * D, D), BF16)] * 2 + [((D, 2 * D), BF16)] * 2 + [((256, 256), BF16)] * 2,
+        micros=2,
+    )
+    entry, stats_1, turned = call(
+        entry_kernel, (scal, tokens[0]), [(big, BF16), ((8, TOKENS), F32), ((TOKENS, TOKENS), BF16)], micros=3.5)
     wq, wkv, wr, wo, first, qs, raw, stat_r, red, kv, kt, vt, bt = call(
         project_kernel,
-        (scal, a_low, a_high, entry, stats_1),
+        (scal, from_tens, from_lower, from_upper, from_rest, a_low, a_high, entry, stats_1),
         [
             ((D, D), BF16), ((2 * D, D), BF16), ((D, 4 * D), BF16), ((D, D), BF16), (big, BF16), (big, BF16),
             (narrow, F32), ((8, QUARTER), F32), (narrow, BF16), ((2 * D, QUARTER), BF16),
@@ -1186,14 +1214,14 @@
         micros=8,
     )
     att, lse = call(attend_kernel, (scal, kt, qs, kv), [(big, BF16), ((HEADS, 1, TOKENS), F32)],
-        [((2, QUARTER, TOKENS), F32), ((QUARTER, TOKENS), BF16)], micros=8.5)
+        [((QUARTER, 512), F32)] * 2 + [((QUARTER, 512), BF16)] * 2, micros=8.5)
     mid, sec, stats_2 = call(
         middle_kernel, (scal, bt, wo, att, entry), [(big, F32), ((384, TOKENS), BF16), ((8, TOKENS), F32)], [(big, F32)],
         micros=5,
     )
     w1, w1t, w2, w2t, taps = call(
         ffn_weights_kernel,
-        (scal, bt, b_low, b_high),
+        (scal, bt, from_tens, from_rest, b_low, b_high),
         [((FF, 384), BF16), ((D, FF), BF16), ((D, FF), BF16), ((FF, D), BF16), ((10, FF, 128), F32)],
         [((D, FF), BF16), ((256, 384), BF16), ((FF, 384), F32)],
         micros=8,
@@ -1235,12 +1263,12 @@
         dks.append(dk)
     b_keep, b_send, g_three = call(
         pack_b_kernel,
-        (scal, *hgs, *dks, sec, branch, act),
+        (scal, to_tens, *hgs, *dks, sec, branch, act),
         [((16, B_ROWS, 128), BF16), ((16, B_ROWS, 128), BF16), ((64, 128), F32)],
         [((FF, 384), F32), ((32, 144, 128), F32), (big, BF16)],
         micros=9,
     )
-    sum_b = scatter(b_keep, b_send, 0, True)
+    sum_b = scatter(b_keep, b_send, B_ROWS // 2, True)
     mid_grad, low_grad, g_two = call(
         middle_back_kernel,
         (scal, bt, w1t, *hgs, end_grad, mid, stats_2),
@@ -1252,13 +1280,13 @@
         attend_back_kernel,
         (scal, kt, vt, qs, kv, wo, low_grad, lse),
         [(big, BF16), ((2 * D, QUARTER), BF16)],
-        [(big, BF16)],
+        [(big, BF16)] + [((QUARTER, 512), F32)] * 4 + [((QUARTER, 512), BF16)] * 4,
         micros=9,
     )
     a_keep, a_send, first_grad = call(
         first_kernel,
         (
-            scal, bt, wq, wkv, wr, first, red, raw, stat_r, dq, dkv, low_grad, att, entry, stats_1, g_one, g_two, g_three,
+            scal, bt, to_tens, to_lower, to_upper, to_rest, wq, wkv, wr, first, red, raw, stat_r, dq, dkv, low_grad, att, entry, stats_1, g_one, g_two, g_three,
         ),
         [((16, A_ROWS, 128), BF16), ((16, A_ROWS, 128), BF16), (big, F32)],
         [
@@ -1270,7 +1298,7 @@
     sum_a = scatter(a_keep, a_send, A_SPLIT, True)
     (token_grad,) = call(
         token_kernel,
-        (scal, bt, first_grad, mid_grad, entry, stats_1),
+        (scal, bt, turned, first_grad, mid_grad, entry, stats_1),
         [(big, F32)],
         [(big, BF16), (big, BF16)],
         micros=5,

time: 223 us -> 207 us (0.928)
  waiting for transfers between devices: 52.3 us -> 42.9 us
  Pallas kernels: 111 us -> 105 us
    ppermute x44 -> x46, waiting for transfers between devices: 52.3 us -> 42.9 us  [flip(): return lax.ppermute(values, axes, pairs)]
    pallas_call x18 -> x19, Pallas kernels: 107 us -> 101 us  [call(): pl.pallas_call(kernel, in_specs=[pl.BlockSpec(memory_space=pltpu.SMEM if...]
    ppermute x44 -> x46, starting transfers between devices: 51.3 us -> 51.5 us  [flip(): return lax.ppermute(values, axes, pairs)]
  transfers between devices with their start and end apart: 44 -> 46, of which waited for: 18 -> 18; matrix products, arithmetic and copies ran while one was open for 2% -> 2% of each run, Pallas kernels for 21% -> 22%
where the time goes in v2:
time: 207 us
  Pallas kernels  105 us (51%)
  starting transfers between devices  51.5 us (25%)
  waiting for transfers between devices  42.9 us (21%)
  other arithmetic  2.85 us (1%)
  local copies, waits for them, and re-layouts  2.73 us (1%)
  between operations  2.08 us (1%)
    pallas_call x19, Pallas kernels, call(): pl.pallas_call(kernel, in_specs=[pl.BlockSpec(memory_space=pltpu.SMEM if...  101 us
    ppermute x46, starting transfers between devices, flip(): return lax.ppermute(values, axes, pairs)  51.5 us
    ppermute x46, waiting for transfers between devices, flip(): return lax.ppermute(values, axes, pairs)  42.9 us
    pallas_call x3, Pallas kernels, select(): pl.pallas_call(functools.partial(select_kernel, len(sources), tuple(bases...  4.43 us
  transfers between devices with their start and end apart: 46, of which 18 were waited for; matrix products, arithmetic and copies ran while one was open for 2% of the time, Pallas kernels for 22%

profile of v2, /device:TPU:0, one launch (start us, length us, event | category | flops | bytes accessed | tf_op | source)
XLA Modules:
  0.0 207.2 jit_solution(7249303559937490970)
XLA Ops:
  3.1 2.9 %shard_map.275 = bf16[208,128]{1,0:T(8,128)(2,1)} custom-call(bf16[25,128]{1,0:T(8,128)(2,1)} %bitcast.112, bf16[25,128]{1,0:T(8,128)(2,1)} %bitcast.113, bf16[50,128]{1,0:T(8,128)(2,1)} %bitcast.111, bf16[100,128]{1,0:T(8,128)(2,1)} %bitcast.110, s32[2]{0:T(128)} %pad_add_fusion.scal.refs_4_, bf16[1,192]{1,0:T(2,128)(2,1)} %broadcast_in_dim.21.refs_5_, ...), custom_call_target="tpu_custom_call" | custom-call | flops 2000000000 | bytes 1000 | tf_op jit(solution)/shard_map/pallas_call | solution.py:148
  6.0 5.1 %collective-permute-start.2 = (bf16[1,208,128]{2,1,0:T(8,128)(2,1)}, bf16[1,208,128]{2,1,0:T(8,128)(2,1)S(1)}, u32[]{:S(2)}, u32[]{:S(2)}) collective-permute-start(bf16[1,208,128]{2,1,0:T(8,128)(2,1)} %bitcast.106), channel_id=1, source_target_pairs={{0,6},{1,7},{2,4},{3,5},{4,2},{5,3},{6,0},{7,1},{8,14},{9,15},{10,... | collective-permute-start | bytes 159752 | tf_op jit(solution)/shard_map/ppermute | solution.py:1125
  12.7 3.8 %collective-permute-start.17 = (bf16[1,224,128]{2,1,0:T(8,128)(2,1)S(1)}, bf16[1,224,128]{2,1,0:T(8,128)(2,1)S(1)}, u32[]{:S(2)}, u32[]{:S(2)}) collective-permute-start(bf16[1,224,128]{2,1,0:T(8,128)(2,1)S(1)} %bitcast.91), channel_id=1, source_target_pairs={{0,6},{1,7},{2,4},{3,5},{4,2},{5,3},{6,0},{7,1},{8,14},{9,15},{10,... | collective-permute-start | bytes 172040 | tf_op jit(solution)/shard_map/ppermute | solution.py:1125
  29.2 3.0 %collective-permute-start.9 = (bf16[2,368,128]{2,1,0:T(8,128)(2,1)S(1)}, bf16[2,368,128]{2,1,0:T(8,128)(2,1)S(1)}, u32[]{:S(2)}, u32[]{:S(2)}) collective-permute-start(bf16[2,368,128]{2,1,0:T(8,128)(2,1)S(1)} %pad_maximum_fusion.10), channel_id=1, source_target_pairs={{0,4},{1,5},{2,6},{3,7},{4,0},{5,1},{6,2},{7,3},{8,12},{9,13},{10,... | collective-permute-start | bytes 565256 | tf_op jit(solution)/shard_map/ppermute | solution.py:1125
  42.4 4.5 %collective-permute-done.12 = bf16[4,184,128]{2,1,0:T(8,128)(2,1)S(1)} collective-permute-done((bf16[4,184,128]{2,1,0:T(8,128)(2,1)S(1)}, bf16[4,184,128]{2,1,0:T(8,128)(2,1)S(1)}, u32[]{:S(2)}, u32[]{:S(2)}) %collective-permute-start.12) | collective-permute-done | bytes 188448 | tf_op jit(solution)/shard_map/ppermute | solution.py:1125
  49.3 5.4 %collective-permute-done.13 = bf16[8,184,128]{2,1,0:T(8,128)(2,1)S(1)} collective-permute-done((bf16[8,184,128]{2,1,0:T(8,128)(2,1)S(1)}, bf16[8,184,128]{2,1,0:T(8,128)(2,1)S(1)}, u32[]{:S(2)}, u32[]{:S(2)}) %collective-permute-start.13) | collective-permute-done | bytes 376864 | tf_op jit(solution)/shard_map/ppermute | solution.py:1125
  56.3 6.8 %shard_map.277 = (bf16[320,320]{1,0:T(8,128)(2,1)S(1)}, bf16[640,320]{1,0:T(8,128)(2,1)S(1)}, bf16[320,1280]{1,0:T(8,128)(2,1)S(1)}, bf16[320,320]{1,0:T(8,128)(...) custom-call(s32[2]{0:T(128)S(1)} %copy-done.9, ...), custom_call_target="tpu_custom_call" | custom-call | flops 8000000000 | bytes 1000 | tf_op jit(solution)/shard_map/pallas_call | solution.py:1104
  63.1 4.1 %shard_map.281 = (bf16[320,1024]{1,0:T(8,128)(2,1)S(1)}, f32[5,1,1024]{2,1,0:T(1,128)S(1)}) custom-call(s32[2]{0:T(128)S(1)} %copy-done.9, bf16[5,256,64]{2,1,0:T(8,128)(2,1)S(1)} %get-tuple-element.91.kt, bf16[320,1024]{1,0:T(8,128)(2,1)S(1)} %get-tuple-element.92.qs, bf16[640,256]{1,0:T(8,128)(2,1)S(1)} %get-tuple-element.93.kv), custom_call_target="tpu_custom_call" | custom-call | flops 8499999744 | bytes 1000 | tf_op jit(solution)/shard_map/pallas_call | solution.py:1104
  70.0 5.4 %shard_map.280 = (bf16[1280,384]{1,0:T(8,128)(2,1)S(1)}, bf16[320,1280]{1,0:T(8,128)(2,1)S(1)}, bf16[320,1280]{1,0:T(8,128)(2,1)S(1)}, bf16[1280,320]{1,0:T(8,128)(2,1)S(1)}, f32[10,1280,128]{2,1,0:T(8,128)S(1)}) custom-call(s32[2]{0:T(128)S(1)} %copy-done.9, f32[64,128]{1,0:T(8,128)S(1)} %get-tuple-element.86.bt, ...), custom_call_target="tpu_custom_call" | custom-call | flops 8000000000 | bytes 1000 | tf_op jit(solution)/shard_map/pallas_call | solution.py:1104
  75.5 10.2 %shard_map.283 = (bf16[1280,1024]{1,0:T(8,128)(2,1)S(1)}, bf16[1280,1024]{1,0:T(8,128)(2,1)S(1)}) custom-call(s32[2]{0:T(128)S(1)} %copy-done.9, bf16[1280,384]{1,0:T(8,128)(2,1)S(1)} %get-tuple-element.88.w1, f32[10,1280,128]{2,1,0:T(8,128)S(1)} %get-tuple-element.89.taps, bf16[384,1024]{1,0:T(8,128)(2,1)S(1)} %get-tuple-element.95.sec), custom_call_target="tpu_custom_call" | custom-call | flops 16999999488 | bytes 1000 | tf_op jit(solution)/shard_map/pallas_call | solution.py:1104
  85.7 3.1 %shard_map.284 = (f32[320,1024]{1,0:T(8,128)S(1)}, bf16[320,1024]{1,0:T(8,128)(2,1)S(1)}, f32[8,1024]{1,0:T(8,128)S(1)}) custom-call(s32[2]{0:T(128)S(1)} %copy-done.9, f32[64,128]{1,0:T(8,128)S(1)} %get-tuple-element.86.bt, bf16[320,1280]{1,0:T(8,128)(2,1)S(1)} %get-tuple-element.87.w2, bf16[1280,1024]{1,0:T(8,128)(2,1)S(1)} %get-tuple-element.96.act, ...), custom_call_target="tpu_custom_call" | custom-call | flops 5000000000 | bytes 1000 | tf_op jit(solution)/shard_map/pallas_call | solution.py:1104
  88.8 10.3 %shard_map.285 = (bf16[512,256]{1,0:T(8,128)(2,1)}, bf16[16,368,128]{2,1,0:T(8,128)(2,1)S(1)}, bf16[16,368,128]{2,1,0:T(8,128)(2,1)S(1)}, f32[320,1024]{1,0:T(8,...) custom-call(s32[2]{0:T(128)S(1)} %copy-done.9, f32[64,128]{1,0:T(8,128)S(1)} %get-tuple-element.86.bt, ...), custom_call_target="tpu_custom_call" | custom-call | flops 20000000000 | bytes 1000 | tf_op jit(solution)/shard_map/pallas_call | solution.py:1104
  99.1 4.6 %shard_map.286 = (bf16[256,1024]{1,0:T(8,128)(2,1)S(1)}, f32[256,128]{1,0:T(8,128)S(1)}) custom-call(s32[2]{0:T(128)S(1)} %copy-done.9, bf16[1280,384]{1,0:T(8,128)(2,1)S(1)} %get-tuple-element.88.w1, bf16[1280,320]{1,0:T(8,128)(2,1)S(1)} %get-tuple-element.116.w2t, f32[10,1280,128]{2,1,0:T(8,128)S(1)} %get-tuple-element.89.taps, ...), custom_call_target="tpu_custom_call" | custom-call | flops 6000000000 | bytes 1000 | tf_op jit(solution)/shard_map/pallas_call | solution.py:1104
  103.7 15.4 %shard_map.287 = (bf16[1024,1024]{1,0:T(8,128)(2,1)S(1)}, f32[1024,128]{1,0:T(8,128)S(1)}) custom-call(s32[2]{0:T(128)S(1)} %copy-done.9, bf16[1280,384]{1,0:T(8,128)(2,1)S(1)} %get-tuple-element.88.w1, bf16[1280,320]{1,0:T(8,128)(2,1)S(1)} %get-tuple-element.116.w2t, f32[10,1280,128]{2,1,0:T(8,128)S(1)} %get-tuple-element.89.taps, ...), custom_call_target="tpu_custom_call" | custom-call | flops 24000000000 | bytes 1000 | tf_op jit(solution)/shard_map/pallas_call | solution.py:1104
  119.1 3.4 %shard_map.288 = (f32[320,1024]{1,0:T(8,128)S(1)}, bf16[320,1024]{1,0:T(8,128)(2,1)S(1)}, f32[64,128]{1,0:T(8,128)S(1)}) custom-call(s32[2]{0:T(128)S(1)} %copy-done.9, f32[64,128]{1,0:T(8,128)S(1)} %get-tuple-element.86.bt, bf16[320,1280]{1,0:T(8,128)(2,1)S(1)} %get-tuple-element.115.w1t, bf16[256,1024]{1,0:T(8,128)(2,1)S(1)} %get-tuple-element.119.hg0, ...), custom_call_target="tpu_custom_call" | custom-call | flops 6000000000 | bytes 1000 | tf_op jit(solution)/shard_map/pallas_call | solution.py:1104
  122.5 6.6 %shard_map.290 = (bf16[16,224,128]{2,1,0:T(8,128)(2,1)S(1)}, bf16[16,224,128]{2,1,0:T(8,128)(2,1)S(1)}, f32[64,128]{1,0:T(8,128)S(1)}) custom-call(s32[2]{0:T(128)S(1)} %copy-done.9, bf16[320,320]{1,0:T(8,128)(2,1)S(1)} %get-tuple-element.103.to_tens, bf16[256,1024]{1,0:T(8,128)(2,1)S(1)} %get-tuple-element.119.hg0, ...), custom_call_target="tpu_custom_call" | custom-call | flops 8999999488 | bytes 1000 | tf_op jit(solution)/shard_map/pallas_call | solution.py:1104
  129.1 6.4 %shard_map.289 = (bf16[320,1024]{1,0:T(8,128)(2,1)S(1)}, bf16[640,256]{1,0:T(8,128)(2,1)S(1)}) custom-call(s32[2]{0:T(128)S(1)} %copy-done.9, bf16[5,256,64]{2,1,0:T(8,128)(2,1)S(1)} %get-tuple-element.91.kt, bf16[5,256,64]{2,1,0:T(8,128)(2,1)S(1)} %get-tuple-element.114.vt, bf16[320,1024]{1,0:T(8,128)(2,1)S(1)} %get-tuple-element.92.qs, ...), custom_call_target="tpu_custom_call" | custom-call | flops 8999999488 | bytes 1000 | tf_op jit(solution)/shard_map/pallas_call | solution.py:1104
  135.5 8.5 %shard_map.291 = (bf16[16,208,128]{2,1,0:T(8,128)(2,1)S(1)}, bf16[16,208,128]{2,1,0:T(8,128)(2,1)S(1)}, f32[320,1024]{1,0:T(8,128)S(1)}) custom-call(s32[2]{0:T(128)S(1)} %copy-done.9, f32[64,128]{1,0:T(8,128)S(1)} %get-tuple-element.86.bt, bf16[320,320]{1,0:T(8,128)(2,1)S(1)} %get-tuple-element.103.to_tens, ...), custom_call_target="tpu_custom_call" | custom-call | flops 11000000512 | bytes 1000 | tf_op jit(solution)/shard_map/pallas_call | solution.py:1104
  145.1 5.0 %shard_map.292 = f32[320,1024]{1,0:T(8,128)} custom-call(s32[2]{0:T(128)S(1)} %copy-done.9, f32[64,128]{1,0:T(8,128)S(1)} %get-tuple-element.86.bt, bf16[1024,1024]{1,0:T(8,128)(2,1)S(1)} %get-tuple-element.102.turned, f32[320,1024]{1,0:T(8,128)S(1)} %get-tuple-element.132.grad_in, f32[320,1024]{1,0:T(8,128)S(1)} %get-tuple-element.133.mid_grad, ...), custom_call_target="tpu_custom_call" | custom-call | flops 5000000000 | bytes 1000 | tf_op jit(solution)/shard_map/pallas_call | solution.py:1104
  155.1 3.5 %collective-permute-done.24 = bf16[8,104,128]{2,1,0:T(8,128)(2,1)S(1)} collective-permute-done((bf16[8,104,128]{2,1,0:T(8,128)(2,1)S(1)}, bf16[8,104,128]{2,1,0:T(8,128)(2,1)S(1)}, u32[]{:S(2)}, u32[]{:S(2)}) %collective-permute-start.24) | collective-permute-done | bytes 213024 | tf_op jit(solution)/shard_map/ppermute | solution.py:1125
  166.4 3.5 %collective-permute-start.30 = (bf16[1,208,128]{2,1,0:T(8,128)(2,1)S(1)}, bf16[1,208,128]{2,1,0:T(8,128)(2,1)S(1)}, u32[]{:S(2)}, u32[]{:S(2)}) collective-permute-start(bf16[1,208,128]{2,1,0:T(8,128)(2,1)S(1)} %get-tuple-element.160), channel_id=1, source_target_pairs={{0,6},{1,7},{2,4},{3,5},{4,2},{5,3},{6,0},{7,1},{8,14},{9,15},{10,... | collective-permute-start | bytes 159752 | tf_op jit(solution)/shard_map/ppermute | solution.py:1125
  178.0 6.6 %collective-permute-done.40 = bf16[8,184,128]{2,1,0:T(8,128)(2,1)S(1)} collective-permute-done((bf16[8,184,128]{2,1,0:T(8,128)(2,1)S(1)}, bf16[8,184,128]{2,1,0:T(8,128)(2,1)S(1)}, u32[]{:S(2)}, u32[]{:S(2)}) %collective-permute-start.40) | collective-permute-done | bytes 376864 | tf_op jit(solution)/shard_map/ppermute | solution.py:1125
  193.2 2.9 %collective-permute-start.36 = (bf16[1,224,128]{2,1,0:T(8,128)(2,1)S(1)}, bf16[1,224,128]{2,1,0:T(8,128)(2,1)S(1)}, u32[]{:S(2)}, u32[]{:S(2)}) collective-permute-start(bf16[1,224,128]{2,1,0:T(8,128)(2,1)S(1)} %get-tuple-element.152), channel_id=1, source_target_pairs={{0,2},{1,3},{2,0},{3,1},{4,6},{5,7},{6,4},{7,5},{8,10},{9,11},{10,... | collective-permute-start | bytes 172040 | tf_op jit(solution)/shard_map/ppermute | solution.py:1125
  197.7 3.5 %collective-permute-done.44 = bf16[2,368,128]{2,1,0:T(8,128)(2,1)S(1)} collective-permute-done((bf16[2,368,128]{2,1,0:T(8,128)(2,1)S(1)}, bf16[2,368,128]{2,1,0:T(8,128)(2,1)S(1)}, u32[]{:S(2)}, u32[]{:S(2)}) %collective-permute-start.44) | collective-permute-done | bytes 188448 | tf_op jit(solution)/shard_map/ppermute | solution.py:1125
  (189 shorter events, 70.6 us)
Async XLA Ops:
  6.0 15.8 %collective-permute-start.2 = (bf16[1,208,128]{2,1,0:T(8,128)(2,1)}, bf16[1,208,128]{2,1,0:T(8,128)(2,1)S(1)}, u32[]{:S(2)}, u32[]{:S(2)}) collective-permute-start(bf16[1,208,128]{2,1,0:T(8,128)(2,1)} %bitcast.106), channel_id=1, source_target_pairs={{0,6},{1,7},{2,4},{3,5},{4,2},{5,3},{6,0},{7,1},{8,14},{9,15},{10,... | collective-permute-start | bytes 159752 | tf_op jit(solution)/shard_map/ppermute | solution.py:1125
  11.2 11.4 %collective-permute-start.1 = (bf16[1,208,128]{2,1,0:T(8,128)(2,1)}, bf16[1,208,128]{2,1,0:T(8,128)(2,1)S(1)}, u32[]{:S(2)}, u32[]{:S(2)}) collective-permute-start(bf16[1,208,128]{2,1,0:T(8,128)(2,1)} %bitcast.107), channel_id=1, source_target_pairs={{0,4},{1,5},{2,6},{3,7},{4,0},{5,1},{6,2},{7,3},{8,12},{9,13},{10,... | collective-permute-start | bytes 159752 | tf_op jit(solution)/shard_map/ppermute | solution.py:1125
  11.2 12.8 %collective-permute-start = (bf16[1,208,128]{2,1,0:T(8,128)(2,1)}, bf16[1,208,128]{2,1,0:T(8,128)(2,1)S(1)}, u32[]{:S(2)}, u32[]{:S(2)}) collective-permute-start(bf16[1,208,128]{2,1,0:T(8,128)(2,1)} %bitcast.108), channel_id=1, source_target_pairs={{0,2},{1,3},{2,0},{3,1},{4,6},{5,7},{6,4},{7,5},{8,10},{9,11},{10,... | collective-permute-start | bytes 159752 | tf_op jit(solution)/shard_map/ppermute | solution.py:1125
  12.7 12.8 %collective-permute-start.17 = (bf16[1,224,128]{2,1,0:T(8,128)(2,1)S(1)}, bf16[1,224,128]{2,1,0:T(8,128)(2,1)S(1)}, u32[]{:S(2)}, u32[]{:S(2)}) collective-permute-start(bf16[1,224,128]{2,1,0:T(8,128)(2,1)S(1)} %bitcast.91), channel_id=1, source_target_pairs={{0,6},{1,7},{2,4},{3,5},{4,2},{5,3},{6,0},{7,1},{8,14},{9,15},{10,... | collective-permute-start | bytes 172040 | tf_op jit(solution)/shard_map/ppermute | solution.py:1125
  16.5 10.5 %collective-permute-start.16 = (bf16[1,224,128]{2,1,0:T(8,128)(2,1)S(1)}, bf16[1,224,128]{2,1,0:T(8,128)(2,1)S(1)}, u32[]{:S(2)}, u32[]{:S(2)}) collective-permute-start(bf16[1,224,128]{2,1,0:T(8,128)(2,1)S(1)} %bitcast.92), channel_id=1, source_target_pairs={{0,4},{1,5},{2,6},{3,7},{4,0},{5,1},{6,2},{7,3},{8,12},{9,13},{10,... | collective-permute-start | bytes 172040 | tf_op jit(solution)/shard_map/ppermute | solution.py:1125
  24.0 8.2 %collective-permute-start.3 = (bf16[4,104,128]{2,1,0:T(8,128)(2,1)S(1)}, bf16[4,104,128]{2,1,0:T(8,128)(2,1)S(1)}, u32[]{:S(2)}, u32[]{:S(2)}) collective-permute-start(bf16[4,104,128]{2,1,0:T(8,128)(2,1)S(1)} %get-tuple-element.162), channel_id=1, source_target_pairs={{0,8},{1,9},{2,10},{3,11},{4,12},{5,13},{6,14},{7,15},{8,0},{9,1},... | collective-permute-start | bytes 319496 | tf_op jit(solution)/shard_map/ppermute | solution.py:1125
  29.2 8.6 %collective-permute-start.9 = (bf16[2,368,128]{2,1,0:T(8,128)(2,1)S(1)}, bf16[2,368,128]{2,1,0:T(8,128)(2,1)S(1)}, u32[]{:S(2)}, u32[]{:S(2)}) collective-permute-start(bf16[2,368,128]{2,1,0:T(8,128)(2,1)S(1)} %pad_maximum_fusion.10), channel_id=1, source_target_pairs={{0,4},{1,5},{2,6},{3,7},{4,0},{5,1},{6,2},{7,3},{8,12},{9,13},{10,... | collective-permute-start | bytes 565256 | tf_op jit(solution)/shard_map/ppermute | solution.py:1125
  32.2 10.0 %collective-permute-start.4 = (bf16[8,104,128]{2,1,0:T(8,128)(2,1)S(1)}, bf16[8,104,128]{2,1,0:T(8,128)(2,1)S(1)}, u32[]{:S(2)}, u32[]{:S(2)}) collective-permute-start(bf16[8,104,128]{2,1,0:T(8,128)(2,1)S(1)} %pad_maximum_fusion.7), channel_id=1, source_target_pairs={{0,16},{1,17},{2,18},{3,19},{4,20},{5,21},{6,22},{7,23},{8,24},{9,... | collective-permute-start | bytes 638984 | tf_op jit(solution)/shard_map/ppermute | solution.py:1125
  32.9 8.1 %collective-permute-start.6 = (bf16[8,104,128]{2,1,0:T(8,128)(2,1)S(1)}, bf16[8,104,128]{2,1,0:T(8,128)(2,1)S(1)}, u32[]{:S(2)}, u32[]{:S(2)}) collective-permute-start(bf16[8,104,128]{2,1,0:T(8,128)(2,1)S(1)} %pad_maximum_fusion.8), channel_id=1, source_target_pairs={{0,8},{1,9},{2,10},{3,11},{4,12},{5,13},{6,14},{7,15},{8,0},{9,1},... | collective-permute-start | bytes 638984 | tf_op jit(solution)/shard_map/ppermute | solution.py:1125
  34.5 14.7 %collective-permute-start.19 = (bf16[8,112,128]{2,1,0:T(8,128)(2,1)S(1)}, bf16[8,112,128]{2,1,0:T(8,128)(2,1)S(1)}, u32[]{:S(2)}, u32[]{:S(2)}) collective-permute-start(bf16[8,112,128]{2,1,0:T(8,128)(2,1)S(1)} %pad_maximum_fusion.4), channel_id=1, source_target_pairs={{0,16},{1,17},{2,18},{3,19},{4,20},{5,21},{6,22},{7,23},{8,24},{9,... | collective-permute-start | bytes 688136 | tf_op jit(solution)/shard_map/ppermute | solution.py:1125
  35.1 13.3 %collective-permute-start.21 = (bf16[8,112,128]{2,1,0:T(8,128)(2,1)S(1)}, bf16[8,112,128]{2,1,0:T(8,128)(2,1)S(1)}, u32[]{:S(2)}, u32[]{:S(2)}) collective-permute-start(bf16[8,112,128]{2,1,0:T(8,128)(2,1)S(1)} %pad_maximum_fusion.5), channel_id=1, source_target_pairs={{0,8},{1,9},{2,10},{3,11},{4,12},{5,13},{6,14},{7,15},{8,0},{9,1},... | collective-permute-start | bytes 688136 | tf_op jit(solution)/shard_map/ppermute | solution.py:1125
  38.0 10.4 %collective-permute-start.10 = (bf16[4,184,128]{2,1,0:T(8,128)(2,1)S(1)}, bf16[4,184,128]{2,1,0:T(8,128)(2,1)S(1)}, u32[]{:S(2)}, u32[]{:S(2)}) collective-permute-start(bf16[4,184,128]{2,1,0:T(8,128)(2,1)S(1)} %get-tuple-element.148), channel_id=1, source_target_pairs={{0,8},{1,9},{2,10},{3,11},{4,12},{5,13},{6,14},{7,15},{8,0},{9,1},... | collective-permute-start | bytes 565256 | tf_op jit(solution)/shard_map/ppermute | solution.py:1125
  42.3 13.9 %collective-permute-start.7 = (bf16[16,208,128]{2,1,0:T(8,128)(2,1)S(1)}, bf16[16,208,128]{2,1,0:T(8,128)(2,1)S(1)}, u32[]{:S(2)}, u32[]{:S(2)}) collective-permute-start(bf16[16,208,128]{2,1,0:T(8,128)(2,1)S(1)} %maximum_maximum_fusion.2.low), channel_id=1, source_target_pairs={{0,1},{1,0},{2,3},{3,2},{4,5},{5,4},{6,7},{7,6},{8,9},{9,8},{10,11... | collective-permute-start | bytes 2555912 | tf_op jit(solution)/shard_map/ppermute | solution.py:1125
  49.2 20.8 %collective-permute-start.22 = (bf16[16,224,128]{2,1,0:T(8,128)(2,1)S(1)}, bf16[16,224,128]{2,1,0:T(8,128)(2,1)S(1)}, u32[]{:S(2)}, u32[]{:S(2)}) collective-permute-start(bf16[16,224,128]{2,1,0:T(8,128)(2,1)S(1)} %maximum_maximum_fusion.1.low), channel_id=1, source_target_pairs={{0,1},{1,0},{2,3},{3,2},{4,5},{5,4},{6,7},{7,6},{8,9},{9,8},{10,11... | collective-permute-start | bytes 2752520 | tf_op jit(solution)/shard_map/ppermute | solution.py:1125
  56.2 32.6 %collective-permute-start.14 = (bf16[16,368,128]{2,1,0:T(8,128)(2,1)S(1)}, bf16[16,368,128]{2,1,0:T(8,128)(2,1)S(1)}, u32[]{:S(2)}, u32[]{:S(2)}) collective-permute-start(bf16[16,368,128]{2,1,0:T(8,128)(2,1)S(1)} %maximum_maximum_fusion.c_low), channel_id=1, source_target_pairs={{0,1},{1,0},{2,3},{3,2},{4,5},{5,4},{6,7},{7,6},{8,9},{9,8},{10,11... | collective-permute-start | bytes 4521992 | tf_op jit(solution)/shard_map/ppermute | solution.py:1125
  144.6 31.7 %collective-permute-start.39 = (bf16[16,368,128]{2,1,0:T(8,128)(2,1)S(1)}, bf16[16,368,128]{2,1,0:T(8,128)(2,1)S(1)}, u32[]{:S(2)}, u32[]{:S(2)}) collective-permute-start(bf16[16,368,128]{2,1,0:T(8,128)(2,1)S(1)} %get-tuple-element.145), channel_id=1, source_target_pairs={{0,1},{1,0},{2,3},{3,2},{4,5},{5,4},{6,7},{7,6},{8,9},{9,8},{10,11... | collective-permute-start | bytes 4521992 | tf_op jit(solution)/shard_map/ppermute | solution.py:1125
  150.4 8.2 %collective-permute-start.24 = (bf16[8,104,128]{2,1,0:T(8,128)(2,1)S(1)}, bf16[8,104,128]{2,1,0:T(8,128)(2,1)S(1)}, u32[]{:S(2)}, u32[]{:S(2)}) collective-permute-start(bf16[8,104,128]{2,1,0:T(8,128)(2,1)S(1)} %slice.245), channel_id=1, source_target_pairs={{0,16},{1,17},{2,18},{3,19},{4,20},{5,21},{6,22},{7,23},{8,24},{9,... | collective-permute-start | bytes 638984 | tf_op jit(solution)/shard_map/ppermute | solution.py:1125
  151.2 8.3 %collective-permute-start.26 = (bf16[2,4,104,128]{3,2,1,0:T(8,128)(2,1)S(1)}, bf16[2,4,104,128]{3,2,1,0:T(8,128)(2,1)S(1)}, u32[]{:S(2)}, u32[]{:S(2)}) collective-permute-start(bf16[2,4,104,128]{3,2,1,0:T(8,128)(2,1)S(1)} %slice_bitcast_fusion.4), channel_id=1, source_target_pairs={{0,8},{1,9},{2,10},{3,11},{4,12},{5,13},{6,14},{7,15},{8,0},{9,1},... | collective-permute-start | bytes 638984 | tf_op jit(solution)/shard_map/ppermute | solution.py:1125
  152.8 10.8 %collective-permute-start.32 = (bf16[8,112,128]{2,1,0:T(8,128)(2,1)S(1)}, bf16[8,112,128]{2,1,0:T(8,128)(2,1)S(1)}, u32[]{:S(2)}, u32[]{:S(2)}) collective-permute-start(bf16[8,112,128]{2,1,0:T(8,128)(2,1)S(1)} %slice.260), channel_id=1, source_target_pairs={{0,16},{1,17},{2,18},{3,19},{4,20},{5,21},{6,22},{7,23},{8,24},{9,... | collective-permute-start | bytes 688136 | tf_op jit(solution)/shard_map/ppermute | solution.py:1125
  153.7 10.7 %collective-permute-start.34 = (bf16[2,4,112,128]{3,2,1,0:T(8,128)(2,1)S(1)}, bf16[2,4,112,128]{3,2,1,0:T(8,128)(2,1)S(1)}, u32[]{:S(2)}, u32[]{:S(2)}) collective-permute-start(bf16[2,4,112,128]{3,2,1,0:T(8,128)(2,1)S(1)} %slice_bitcast_fusion.2), channel_id=1, source_target_pairs={{0,8},{1,9},{2,10},{3,11},{4,12},{5,13},{6,14},{7,15},{8,0},{9,1},... | collective-permute-start | bytes 688136 | tf_op jit(solution)/shard_map/ppermute | solution.py:1125
  163.6 14.4 %collective-permute-start.33 = (bf16[4,112,128]{2,1,0:T(8,128)(2,1)S(1)}, bf16[4,112,128]{2,1,0:T(8,128)(2,1)S(1)}, u32[]{:S(2)}, u32[]{:S(2)}) collective-permute-start(bf16[4,112,128]{2,1,0:T(8,128)(2,1)S(1)} %slice.262), channel_id=1, source_target_pairs={{0,8},{1,9},{2,10},{3,11},{4,12},{5,13},{6,14},{7,15},{8,0},{9,1},... | collective-permute-start | bytes 344072 | tf_op jit(solution)/shard_map/ppermute | solution.py:1125
  170.5 22.6 %collective-permute-start.35 = (bf16[4,112,128]{2,1,0:T(8,128)(2,1)S(1)}, bf16[4,112,128]{2,1,0:T(8,128)(2,1)S(1)}, u32[]{:S(2)}, u32[]{:S(2)}) collective-permute-start(bf16[4,112,128]{2,1,0:T(8,128)(2,1)S(1)} %slice_bitcast_fusion.8), channel_id=1, source_target_pairs={{0,16},{1,17},{2,18},{3,19},{4,20},{5,21},{6,22},{7,23},{8,24},{9,... | collective-permute-start | bytes 344072 | tf_op jit(solution)/shard_map/ppermute | solution.py:1125
  177.5 9.7 %collective-permute-start.42 = (bf16[2,4,184,128]{3,2,1,0:T(8,128)(2,1)S(1)}, bf16[2,4,184,128]{3,2,1,0:T(8,128)(2,1)S(1)}, u32[]{:S(2)}, u32[]{:S(2)}) collective-permute-start(bf16[2,4,184,128]{3,2,1,0:T(8,128)(2,1)S(1)} %slice_bitcast_fusion), channel_id=1, source_target_pairs={{0,8},{1,9},{2,10},{3,11},{4,12},{5,13},{6,14},{7,15},{8,0},{9,1},... | collective-permute-start | bytes 1130504 | tf_op jit(solution)/shard_map/ppermute | solution.py:1125
  193.2 8.7 %collective-permute-start.36 = (bf16[1,224,128]{2,1,0:T(8,128)(2,1)S(1)}, bf16[1,224,128]{2,1,0:T(8,128)(2,1)S(1)}, u32[]{:S(2)}, u32[]{:S(2)}) collective-permute-start(bf16[1,224,128]{2,1,0:T(8,128)(2,1)S(1)} %get-tuple-element.152), channel_id=1, source_target_pairs={{0,2},{1,3},{2,0},{3,1},{4,6},{5,7},{6,4},{7,5},{8,10},{9,11},{10,... | collective-permute-start | bytes 172040 | tf_op jit(solution)/shard_map/ppermute | solution.py:1125
  (40 other events, 242.5 us)

commit v3 on v2

--- a/solution.py
+++ b/solution.py
@@ -62,6 +62,8 @@
 
 
 def lanes(index, width=128):
+    if isinstance(index, int):
+        return slice(index * width, (index + 1) * width)
     return pl.ds(pl.multiple_of(index * width, width), width)
 
 
@@ -421,6 +423,11 @@
     loop(8, body)
     for quad in range(4):
         redin[D * quad : D * quad + D, :] = first[:, 256 * quad : 256 * quad + 256]
+    bias = column(bt, B_Q, 5)
+    bias = jnp.concatenate([bias, bias], axis=1)
+    for quad in range(4):
+        at = lanes(quad, 256)
+        qs[:, at] = (dot(wq[...], first[:, at]) + bias).astype(BF16) * BF16(0.125)
     bias = column(bt, B_R, 5)
     bias = jnp.concatenate([bias, bias], axis=1)
     mixed = dot(wrs[...], redin[...])
@@ -442,14 +449,6 @@
     for h in range(HEADS):
         kt[h] = turned[:, 64 * h : 64 * h + 64].astype(BF16)
         vt[h] = turned[:, D + 64 * h : D + 64 * h + 64].astype(BF16)
-    bias = column(bt, B_Q, 5)
-    bias = jnp.concatenate([bias, bias], axis=1)
-
-    def query(quad):
-        at = lanes(quad, 256)
-        qs[:, at] = (dot(wq[...], first[:, at]) + bias).astype(BF16) * BF16(0.125)
-
-    loop(4, query)
 
 
 def key_bias(side):
@@ -493,7 +492,6 @@
 
 def middle_kernel(scal, bt, wo, att, entry, mid, sec, stats, work):
     side = scal[1]
-    work[...] = dot(wo[...], att[...])
     bias, gain, shift = column(bt, B_O, 5), column(bt, G_2, 5), column(bt, C_2, 5)
 
     def body(tile):
@@ -506,7 +504,11 @@
         sec[0:D, at] = (normed.astype(BF16).astype(F32) * mask).astype(BF16)
         sec[D : D + 64, at] = jnp.where(iota((64, 128), 0) == 9, mask, 0.0).astype(BF16)
 
-    loop(8, body)
+    for quad in range(4):
+        at = lanes(quad, 256)
+        work[:, at] = dot(wo[...], att[:, at])
+        body(2 * quad)
+        body(2 * quad + 1)
 
 
 def ffn_weights_kernel(scal, bt, from_tens, from_rest, low, high, w1, w1t, w2, w2t, taps, main, rest, wide):
@@ -538,19 +540,21 @@
             main[256:320, 128 * c : 128 * c + 128] = part[64 * k : 64 * k + 64]
 
     def block(p):
-        rows = pl.ds(pl.multiple_of(256 * p, 256), 256)
+        rows = lanes(p, 256)
         full = dot(from_tens[...], main[:, lanes(p, 256)])
         w2[:, lanes(p, 256)] = full.astype(BF16)
         w2t[rows, :] = jnp.transpose(full).astype(BF16)
         w1t[:, lanes(p, 256)] = jnp.transpose(wide[rows, :])[0:D].astype(BF16)
 
-    loop(5, block)
+    for p in range(5):
+        block(p)
     low_tail = wide[:, 256:384].astype(BF16)
 
     def spread(tap):
         taps[tap] = dot(low_tail, one_hot(iota((128, 128), 0) == 64 + tap))
 
-    loop(9, spread)
+    for tap in range(9):
+        spread(tap)
     w1[:, 0:256] = wide[:, 0:256].astype(BF16)
     lane = iota((64, 128), 1)
     for h in range(20):
@@ -660,7 +664,6 @@
 
 def ending_kernel(scal, bt, w2, act, mid, end, sect, stats, work):
     side = scal[1]
-    work[...] = dot(w2[...], act[...])
     bias, gain, shift = column(bt, B_2, 5), column(bt, G_S, 5), column(bt, C_S, 5)
 
     def body(tile):
@@ -672,7 +675,11 @@
         stats[:, at] = stat_rows(mean, rstd)
         sect[:, at] = (normed.astype(BF16).astype(F32) * mask).astype(BF16)
 
-    loop(8, body)
+    for quad in range(4):
+        at = lanes(quad, 256)
+        work[:, at] = dot(w2[...], act[:, at])
+        body(2 * quad)
+        body(2 * quad + 1)
 
 
 def lane_sum(values):
@@ -800,11 +807,10 @@
         branch[:, at] = low
         return grad * hat, grad, low.astype(F32)
 
-    def body(step, carry):
-        pairs = zip(carry, one(2 * step), one(2 * step + 1))
-        return tuple(total + (x + y) for total, x, y in pairs)
-
-    sums = lax.fori_loop(0, 4, body, (zeros, zeros, zeros))
+    sums = (zeros, zeros, zeros)
+    for step in range(4):
+        pairs = zip(sums, one(2 * step), one(2 * step + 1))
+        sums = tuple(total + (x + y) for total, x, y in pairs)
     put_column(grads, G_S, lane_sum(sums[0]))
     put_column(grads, C_S, lane_sum(sums[1]))
     put_column(grads, B_2, lane_sum(sums[2]))
@@ -870,9 +876,6 @@
 
 def middle_back_kernel(scal, bt, w1t, hg0, hg1, end_grad, mid, stats, mid_grad, low_grad, grads, work):
     side = scal[1]
-    work[...] = sum(
-        dot(w1t[:, 256 * at : 256 * (at + count)], hg[...]) for hg, (at, count) in zip((hg0, hg1), PARTS)
-    )
     grads[...] = jnp.zeros_like(grads)
     gain = column(bt, G_2, 5)
     zeros = jnp.zeros((D, 128), F32)
@@ -888,11 +891,14 @@
         low_grad[:, at] = low
         return grad * hat, grad, low.astype(F32)
 
-    def body(step, carry):
-        pairs = zip(carry, one(2 * step), one(2 * step + 1))
-        return tuple(total + (x + y) for total, x, y in pairs)
-
-    sums = lax.fori_loop(0, 4, body, (zeros, zeros, zeros))
+    sums = (zeros, zeros, zeros)
+    for quad in range(4):
+        at = lanes(quad, 256)
+        work[:, at] = sum(
+            dot(w1t[:, 256 * start : 256 * (start + count)], hg[:, at]) for hg, (start, count) in zip((hg0, hg1), PARTS)
+        )
+        pairs = zip(sums, one(2 * quad), one(2 * quad + 1))
+        sums = tuple(total + (x + y) for total, x, y in pairs)
     put_column(grads, G_2, lane_sum(sums[0]))
     put_column(grads, C_2, lane_sum(sums[1]))
     put_column(grads, B_O, lane_sum(sums[2]))
@@ -902,6 +908,21 @@
     me = scal[0]
     grads[...] = jnp.zeros_like(grads)
     lane = iota((256, 128), 1)
+    mixed[...] = dot(to_tens[...], branch[...]).astype(BF16)
+    gather[:, 0:24, :] = jnp.zeros((32, 24, 128), F32)
+
+    def contraction(p):
+        block = dot_nt(mixed[...], act[pl.ds(pl.multiple_of(256 * p, 256), 256), :])
+        parts = [block[0:256, 128 * e : 128 * e + 128].reshape(32, 1, 8, 128) for e in range(2)]
+        full = jnp.concatenate(parts, axis=1).reshape(32, 16, 128).astype(BF16)
+        to = pl.ds(pl.multiple_of(16 * p, 16), 16)
+        keep[:, to, :] = full[0:16]
+        send[:, to, :] = full[16:32]
+        tail = jnp.concatenate([block[256:320, 0:128], block[256:320, 128:256]], axis=0).astype(BF16)
+        place = rest_row(iota((256, 1), 0)) - 128 * (p & 1)
+        to = pl.ds(pl.multiple_of(8 * (p >> 1), 8), 8)
+        gather[:, to, :] += dot(one_hot(iota((256, 128), 1) == place), tail).reshape(32, 8, 128)
+
     for hg, dkx, (at, count) in zip((hg0, hg1), (dk0, dk1), PARTS):
 
         def outer(n, hg=hg, dkx=dkx, at=at):
@@ -918,24 +939,9 @@
                 table = jnp.where(lane[here] == B_1 + number, part[here, 329:330], table)
                 table = jnp.where(lane[here] == B_DW + number, dkx[rows, :][here, 9:10], table)
             grads[...] = table
+            contraction(n + at)
 
         loop(count, outer)
-    mixed[...] = dot(to_tens[...], branch[...]).astype(BF16)
-    gather[:, 0:24, :] = jnp.zeros((32, 24, 128), F32)
-
-    def contraction(p):
-        block = dot_nt(mixed[...], act[pl.ds(pl.multiple_of(256 * p, 256), 256), :])
-        parts = [block[0:256, 128 * e : 128 * e + 128].reshape(32, 1, 8, 128) for e in range(2)]
-        full = jnp.concatenate(parts, axis=1).reshape(32, 16, 128).astype(BF16)
-        to = pl.ds(pl.multiple_of(16 * p, 16), 16)
-        keep[:, to, :] = full[0:16]
-        send[:, to, :] = full[16:32]
-        tail = jnp.concatenate([block[256:320, 0:128], block[256:320, 128:256]], axis=0).astype(BF16)
-        place = rest_row(iota((256, 1), 0)) - 128 * (p & 1)
-        to = pl.ds(pl.multiple_of(8 * (p >> 1), 8), 8)
-        gather[:, to, :] += dot(one_hot(iota((256, 128), 1) == place), tail).reshape(32, 8, 128)
-
-    loop(5, contraction)
 
     def expansion(owner):
         slot = slot_of(owner ^ me)
@@ -1017,11 +1023,10 @@
         hat = (entry[:, at].astype(F32) - stats[0:1, at]) * stats[1:2, at]
         return grad * hat, grad, dq[:, at].astype(F32)
 
-    def body(step, carry):
-        pairs = zip(carry, one(2 * step), one(2 * step + 1))
-        return tuple(total + (x + y) for total, x, y in pairs)
-
-    sums = lax.fori_loop(0, 4, body, (zeros, zeros, zeros))
+    sums = (zeros, zeros, zeros)
+    for step in range(4):
+        pairs = zip(sums, one(2 * step), one(2 * step + 1))
+        sums = tuple(total + (x + y) for total, x, y in pairs)
     put_column(grads, G_1, lane_sum(sums[0]))
     put_column(grads, C_1, lane_sum(sums[1]))
     put_column(grads, B_Q, lane_sum(sums[2]))
@@ -1087,7 +1092,8 @@
         high[:, at] = upper
         rest[:, at] = (result - upper.astype(F32)).astype(BF16)
 
-    loop(8, body)
+    for tile in range(8):
+        body(tile)
 
     def quad(index):
         pick = turned[pl.ds(pl.multiple_of(256 * index, 256), 256), :]

time: 207 us -> 196 us (0.947)
  Pallas kernels: 105 us -> 93.4 us
    pallas_call x19, Pallas kernels: 101 us -> 88.9 us  [call(): pl.pallas_call(kernel, in_specs=[pl.BlockSpec(memory_space=pltpu.SMEM if...]
  transfers between devices with their start and end apart: 46 -> 46, of which waited for: 18 -> 18; matrix products, arithmetic and copies ran while one was open for 2% -> 2% of each run, Pallas kernels for 22% -> 21%
where the time goes in v3:
time: 196 us; the launch traced here: 195 us
  Pallas kernels  93.4 us (48%)
  starting transfers between devices  51.5 us (26%)
  waiting for transfers between devices  42.9 us (22%)
  other arithmetic  2.85 us (1%)
  local copies, waits for them, and re-layouts  2.73 us (1%)
  between operations  2.07 us (1%)
    pallas_call x19, Pallas kernels, call(): pl.pallas_call(kernel, in_specs=[pl.BlockSpec(memory_space=pltpu.SMEM if...  88.9 us
    ppermute x46, starting transfers between devices, flip(): return lax.ppermute(values, axes, pairs)  51.5 us
    ppermute x46, waiting for transfers between devices, flip(): return lax.ppermute(values, axes, pairs)  42.9 us
    pallas_call x3, Pallas kernels, select(): pl.pallas_call(functools.partial(select_kernel, len(sources), tuple(bases...  4.43 us
  transfers between devices with their start and end apart: 46, of which 18 were waited for; matrix products, arithmetic and copies ran while one was open for 2% of the time, Pallas kernels for 21%

profile of v3, /device:TPU:0, one launch (start us, length us, event | category | flops | bytes accessed | tf_op | source)
XLA Modules:
  0.0 195.5 jit_solution(16828883861113010525)
XLA Ops:
  3.1 2.9 %shard_map.275 = bf16[208,128]{1,0:T(8,128)(2,1)} custom-call(bf16[25,128]{1,0:T(8,128)(2,1)} %bitcast.112, bf16[25,128]{1,0:T(8,128)(2,1)} %bitcast.113, bf16[50,128]{1,0:T(8,128)(2,1)} %bitcast.111, bf16[100,128]{1,0:T(8,128)(2,1)} %bitcast.110, s32[2]{0:T(128)} %pad_add_fusion.scal.refs_4_, bf16[1,192]{1,0:T(2,128)(2,1)} %broadcast_in_dim.21.refs_5_, ...), custom_call_target="tpu_custom_call" | custom-call | flops 2000000000 | bytes 1000 | tf_op jit(solution)/shard_map/pallas_call | solution.py:150
  6.0 5.1 %collective-permute-start.2 = (bf16[1,208,128]{2,1,0:T(8,128)(2,1)}, bf16[1,208,128]{2,1,0:T(8,128)(2,1)S(1)}, u32[]{:S(2)}, u32[]{:S(2)}) collective-permute-start(bf16[1,208,128]{2,1,0:T(8,128)(2,1)} %bitcast.106), channel_id=1, source_target_pairs={{0,6},{1,7},{2,4},{3,5},{4,2},{5,3},{6,0},{7,1},{8,14},{9,15},{10,... | collective-permute-start | bytes 159752 | tf_op jit(solution)/shard_map/ppermute | solution.py:1131
  12.7 3.8 %collective-permute-start.17 = (bf16[1,224,128]{2,1,0:T(8,128)(2,1)S(1)}, bf16[1,224,128]{2,1,0:T(8,128)(2,1)S(1)}, u32[]{:S(2)}, u32[]{:S(2)}) collective-permute-start(bf16[1,224,128]{2,1,0:T(8,128)(2,1)S(1)} %bitcast.91), channel_id=1, source_target_pairs={{0,6},{1,7},{2,4},{3,5},{4,2},{5,3},{6,0},{7,1},{8,14},{9,15},{10,... | collective-permute-start | bytes 172040 | tf_op jit(solution)/shard_map/ppermute | solution.py:1131
  18.3 2.5 %shard_map.276 = (bf16[320,1024]{1,0:T(8,128)(2,1)S(1)}, f32[8,1024]{1,0:T(8,128)S(1)}, bf16[1024,1024]{1,0:T(8,128)(2,1)S(1)}) custom-call(s32[2]{0:T(128)S(1)} %copy-done.9, bf16[320,1024]{1,0:T(8,128)(2,1)S(1)} %bitcast.95), custom_call_target="tpu_custom_call" | custom-call | flops 3500000000 | bytes 1000 | tf_op jit(solution)/shard_map/pallas_call | solution.py:1110
  29.2 3.0 %collective-permute-start.9 = (bf16[2,368,128]{2,1,0:T(8,128)(2,1)S(1)}, bf16[2,368,128]{2,1,0:T(8,128)(2,1)S(1)}, u32[]{:S(2)}, u32[]{:S(2)}) collective-permute-start(bf16[2,368,128]{2,1,0:T(8,128)(2,1)S(1)} %pad_maximum_fusion.10), channel_id=1, source_target_pairs={{0,4},{1,5},{2,6},{3,7},{4,0},{5,1},{6,2},{7,3},{8,12},{9,13},{10,... | collective-permute-start | bytes 565256 | tf_op jit(solution)/shard_map/ppermute | solution.py:1131
  42.4 4.5 %collective-permute-done.12 = bf16[4,184,128]{2,1,0:T(8,128)(2,1)S(1)} collective-permute-done((bf16[4,184,128]{2,1,0:T(8,128)(2,1)S(1)}, bf16[4,184,128]{2,1,0:T(8,128)(2,1)S(1)}, u32[]{:S(2)}, u32[]{:S(2)}) %collective-permute-start.12) | collective-permute-done | bytes 188448 | tf_op jit(solution)/shard_map/ppermute | solution.py:1131
  49.3 5.4 %collective-permute-done.13 = bf16[8,184,128]{2,1,0:T(8,128)(2,1)S(1)} collective-permute-done((bf16[8,184,128]{2,1,0:T(8,128)(2,1)S(1)}, bf16[8,184,128]{2,1,0:T(8,128)(2,1)S(1)}, u32[]{:S(2)}, u32[]{:S(2)}) %collective-permute-start.13) | collective-permute-done | bytes 376864 | tf_op jit(solution)/shard_map/ppermute | solution.py:1131
  56.3 6.2 %shard_map.277 = (bf16[320,320]{1,0:T(8,128)(2,1)S(1)}, bf16[640,320]{1,0:T(8,128)(2,1)S(1)}, bf16[320,1280]{1,0:T(8,128)(2,1)S(1)}, bf16[320,320]{1,0:T(8,128)(...) custom-call(s32[2]{0:T(128)S(1)} %copy-done.9, ...), custom_call_target="tpu_custom_call" | custom-call | flops 8000000000 | bytes 1000 | tf_op jit(solution)/shard_map/pallas_call | solution.py:1110
  62.5 4.1 %shard_map.281 = (bf16[320,1024]{1,0:T(8,128)(2,1)S(1)}, f32[5,1,1024]{2,1,0:T(1,128)S(1)}) custom-call(s32[2]{0:T(128)S(1)} %copy-done.9, bf16[5,256,64]{2,1,0:T(8,128)(2,1)S(1)} %get-tuple-element.91.kt, bf16[320,1024]{1,0:T(8,128)(2,1)S(1)} %get-tuple-element.92.qs, bf16[640,256]{1,0:T(8,128)(2,1)S(1)} %get-tuple-element.93.kv), custom_call_target="tpu_custom_call" | custom-call | flops 8499999744 | bytes 1000 | tf_op jit(solution)/shard_map/pallas_call | solution.py:1110
  68.2 2.6 %shard_map.280 = (bf16[1280,384]{1,0:T(8,128)(2,1)S(1)}, bf16[320,1280]{1,0:T(8,128)(2,1)S(1)}, bf16[320,1280]{1,0:T(8,128)(2,1)S(1)}, bf16[1280,320]{1,0:T(8,128)(2,1)S(1)}, f32[10,1280,128]{2,1,0:T(8,128)S(1)}) custom-call(s32[2]{0:T(128)S(1)} %copy-done.9, f32[64,128]{1,0:T(8,128)S(1)} %get-tuple-element.86.bt, ...), custom_call_target="tpu_custom_call" | custom-call | flops 8000000000 | bytes 1000 | tf_op jit(solution)/shard_map/pallas_call | solution.py:1110
  70.9 10.0 %shard_map.283 = (bf16[1280,1024]{1,0:T(8,128)(2,1)S(1)}, bf16[1280,1024]{1,0:T(8,128)(2,1)S(1)}) custom-call(s32[2]{0:T(128)S(1)} %copy-done.9, bf16[1280,384]{1,0:T(8,128)(2,1)S(1)} %get-tuple-element.88.w1, f32[10,1280,128]{2,1,0:T(8,128)S(1)} %get-tuple-element.89.taps, bf16[384,1024]{1,0:T(8,128)(2,1)S(1)} %get-tuple-element.95.sec), custom_call_target="tpu_custom_call" | custom-call | flops 16999999488 | bytes 1000 | tf_op jit(solution)/shard_map/pallas_call | solution.py:1110
  83.1 9.0 %shard_map.285 = (bf16[512,256]{1,0:T(8,128)(2,1)}, bf16[16,368,128]{2,1,0:T(8,128)(2,1)S(1)}, bf16[16,368,128]{2,1,0:T(8,128)(2,1)S(1)}, f32[320,1024]{1,0:T(8,...) custom-call(s32[2]{0:T(128)S(1)} %copy-done.9, f32[64,128]{1,0:T(8,128)S(1)} %get-tuple-element.86.bt, ...), custom_call_target="tpu_custom_call" | custom-call | flops 20000000000 | bytes 1000 | tf_op jit(solution)/shard_map/pallas_call | solution.py:1110
  92.1 4.6 %shard_map.286 = (bf16[256,1024]{1,0:T(8,128)(2,1)S(1)}, f32[256,128]{1,0:T(8,128)S(1)}) custom-call(s32[2]{0:T(128)S(1)} %copy-done.9, bf16[1280,384]{1,0:T(8,128)(2,1)S(1)} %get-tuple-element.88.w1, bf16[1280,320]{1,0:T(8,128)(2,1)S(1)} %get-tuple-element.116.w2t, f32[10,1280,128]{2,1,0:T(8,128)S(1)} %get-tuple-element.89.taps, ...), custom_call_target="tpu_custom_call" | custom-call | flops 6000000000 | bytes 1000 | tf_op jit(solution)/shard_map/pallas_call | solution.py:1110
  96.7 15.6 %shard_map.287 = (bf16[1024,1024]{1,0:T(8,128)(2,1)S(1)}, f32[1024,128]{1,0:T(8,128)S(1)}) custom-call(s32[2]{0:T(128)S(1)} %copy-done.9, bf16[1280,384]{1,0:T(8,128)(2,1)S(1)} %get-tuple-element.88.w1, bf16[1280,320]{1,0:T(8,128)(2,1)S(1)} %get-tuple-element.116.w2t, f32[10,1280,128]{2,1,0:T(8,128)S(1)} %get-tuple-element.89.taps, ...), custom_call_target="tpu_custom_call" | custom-call | flops 24000000000 | bytes 1000 | tf_op jit(solution)/shard_map/pallas_call | solution.py:1110
  114.7 5.2 %shard_map.290 = (bf16[16,224,128]{2,1,0:T(8,128)(2,1)S(1)}, bf16[16,224,128]{2,1,0:T(8,128)(2,1)S(1)}, f32[64,128]{1,0:T(8,128)S(1)}) custom-call(s32[2]{0:T(128)S(1)} %copy-done.9, bf16[320,320]{1,0:T(8,128)(2,1)S(1)} %get-tuple-element.103.to_tens, bf16[256,1024]{1,0:T(8,128)(2,1)S(1)} %get-tuple-element.119.hg0, ...), custom_call_target="tpu_custom_call" | custom-call | flops 8999999488 | bytes 1000 | tf_op jit(solution)/shard_map/pallas_call | solution.py:1110
  119.9 6.2 %shard_map.289 = (bf16[320,1024]{1,0:T(8,128)(2,1)S(1)}, bf16[640,256]{1,0:T(8,128)(2,1)S(1)}) custom-call(s32[2]{0:T(128)S(1)} %copy-done.9, bf16[5,256,64]{2,1,0:T(8,128)(2,1)S(1)} %get-tuple-element.91.kt, bf16[5,256,64]{2,1,0:T(8,128)(2,1)S(1)} %get-tuple-element.114.vt, bf16[320,1024]{1,0:T(8,128)(2,1)S(1)} %get-tuple-element.92.qs, ...), custom_call_target="tpu_custom_call" | custom-call | flops 8999999488 | bytes 1000 | tf_op jit(solution)/shard_map/pallas_call | solution.py:1110
  126.1 5.9 %shard_map.291 = (bf16[16,208,128]{2,1,0:T(8,128)(2,1)S(1)}, bf16[16,208,128]{2,1,0:T(8,128)(2,1)S(1)}, f32[320,1024]{1,0:T(8,128)S(1)}) custom-call(s32[2]{0:T(128)S(1)} %copy-done.9, f32[64,128]{1,0:T(8,128)S(1)} %get-tuple-element.86.bt, bf16[320,320]{1,0:T(8,128)(2,1)S(1)} %get-tuple-element.103.to_tens, ...), custom_call_target="tpu_custom_call" | custom-call | flops 11000000512 | bytes 1000 | tf_op jit(solution)/shard_map/pallas_call | solution.py:1110
  133.1 5.3 %shard_map.292 = f32[320,1024]{1,0:T(8,128)} custom-call(s32[2]{0:T(128)S(1)} %copy-done.9, f32[64,128]{1,0:T(8,128)S(1)} %get-tuple-element.86.bt, bf16[1024,1024]{1,0:T(8,128)(2,1)S(1)} %get-tuple-element.102.turned, f32[320,1024]{1,0:T(8,128)S(1)} %get-tuple-element.132.grad_in, f32[320,1024]{1,0:T(8,128)S(1)} %get-tuple-element.133.mid_grad, ...), custom_call_target="tpu_custom_call" | custom-call | flops 5000000000 | bytes 1000 | tf_op jit(solution)/shard_map/pallas_call | solution.py:1110
  143.3 3.5 %collective-permute-done.24 = bf16[8,104,128]{2,1,0:T(8,128)(2,1)S(1)} collective-permute-done((bf16[8,104,128]{2,1,0:T(8,128)(2,1)S(1)}, bf16[8,104,128]{2,1,0:T(8,128)(2,1)S(1)}, u32[]{:S(2)}, u32[]{:S(2)}) %collective-permute-start.24) | collective-permute-done | bytes 213024 | tf_op jit(solution)/shard_map/ppermute | solution.py:1131
  149.1 2.7 %collective-permute-done.32 = bf16[8,112,128]{2,1,0:T(8,128)(2,1)S(1)} collective-permute-done((bf16[8,112,128]{2,1,0:T(8,128)(2,1)S(1)}, bf16[8,112,128]{2,1,0:T(8,128)(2,1)S(1)}, u32[]{:S(2)}, u32[]{:S(2)}) %collective-permute-start.32) | collective-permute-done | bytes 229408 | tf_op jit(solution)/shard_map/ppermute | solution.py:1131
  154.6 3.6 %collective-permute-start.30 = (bf16[1,208,128]{2,1,0:T(8,128)(2,1)S(1)}, bf16[1,208,128]{2,1,0:T(8,128)(2,1)S(1)}, u32[]{:S(2)}, u32[]{:S(2)}) collective-permute-start(bf16[1,208,128]{2,1,0:T(8,128)(2,1)S(1)} %get-tuple-element.160), channel_id=1, source_target_pairs={{0,6},{1,7},{2,4},{3,5},{4,2},{5,3},{6,0},{7,1},{8,14},{9,15},{10,... | collective-permute-start | bytes 159752 | tf_op jit(solution)/shard_map/ppermute | solution.py:1131
  166.3 6.6 %collective-permute-done.40 = bf16[8,184,128]{2,1,0:T(8,128)(2,1)S(1)} collective-permute-done((bf16[8,184,128]{2,1,0:T(8,128)(2,1)S(1)}, bf16[8,184,128]{2,1,0:T(8,128)(2,1)S(1)}, u32[]{:S(2)}, u32[]{:S(2)}) %collective-permute-start.40) | collective-permute-done | bytes 376864 | tf_op jit(solution)/shard_map/ppermute | solution.py:1131
  181.5 2.9 %collective-permute-start.36 = (bf16[1,224,128]{2,1,0:T(8,128)(2,1)S(1)}, bf16[1,224,128]{2,1,0:T(8,128)(2,1)S(1)}, u32[]{:S(2)}, u32[]{:S(2)}) collective-permute-start(bf16[1,224,128]{2,1,0:T(8,128)(2,1)S(1)} %get-tuple-element.152), channel_id=1, source_target_pairs={{0,2},{1,3},{2,0},{3,1},{4,6},{5,7},{6,4},{7,5},{8,10},{9,11},{10,... | collective-permute-start | bytes 172040 | tf_op jit(solution)/shard_map/ppermute | solution.py:1131
  185.9 3.5 %collective-permute-done.44 = bf16[2,368,128]{2,1,0:T(8,128)(2,1)S(1)} collective-permute-done((bf16[2,368,128]{2,1,0:T(8,128)(2,1)S(1)}, bf16[2,368,128]{2,1,0:T(8,128)(2,1)S(1)}, u32[]{:S(2)}, u32[]{:S(2)}) %collective-permute-start.44) | collective-permute-done | bytes 188448 | tf_op jit(solution)/shard_map/ppermute | solution.py:1131
  (189 shorter events, 68.8 us)
Async XLA Ops:
  6.0 15.8 %collective-permute-start.2 = (bf16[1,208,128]{2,1,0:T(8,128)(2,1)}, bf16[1,208,128]{2,1,0:T(8,128)(2,1)S(1)}, u32[]{:S(2)}, u32[]{:S(2)}) collective-permute-start(bf16[1,208,128]{2,1,0:T(8,128)(2,1)} %bitcast.106), channel_id=1, source_target_pairs={{0,6},{1,7},{2,4},{3,5},{4,2},{5,3},{6,0},{7,1},{8,14},{9,15},{10,... | collective-permute-start | bytes 159752 | tf_op jit(solution)/shard_map/ppermute | solution.py:1131
  11.2 11.4 %collective-permute-start.1 = (bf16[1,208,128]{2,1,0:T(8,128)(2,1)}, bf16[1,208,128]{2,1,0:T(8,128)(2,1)S(1)}, u32[]{:S(2)}, u32[]{:S(2)}) collective-permute-start(bf16[1,208,128]{2,1,0:T(8,128)(2,1)} %bitcast.107), channel_id=1, source_target_pairs={{0,4},{1,5},{2,6},{3,7},{4,0},{5,1},{6,2},{7,3},{8,12},{9,13},{10,... | collective-permute-start | bytes 159752 | tf_op jit(solution)/shard_map/ppermute | solution.py:1131
  11.2 12.8 %collective-permute-start = (bf16[1,208,128]{2,1,0:T(8,128)(2,1)}, bf16[1,208,128]{2,1,0:T(8,128)(2,1)S(1)}, u32[]{:S(2)}, u32[]{:S(2)}) collective-permute-start(bf16[1,208,128]{2,1,0:T(8,128)(2,1)} %bitcast.108), channel_id=1, source_target_pairs={{0,2},{1,3},{2,0},{3,1},{4,6},{5,7},{6,4},{7,5},{8,10},{9,11},{10,... | collective-permute-start | bytes 159752 | tf_op jit(solution)/shard_map/ppermute | solution.py:1131
  12.7 12.8 %collective-permute-start.17 = (bf16[1,224,128]{2,1,0:T(8,128)(2,1)S(1)}, bf16[1,224,128]{2,1,0:T(8,128)(2,1)S(1)}, u32[]{:S(2)}, u32[]{:S(2)}) collective-permute-start(bf16[1,224,128]{2,1,0:T(8,128)(2,1)S(1)} %bitcast.91), channel_id=1, source_target_pairs={{0,6},{1,7},{2,4},{3,5},{4,2},{5,3},{6,0},{7,1},{8,14},{9,15},{10,... | collective-permute-start | bytes 172040 | tf_op jit(solution)/shard_map/ppermute | solution.py:1131
  16.5 10.5 %collective-permute-start.16 = (bf16[1,224,128]{2,1,0:T(8,128)(2,1)S(1)}, bf16[1,224,128]{2,1,0:T(8,128)(2,1)S(1)}, u32[]{:S(2)}, u32[]{:S(2)}) collective-permute-start(bf16[1,224,128]{2,1,0:T(8,128)(2,1)S(1)} %bitcast.92), channel_id=1, source_target_pairs={{0,4},{1,5},{2,6},{3,7},{4,0},{5,1},{6,2},{7,3},{8,12},{9,13},{10,... | collective-permute-start | bytes 172040 | tf_op jit(solution)/shard_map/ppermute | solution.py:1131
  24.0 8.2 %collective-permute-start.3 = (bf16[4,104,128]{2,1,0:T(8,128)(2,1)S(1)}, bf16[4,104,128]{2,1,0:T(8,128)(2,1)S(1)}, u32[]{:S(2)}, u32[]{:S(2)}) collective-permute-start(bf16[4,104,128]{2,1,0:T(8,128)(2,1)S(1)} %get-tuple-element.162), channel_id=1, source_target_pairs={{0,8},{1,9},{2,10},{3,11},{4,12},{5,13},{6,14},{7,15},{8,0},{9,1},... | collective-permute-start | bytes 319496 | tf_op jit(solution)/shard_map/ppermute | solution.py:1131
  29.2 8.6 %collective-permute-start.9 = (bf16[2,368,128]{2,1,0:T(8,128)(2,1)S(1)}, bf16[2,368,128]{2,1,0:T(8,128)(2,1)S(1)}, u32[]{:S(2)}, u32[]{:S(2)}) collective-permute-start(bf16[2,368,128]{2,1,0:T(8,128)(2,1)S(1)} %pad_maximum_fusion.10), channel_id=1, source_target_pairs={{0,4},{1,5},{2,6},{3,7},{4,0},{5,1},{6,2},{7,3},{8,12},{9,13},{10,... | collective-permute-start | bytes 565256 | tf_op jit(solution)/shard_map/ppermute | solution.py:1131
  32.2 10.0 %collective-permute-start.4 = (bf16[8,104,128]{2,1,0:T(8,128)(2,1)S(1)}, bf16[8,104,128]{2,1,0:T(8,128)(2,1)S(1)}, u32[]{:S(2)}, u32[]{:S(2)}) collective-permute-start(bf16[8,104,128]{2,1,0:T(8,128)(2,1)S(1)} %pad_maximum_fusion.7), channel_id=1, source_target_pairs={{0,16},{1,17},{2,18},{3,19},{4,20},{5,21},{6,22},{7,23},{8,24},{9,... | collective-permute-start | bytes 638984 | tf_op jit(solution)/shard_map/ppermute | solution.py:1131
  32.9 8.1 %collective-permute-start.6 = (bf16[8,104,128]{2,1,0:T(8,128)(2,1)S(1)}, bf16[8,104,128]{2,1,0:T(8,128)(2,1)S(1)}, u32[]{:S(2)}, u32[]{:S(2)}) collective-permute-start(bf16[8,104,128]{2,1,0:T(8,128)(2,1)S(1)} %pad_maximum_fusion.8), channel_id=1, source_target_pairs={{0,8},{1,9},{2,10},{3,11},{4,12},{5,13},{6,14},{7,15},{8,0},{9,1},... | collective-permute-start | bytes 638984 | tf_op jit(solution)/shard_map/ppermute | solution.py:1131
  34.5 14.7 %collective-permute-start.19 = (bf16[8,112,128]{2,1,0:T(8,128)(2,1)S(1)}, bf16[8,112,128]{2,1,0:T(8,128)(2,1)S(1)}, u32[]{:S(2)}, u32[]{:S(2)}) collective-permute-start(bf16[8,112,128]{2,1,0:T(8,128)(2,1)S(1)} %pad_maximum_fusion.4), channel_id=1, source_target_pairs={{0,16},{1,17},{2,18},{3,19},{4,20},{5,21},{6,22},{7,23},{8,24},{9,... | collective-permute-start | bytes 688136 | tf_op jit(solution)/shard_map/ppermute | solution.py:1131
  35.1 13.3 %collective-permute-start.21 = (bf16[8,112,128]{2,1,0:T(8,128)(2,1)S(1)}, bf16[8,112,128]{2,1,0:T(8,128)(2,1)S(1)}, u32[]{:S(2)}, u32[]{:S(2)}) collective-permute-start(bf16[8,112,128]{2,1,0:T(8,128)(2,1)S(1)} %pad_maximum_fusion.5), channel_id=1, source_target_pairs={{0,8},{1,9},{2,10},{3,11},{4,12},{5,13},{6,14},{7,15},{8,0},{9,1},... | collective-permute-start | bytes 688136 | tf_op jit(solution)/shard_map/ppermute | solution.py:1131
  38.0 10.4 %collective-permute-start.10 = (bf16[4,184,128]{2,1,0:T(8,128)(2,1)S(1)}, bf16[4,184,128]{2,1,0:T(8,128)(2,1)S(1)}, u32[]{:S(2)}, u32[]{:S(2)}) collective-permute-start(bf16[4,184,128]{2,1,0:T(8,128)(2,1)S(1)} %get-tuple-element.148), channel_id=1, source_target_pairs={{0,8},{1,9},{2,10},{3,11},{4,12},{5,13},{6,14},{7,15},{8,0},{9,1},... | collective-permute-start | bytes 565256 | tf_op jit(solution)/shard_map/ppermute | solution.py:1131
  42.3 13.9 %collective-permute-start.7 = (bf16[16,208,128]{2,1,0:T(8,128)(2,1)S(1)}, bf16[16,208,128]{2,1,0:T(8,128)(2,1)S(1)}, u32[]{:S(2)}, u32[]{:S(2)}) collective-permute-start(bf16[16,208,128]{2,1,0:T(8,128)(2,1)S(1)} %maximum_maximum_fusion.2.low), channel_id=1, source_target_pairs={{0,1},{1,0},{2,3},{3,2},{4,5},{5,4},{6,7},{7,6},{8,9},{9,8},{10,11... | collective-permute-start | bytes 2555912 | tf_op jit(solution)/shard_map/ppermute | solution.py:1131
  49.2 19.0 %collective-permute-start.22 = (bf16[16,224,128]{2,1,0:T(8,128)(2,1)S(1)}, bf16[16,224,128]{2,1,0:T(8,128)(2,1)S(1)}, u32[]{:S(2)}, u32[]{:S(2)}) collective-permute-start(bf16[16,224,128]{2,1,0:T(8,128)(2,1)S(1)} %maximum_maximum_fusion.1.low), channel_id=1, source_target_pairs={{0,1},{1,0},{2,3},{3,2},{4,5},{5,4},{6,7},{7,6},{8,9},{9,8},{10,11... | collective-permute-start | bytes 2752520 | tf_op jit(solution)/shard_map/ppermute | solution.py:1131
  56.2 26.9 %collective-permute-start.14 = (bf16[16,368,128]{2,1,0:T(8,128)(2,1)S(1)}, bf16[16,368,128]{2,1,0:T(8,128)(2,1)S(1)}, u32[]{:S(2)}, u32[]{:S(2)}) collective-permute-start(bf16[16,368,128]{2,1,0:T(8,128)(2,1)S(1)} %maximum_maximum_fusion.c_low), channel_id=1, source_target_pairs={{0,1},{1,0},{2,3},{3,2},{4,5},{5,4},{6,7},{7,6},{8,9},{9,8},{10,11... | collective-permute-start | bytes 4521992 | tf_op jit(solution)/shard_map/ppermute | solution.py:1131
  132.7 31.9 %collective-permute-start.39 = (bf16[16,368,128]{2,1,0:T(8,128)(2,1)S(1)}, bf16[16,368,128]{2,1,0:T(8,128)(2,1)S(1)}, u32[]{:S(2)}, u32[]{:S(2)}) collective-permute-start(bf16[16,368,128]{2,1,0:T(8,128)(2,1)S(1)} %get-tuple-element.145), channel_id=1, source_target_pairs={{0,1},{1,0},{2,3},{3,2},{4,5},{5,4},{6,7},{7,6},{8,9},{9,8},{10,11... | collective-permute-start | bytes 4521992 | tf_op jit(solution)/shard_map/ppermute | solution.py:1131
  138.7 8.2 %collective-permute-start.24 = (bf16[8,104,128]{2,1,0:T(8,128)(2,1)S(1)}, bf16[8,104,128]{2,1,0:T(8,128)(2,1)S(1)}, u32[]{:S(2)}, u32[]{:S(2)}) collective-permute-start(bf16[8,104,128]{2,1,0:T(8,128)(2,1)S(1)} %slice.245), channel_id=1, source_target_pairs={{0,16},{1,17},{2,18},{3,19},{4,20},{5,21},{6,22},{7,23},{8,24},{9,... | collective-permute-start | bytes 638984 | tf_op jit(solution)/shard_map/ppermute | solution.py:1131
  139.4 8.3 %collective-permute-start.26 = (bf16[2,4,104,128]{3,2,1,0:T(8,128)(2,1)S(1)}, bf16[2,4,104,128]{3,2,1,0:T(8,128)(2,1)S(1)}, u32[]{:S(2)}, u32[]{:S(2)}) collective-permute-start(bf16[2,4,104,128]{3,2,1,0:T(8,128)(2,1)S(1)} %slice_bitcast_fusion.4), channel_id=1, source_target_pairs={{0,8},{1,9},{2,10},{3,11},{4,12},{5,13},{6,14},{7,15},{8,0},{9,1},... | collective-permute-start | bytes 638984 | tf_op jit(solution)/shard_map/ppermute | solution.py:1131
  141.0 10.8 %collective-permute-start.32 = (bf16[8,112,128]{2,1,0:T(8,128)(2,1)S(1)}, bf16[8,112,128]{2,1,0:T(8,128)(2,1)S(1)}, u32[]{:S(2)}, u32[]{:S(2)}) collective-permute-start(bf16[8,112,128]{2,1,0:T(8,128)(2,1)S(1)} %slice.260), channel_id=1, source_target_pairs={{0,16},{1,17},{2,18},{3,19},{4,20},{5,21},{6,22},{7,23},{8,24},{9,... | collective-permute-start | bytes 688136 | tf_op jit(solution)/shard_map/ppermute | solution.py:1131
  142.0 10.7 %collective-permute-start.34 = (bf16[2,4,112,128]{3,2,1,0:T(8,128)(2,1)S(1)}, bf16[2,4,112,128]{3,2,1,0:T(8,128)(2,1)S(1)}, u32[]{:S(2)}, u32[]{:S(2)}) collective-permute-start(bf16[2,4,112,128]{3,2,1,0:T(8,128)(2,1)S(1)} %slice_bitcast_fusion.2), channel_id=1, source_target_pairs={{0,8},{1,9},{2,10},{3,11},{4,12},{5,13},{6,14},{7,15},{8,0},{9,1},... | collective-permute-start | bytes 688136 | tf_op jit(solution)/shard_map/ppermute | solution.py:1131
  151.9 14.4 %collective-permute-start.33 = (bf16[4,112,128]{2,1,0:T(8,128)(2,1)S(1)}, bf16[4,112,128]{2,1,0:T(8,128)(2,1)S(1)}, u32[]{:S(2)}, u32[]{:S(2)}) collective-permute-start(bf16[4,112,128]{2,1,0:T(8,128)(2,1)S(1)} %slice.262), channel_id=1, source_target_pairs={{0,8},{1,9},{2,10},{3,11},{4,12},{5,13},{6,14},{7,15},{8,0},{9,1},... | collective-permute-start | bytes 344072 | tf_op jit(solution)/shard_map/ppermute | solution.py:1131
  158.8 22.6 %collective-permute-start.35 = (bf16[4,112,128]{2,1,0:T(8,128)(2,1)S(1)}, bf16[4,112,128]{2,1,0:T(8,128)(2,1)S(1)}, u32[]{:S(2)}, u32[]{:S(2)}) collective-permute-start(bf16[4,112,128]{2,1,0:T(8,128)(2,1)S(1)} %slice_bitcast_fusion.8), channel_id=1, source_target_pairs={{0,16},{1,17},{2,18},{3,19},{4,20},{5,21},{6,22},{7,23},{8,24},{9,... | collective-permute-start | bytes 344072 | tf_op jit(solution)/shard_map/ppermute | solution.py:1131
  165.8 9.7 %collective-permute-start.42 = (bf16[2,4,184,128]{3,2,1,0:T(8,128)(2,1)S(1)}, bf16[2,4,184,128]{3,2,1,0:T(8,128)(2,1)S(1)}, u32[]{:S(2)}, u32[]{:S(2)}) collective-permute-start(bf16[2,4,184,128]{3,2,1,0:T(8,128)(2,1)S(1)} %slice_bitcast_fusion), channel_id=1, source_target_pairs={{0,8},{1,9},{2,10},{3,11},{4,12},{5,13},{6,14},{7,15},{8,0},{9,1},... | collective-permute-start | bytes 1130504 | tf_op jit(solution)/shard_map/ppermute | solution.py:1131
  181.5 8.7 %collective-permute-start.36 = (bf16[1,224,128]{2,1,0:T(8,128)(2,1)S(1)}, bf16[1,224,128]{2,1,0:T(8,128)(2,1)S(1)}, u32[]{:S(2)}, u32[]{:S(2)}) collective-permute-start(bf16[1,224,128]{2,1,0:T(8,128)(2,1)S(1)} %get-tuple-element.152), channel_id=1, source_target_pairs={{0,2},{1,3},{2,0},{3,1},{4,6},{5,7},{6,4},{7,5},{8,10},{9,11},{10,... | collective-permute-start | bytes 172040 | tf_op jit(solution)/shard_map/ppermute | solution.py:1131
  (40 other events, 241.4 us)

commit v4 on v3

--- a/solution.py
+++ b/solution.py
@@ -388,12 +388,13 @@
     for half, source in enumerate((low, high)):
 
         def chunk(c, half=half, source=source):
-            block = source[:, pl.ds(pl.multiple_of(16 * c, 16), 16), :].astype(F32)
+            block = source[:, 16 * c : 16 * c + 16, :].astype(F32)
             rows = slice(128 * half, 128 * half + 128)
             wrs[rows, lanes(c)] = block[:, 0:8].reshape(128, 128).astype(BF16)
             square[rows, lanes(c)] = block[:, 8:16].reshape(128, 128).astype(BF16)
 
-        loop(10, chunk)
+        for c in range(10):
+            chunk(c)
         block = source[:, 160:208, :].astype(F32)
         for c in range(5):
             part = block[:, 8 * c : 8 * c + 8].reshape(128, 128).astype(BF16)
@@ -404,7 +405,8 @@
         wrs[256:320, lanes(p, 256)] = jnp.concatenate([part[0:64], part[64:128]], axis=1)
         square[256:320, lanes(p, 256)] = jnp.concatenate([part[128:192], part[192:256]], axis=1)
 
-    loop(5, last_two)
+    for p in range(5):
+        last_two(p)
     wq[:, 0:256] = dot(from_tens[...], square[:, 0:256]).astype(BF16)
     wo[:, 0:256] = dot(from_tens[...], square[:, 1024:1280]).astype(BF16)
     tails = dot(from_tens[...], square[:, 768:1024])
@@ -420,7 +422,8 @@
         centred = entry[:, lanes(tile)].astype(F32) - stats[0:1, lanes(tile)]
         first[:, lanes(tile)] = (centred * stats[1:2, lanes(tile)] * gain + shift).astype(BF16)
 
-    loop(8, body)
+    for tile in range(8):
+        body(tile)
     for quad in range(4):
         redin[D * quad : D * quad + D, :] = first[:, 256 * quad : 256 * quad + 256]
     bias = column(bt, B_Q, 5)
@@ -692,10 +695,11 @@
     for half, source in enumerate((c_low, c_high)):
 
         def place(c, half=half, source=source):
-            block = source[:, pl.ds(pl.multiple_of(16 * c, 16), 16), :].reshape(256, 128)
+            block = source[:, 16 * c : 16 * c + 16, :].reshape(256, 128)
             wm[256 * half : 256 * half + 256, lanes(c)] = block
 
-        loop(23, place)
+        for c in range(23):
+            place(c)
 
     def reorder(to_owner):
         def one(slot):

time: 196 us -> 193 us (0.985)
  Pallas kernels: 93.4 us -> 90.4 us
    pallas_call x19, Pallas kernels: 88.9 us -> 86 us  [call(): pl.pallas_call(kernel, in_specs=[pl.BlockSpec(memory_space=pltpu.SMEM if...]
  transfers between devices with their start and end apart: 46 -> 46, of which waited for: 18 -> 18; matrix products, arithmetic and copies ran while one was open for 2% -> 2% of each run, Pallas kernels for 21% -> 20%
where the time goes in v4:
time: 193 us
  Pallas kernels  90.4 us (47%)
  starting transfers between devices  51.5 us (27%)
  waiting for transfers between devices  42.9 us (22%)
  other arithmetic  2.85 us (1%)
  local copies, waits for them, and re-layouts  2.73 us (1%)
  between operations  2.07 us (1%)
    pallas_call x19, Pallas kernels, call(): pl.pallas_call(kernel, in_specs=[pl.BlockSpec(memory_space=pltpu.SMEM if...  86 us
    ppermute x46, starting transfers between devices, flip(): return lax.ppermute(values, axes, pairs)  51.5 us
    ppermute x46, waiting for transfers between devices, flip(): return lax.ppermute(values, axes, pairs)  42.9 us
    pallas_call x3, Pallas kernels, select(): pl.pallas_call(functools.partial(select_kernel, len(sources), tuple(bases...  4.43 us
  transfers between devices with their start and end apart: 46, of which 18 were waited for; matrix products, arithmetic and copies ran while one was open for 2% of the time, Pallas kernels for 20%

profile of v4, /device:TPU:0, one launch (start us, length us, event | category | flops | bytes accessed | tf_op | source)
XLA Modules:
  0.0 192.5 jit_solution(12124371610078368125)
XLA Ops:
  3.1 2.9 %shard_map.275 = bf16[208,128]{1,0:T(8,128)(2,1)} custom-call(bf16[25,128]{1,0:T(8,128)(2,1)} %bitcast.112, bf16[25,128]{1,0:T(8,128)(2,1)} %bitcast.113, bf16[50,128]{1,0:T(8,128)(2,1)} %bitcast.111, bf16[100,128]{1,0:T(8,128)(2,1)} %bitcast.110, s32[2]{0:T(128)} %pad_add_fusion.scal.refs_4_, bf16[1,192]{1,0:T(2,128)(2,1)} %broadcast_in_dim.21.refs_5_, ...), custom_call_target="tpu_custom_call" | custom-call | flops 2000000000 | bytes 1000 | tf_op jit(solution)/shard_map/pallas_call | solution.py:150
  6.0 5.1 %collective-permute-start.2 = (bf16[1,208,128]{2,1,0:T(8,128)(2,1)}, bf16[1,208,128]{2,1,0:T(8,128)(2,1)S(1)}, u32[]{:S(2)}, u32[]{:S(2)}) collective-permute-start(bf16[1,208,128]{2,1,0:T(8,128)(2,1)} %bitcast.106), channel_id=1, source_target_pairs={{0,6},{1,7},{2,4},{3,5},{4,2},{5,3},{6,0},{7,1},{8,14},{9,15},{10,... | collective-permute-start | bytes 159752 | tf_op jit(solution)/shard_map/ppermute | solution.py:1135
  12.7 3.8 %collective-permute-start.17 = (bf16[1,224,128]{2,1,0:T(8,128)(2,1)S(1)}, bf16[1,224,128]{2,1,0:T(8,128)(2,1)S(1)}, u32[]{:S(2)}, u32[]{:S(2)}) collective-permute-start(bf16[1,224,128]{2,1,0:T(8,128)(2,1)S(1)} %bitcast.91), channel_id=1, source_target_pairs={{0,6},{1,7},{2,4},{3,5},{4,2},{5,3},{6,0},{7,1},{8,14},{9,15},{10,... | collective-permute-start | bytes 172040 | tf_op jit(solution)/shard_map/ppermute | solution.py:1135
  18.3 2.5 %shard_map.276 = (bf16[320,1024]{1,0:T(8,128)(2,1)S(1)}, f32[8,1024]{1,0:T(8,128)S(1)}, bf16[1024,1024]{1,0:T(8,128)(2,1)S(1)}) custom-call(s32[2]{0:T(128)S(1)} %copy-done.9, bf16[320,1024]{1,0:T(8,128)(2,1)S(1)} %bitcast.95), custom_call_target="tpu_custom_call" | custom-call | flops 3500000000 | bytes 1000 | tf_op jit(solution)/shard_map/pallas_call | solution.py:1114
  29.2 3.0 %collective-permute-start.9 = (bf16[2,368,128]{2,1,0:T(8,128)(2,1)S(1)}, bf16[2,368,128]{2,1,0:T(8,128)(2,1)S(1)}, u32[]{:S(2)}, u32[]{:S(2)}) collective-permute-start(bf16[2,368,128]{2,1,0:T(8,128)(2,1)S(1)} %pad_maximum_fusion.10), channel_id=1, source_target_pairs={{0,4},{1,5},{2,6},{3,7},{4,0},{5,1},{6,2},{7,3},{8,12},{9,13},{10,... | collective-permute-start | bytes 565256 | tf_op jit(solution)/shard_map/ppermute | solution.py:1135
  42.4 4.5 %collective-permute-done.12 = bf16[4,184,128]{2,1,0:T(8,128)(2,1)S(1)} collective-permute-done((bf16[4,184,128]{2,1,0:T(8,128)(2,1)S(1)}, bf16[4,184,128]{2,1,0:T(8,128)(2,1)S(1)}, u32[]{:S(2)}, u32[]{:S(2)}) %collective-permute-start.12) | collective-permute-done | bytes 188448 | tf_op jit(solution)/shard_map/ppermute | solution.py:1135
  49.3 5.4 %collective-permute-done.13 = bf16[8,184,128]{2,1,0:T(8,128)(2,1)S(1)} collective-permute-done((bf16[8,184,128]{2,1,0:T(8,128)(2,1)S(1)}, bf16[8,184,128]{2,1,0:T(8,128)(2,1)S(1)}, u32[]{:S(2)}, u32[]{:S(2)}) %collective-permute-start.13) | collective-permute-done | bytes 376864 | tf_op jit(solution)/shard_map/ppermute | solution.py:1135
  56.3 4.2 %shard_map.277 = (bf16[320,320]{1,0:T(8,128)(2,1)S(1)}, bf16[640,320]{1,0:T(8,128)(2,1)S(1)}, bf16[320,1280]{1,0:T(8,128)(2,1)S(1)}, bf16[320,320]{1,0:T(8,128)(...) custom-call(s32[2]{0:T(128)S(1)} %copy-done.9, ...), custom_call_target="tpu_custom_call" | custom-call | flops 8000000000 | bytes 1000 | tf_op jit(solution)/shard_map/pallas_call | solution.py:1114
  60.5 4.1 %shard_map.281 = (bf16[320,1024]{1,0:T(8,128)(2,1)S(1)}, f32[5,1,1024]{2,1,0:T(1,128)S(1)}) custom-call(s32[2]{0:T(128)S(1)} %copy-done.9, bf16[5,256,64]{2,1,0:T(8,128)(2,1)S(1)} %get-tuple-element.91.kt, bf16[320,1024]{1,0:T(8,128)(2,1)S(1)} %get-tuple-element.92.qs, bf16[640,256]{1,0:T(8,128)(2,1)S(1)} %get-tuple-element.93.kv), custom_call_target="tpu_custom_call" | custom-call | flops 8499999744 | bytes 1000 | tf_op jit(solution)/shard_map/pallas_call | solution.py:1114
  68.7 10.2 %shard_map.283 = (bf16[1280,1024]{1,0:T(8,128)(2,1)S(1)}, bf16[1280,1024]{1,0:T(8,128)(2,1)S(1)}) custom-call(s32[2]{0:T(128)S(1)} %copy-done.9, bf16[1280,384]{1,0:T(8,128)(2,1)S(1)} %get-tuple-element.88.w1, f32[10,1280,128]{2,1,0:T(8,128)S(1)} %get-tuple-element.89.taps, bf16[384,1024]{1,0:T(8,128)(2,1)S(1)} %get-tuple-element.95.sec), custom_call_target="tpu_custom_call" | custom-call | flops 16999999488 | bytes 1000 | tf_op jit(solution)/shard_map/pallas_call | solution.py:1114
  81.1 8.3 %shard_map.285 = (bf16[512,256]{1,0:T(8,128)(2,1)}, bf16[16,368,128]{2,1,0:T(8,128)(2,1)S(1)}, bf16[16,368,128]{2,1,0:T(8,128)(2,1)S(1)}, f32[320,1024]{1,0:T(8,...) custom-call(s32[2]{0:T(128)S(1)} %copy-done.9, f32[64,128]{1,0:T(8,128)S(1)} %get-tuple-element.86.bt, ...), custom_call_target="tpu_custom_call" | custom-call | flops 20000000000 | bytes 1000 | tf_op jit(solution)/shard_map/pallas_call | solution.py:1114
  89.4 4.6 %shard_map.286 = (bf16[256,1024]{1,0:T(8,128)(2,1)S(1)}, f32[256,128]{1,0:T(8,128)S(1)}) custom-call(s32[2]{0:T(128)S(1)} %copy-done.9, bf16[1280,384]{1,0:T(8,128)(2,1)S(1)} %get-tuple-element.88.w1, bf16[1280,320]{1,0:T(8,128)(2,1)S(1)} %get-tuple-element.116.w2t, f32[10,1280,128]{2,1,0:T(8,128)S(1)} %get-tuple-element.89.taps, ...), custom_call_target="tpu_custom_call" | custom-call | flops 6000000000 | bytes 1000 | tf_op jit(solution)/shard_map/pallas_call | solution.py:1114
  93.9 15.4 %shard_map.287 = (bf16[1024,1024]{1,0:T(8,128)(2,1)S(1)}, f32[1024,128]{1,0:T(8,128)S(1)}) custom-call(s32[2]{0:T(128)S(1)} %copy-done.9, bf16[1280,384]{1,0:T(8,128)(2,1)S(1)} %get-tuple-element.88.w1, bf16[1280,320]{1,0:T(8,128)(2,1)S(1)} %get-tuple-element.116.w2t, f32[10,1280,128]{2,1,0:T(8,128)S(1)} %get-tuple-element.89.taps, ...), custom_call_target="tpu_custom_call" | custom-call | flops 24000000000 | bytes 1000 | tf_op jit(solution)/shard_map/pallas_call | solution.py:1114
  111.8 5.4 %shard_map.290 = (bf16[16,224,128]{2,1,0:T(8,128)(2,1)S(1)}, bf16[16,224,128]{2,1,0:T(8,128)(2,1)S(1)}, f32[64,128]{1,0:T(8,128)S(1)}) custom-call(s32[2]{0:T(128)S(1)} %copy-done.9, bf16[320,320]{1,0:T(8,128)(2,1)S(1)} %get-tuple-element.103.to_tens, bf16[256,1024]{1,0:T(8,128)(2,1)S(1)} %get-tuple-element.119.hg0, ...), custom_call_target="tpu_custom_call" | custom-call | flops 8999999488 | bytes 1000 | tf_op jit(solution)/shard_map/pallas_call | solution.py:1114
  117.2 6.2 %shard_map.289 = (bf16[320,1024]{1,0:T(8,128)(2,1)S(1)}, bf16[640,256]{1,0:T(8,128)(2,1)S(1)}) custom-call(s32[2]{0:T(128)S(1)} %copy-done.9, bf16[5,256,64]{2,1,0:T(8,128)(2,1)S(1)} %get-tuple-element.91.kt, bf16[5,256,64]{2,1,0:T(8,128)(2,1)S(1)} %get-tuple-element.114.vt, bf16[320,1024]{1,0:T(8,128)(2,1)S(1)} %get-tuple-element.92.qs, ...), custom_call_target="tpu_custom_call" | custom-call | flops 8999999488 | bytes 1000 | tf_op jit(solution)/shard_map/pallas_call | solution.py:1114
  123.4 5.9 %shard_map.291 = (bf16[16,208,128]{2,1,0:T(8,128)(2,1)S(1)}, bf16[16,208,128]{2,1,0:T(8,128)(2,1)S(1)}, f32[320,1024]{1,0:T(8,128)S(1)}) custom-call(s32[2]{0:T(128)S(1)} %copy-done.9, f32[64,128]{1,0:T(8,128)S(1)} %get-tuple-element.86.bt, bf16[320,320]{1,0:T(8,128)(2,1)S(1)} %get-tuple-element.103.to_tens, ...), custom_call_target="tpu_custom_call" | custom-call | flops 11000000512 | bytes 1000 | tf_op jit(solution)/shard_map/pallas_call | solution.py:1114
  130.4 5.0 %shard_map.292 = f32[320,1024]{1,0:T(8,128)} custom-call(s32[2]{0:T(128)S(1)} %copy-done.9, f32[64,128]{1,0:T(8,128)S(1)} %get-tuple-element.86.bt, bf16[1024,1024]{1,0:T(8,128)(2,1)S(1)} %get-tuple-element.102.turned, f32[320,1024]{1,0:T(8,128)S(1)} %get-tuple-element.132.grad_in, f32[320,1024]{1,0:T(8,128)S(1)} %get-tuple-element.133.mid_grad, ...), custom_call_target="tpu_custom_call" | custom-call | flops 5000000000 | bytes 1000 | tf_op jit(solution)/shard_map/pallas_call | solution.py:1114
  140.4 3.5 %collective-permute-done.24 = bf16[8,104,128]{2,1,0:T(8,128)(2,1)S(1)} collective-permute-done((bf16[8,104,128]{2,1,0:T(8,128)(2,1)S(1)}, bf16[8,104,128]{2,1,0:T(8,128)(2,1)S(1)}, u32[]{:S(2)}, u32[]{:S(2)}) %collective-permute-start.24) | collective-permute-done | bytes 213024 | tf_op jit(solution)/shard_map/ppermute | solution.py:1135
  146.2 2.7 %collective-permute-done.32 = bf16[8,112,128]{2,1,0:T(8,128)(2,1)S(1)} collective-permute-done((bf16[8,112,128]{2,1,0:T(8,128)(2,1)S(1)}, bf16[8,112,128]{2,1,0:T(8,128)(2,1)S(1)}, u32[]{:S(2)}, u32[]{:S(2)}) %collective-permute-start.32) | collective-permute-done | bytes 229408 | tf_op jit(solution)/shard_map/ppermute | solution.py:1135
  151.7 3.6 %collective-permute-start.30 = (bf16[1,208,128]{2,1,0:T(8,128)(2,1)S(1)}, bf16[1,208,128]{2,1,0:T(8,128)(2,1)S(1)}, u32[]{:S(2)}, u32[]{:S(2)}) collective-permute-start(bf16[1,208,128]{2,1,0:T(8,128)(2,1)S(1)} %get-tuple-element.160), channel_id=1, source_target_pairs={{0,6},{1,7},{2,4},{3,5},{4,2},{5,3},{6,0},{7,1},{8,14},{9,15},{10,... | collective-permute-start | bytes 159752 | tf_op jit(solution)/shard_map/ppermute | solution.py:1135
  163.3 6.6 %collective-permute-done.40 = bf16[8,184,128]{2,1,0:T(8,128)(2,1)S(1)} collective-permute-done((bf16[8,184,128]{2,1,0:T(8,128)(2,1)S(1)}, bf16[8,184,128]{2,1,0:T(8,128)(2,1)S(1)}, u32[]{:S(2)}, u32[]{:S(2)}) %collective-permute-start.40) | collective-permute-done | bytes 376864 | tf_op jit(solution)/shard_map/ppermute | solution.py:1135
  175.8 2.5 %collective-permute-done.43 = bf16[4,184,128]{2,1,0:T(8,128)(2,1)S(1)} collective-permute-done((bf16[4,184,128]{2,1,0:T(8,128)(2,1)S(1)}, bf16[4,184,128]{2,1,0:T(8,128)(2,1)S(1)}, u32[]{:S(2)}, u32[]{:S(2)}) %collective-permute-start.43) | collective-permute-done | bytes 188448 | tf_op jit(solution)/shard_map/ppermute | solution.py:1135
  178.5 2.9 %collective-permute-start.36 = (bf16[1,224,128]{2,1,0:T(8,128)(2,1)S(1)}, bf16[1,224,128]{2,1,0:T(8,128)(2,1)S(1)}, u32[]{:S(2)}, u32[]{:S(2)}) collective-permute-start(bf16[1,224,128]{2,1,0:T(8,128)(2,1)S(1)} %get-tuple-element.152), channel_id=1, source_target_pairs={{0,2},{1,3},{2,0},{3,1},{4,6},{5,7},{6,4},{7,5},{8,10},{9,11},{10,... | collective-permute-start | bytes 172040 | tf_op jit(solution)/shard_map/ppermute | solution.py:1135
  182.9 3.5 %collective-permute-done.44 = bf16[2,368,128]{2,1,0:T(8,128)(2,1)S(1)} collective-permute-done((bf16[2,368,128]{2,1,0:T(8,128)(2,1)S(1)}, bf16[2,368,128]{2,1,0:T(8,128)(2,1)S(1)}, u32[]{:S(2)}, u32[]{:S(2)}) %collective-permute-start.44) | collective-permute-done | bytes 188448 | tf_op jit(solution)/shard_map/ppermute | solution.py:1135
  (189 shorter events, 68.7 us)
Async XLA Ops:
  6.0 15.8 %collective-permute-start.2 = (bf16[1,208,128]{2,1,0:T(8,128)(2,1)}, bf16[1,208,128]{2,1,0:T(8,128)(2,1)S(1)}, u32[]{:S(2)}, u32[]{:S(2)}) collective-permute-start(bf16[1,208,128]{2,1,0:T(8,128)(2,1)} %bitcast.106), channel_id=1, source_target_pairs={{0,6},{1,7},{2,4},{3,5},{4,2},{5,3},{6,0},{7,1},{8,14},{9,15},{10,... | collective-permute-start | bytes 159752 | tf_op jit(solution)/shard_map/ppermute | solution.py:1135
  11.2 11.4 %collective-permute-start.1 = (bf16[1,208,128]{2,1,0:T(8,128)(2,1)}, bf16[1,208,128]{2,1,0:T(8,128)(2,1)S(1)}, u32[]{:S(2)}, u32[]{:S(2)}) collective-permute-start(bf16[1,208,128]{2,1,0:T(8,128)(2,1)} %bitcast.107), channel_id=1, source_target_pairs={{0,4},{1,5},{2,6},{3,7},{4,0},{5,1},{6,2},{7,3},{8,12},{9,13},{10,... | collective-permute-start | bytes 159752 | tf_op jit(solution)/shard_map/ppermute | solution.py:1135
  11.2 12.8 %collective-permute-start = (bf16[1,208,128]{2,1,0:T(8,128)(2,1)}, bf16[1,208,128]{2,1,0:T(8,128)(2,1)S(1)}, u32[]{:S(2)}, u32[]{:S(2)}) collective-permute-start(bf16[1,208,128]{2,1,0:T(8,128)(2,1)} %bitcast.108), channel_id=1, source_target_pairs={{0,2},{1,3},{2,0},{3,1},{4,6},{5,7},{6,4},{7,5},{8,10},{9,11},{10,... | collective-permute-start | bytes 159752 | tf_op jit(solution)/shard_map/ppermute | solution.py:1135
  12.7 12.8 %collective-permute-start.17 = (bf16[1,224,128]{2,1,0:T(8,128)(2,1)S(1)}, bf16[1,224,128]{2,1,0:T(8,128)(2,1)S(1)}, u32[]{:S(2)}, u32[]{:S(2)}) collective-permute-start(bf16[1,224,128]{2,1,0:T(8,128)(2,1)S(1)} %bitcast.91), channel_id=1, source_target_pairs={{0,6},{1,7},{2,4},{3,5},{4,2},{5,3},{6,0},{7,1},{8,14},{9,15},{10,... | collective-permute-start | bytes 172040 | tf_op jit(solution)/shard_map/ppermute | solution.py:1135
  16.5 10.5 %collective-permute-start.16 = (bf16[1,224,128]{2,1,0:T(8,128)(2,1)S(1)}, bf16[1,224,128]{2,1,0:T(8,128)(2,1)S(1)}, u32[]{:S(2)}, u32[]{:S(2)}) collective-permute-start(bf16[1,224,128]{2,1,0:T(8,128)(2,1)S(1)} %bitcast.92), channel_id=1, source_target_pairs={{0,4},{1,5},{2,6},{3,7},{4,0},{5,1},{6,2},{7,3},{8,12},{9,13},{10,... | collective-permute-start | bytes 172040 | tf_op jit(solution)/shard_map/ppermute | solution.py:1135
  24.0 8.2 %collective-permute-start.3 = (bf16[4,104,128]{2,1,0:T(8,128)(2,1)S(1)}, bf16[4,104,128]{2,1,0:T(8,128)(2,1)S(1)}, u32[]{:S(2)}, u32[]{:S(2)}) collective-permute-start(bf16[4,104,128]{2,1,0:T(8,128)(2,1)S(1)} %get-tuple-element.162), channel_id=1, source_target_pairs={{0,8},{1,9},{2,10},{3,11},{4,12},{5,13},{6,14},{7,15},{8,0},{9,1},... | collective-permute-start | bytes 319496 | tf_op jit(solution)/shard_map/ppermute | solution.py:1135
  29.2 8.6 %collective-permute-start.9 = (bf16[2,368,128]{2,1,0:T(8,128)(2,1)S(1)}, bf16[2,368,128]{2,1,0:T(8,128)(2,1)S(1)}, u32[]{:S(2)}, u32[]{:S(2)}) collective-permute-start(bf16[2,368,128]{2,1,0:T(8,128)(2,1)S(1)} %pad_maximum_fusion.10), channel_id=1, source_target_pairs={{0,4},{1,5},{2,6},{3,7},{4,0},{5,1},{6,2},{7,3},{8,12},{9,13},{10,... | collective-permute-start | bytes 565256 | tf_op jit(solution)/shard_map/ppermute | solution.py:1135
  32.2 10.0 %collective-permute-start.4 = (bf16[8,104,128]{2,1,0:T(8,128)(2,1)S(1)}, bf16[8,104,128]{2,1,0:T(8,128)(2,1)S(1)}, u32[]{:S(2)}, u32[]{:S(2)}) collective-permute-start(bf16[8,104,128]{2,1,0:T(8,128)(2,1)S(1)} %pad_maximum_fusion.7), channel_id=1, source_target_pairs={{0,16},{1,17},{2,18},{3,19},{4,20},{5,21},{6,22},{7,23},{8,24},{9,... | collective-permute-start | bytes 638984 | tf_op jit(solution)/shard_map/ppermute | solution.py:1135
  32.9 8.1 %collective-permute-start.6 = (bf16[8,104,128]{2,1,0:T(8,128)(2,1)S(1)}, bf16[8,104,128]{2,1,0:T(8,128)(2,1)S(1)}, u32[]{:S(2)}, u32[]{:S(2)}) collective-permute-start(bf16[8,104,128]{2,1,0:T(8,128)(2,1)S(1)} %pad_maximum_fusion.8), channel_id=1, source_target_pairs={{0,8},{1,9},{2,10},{3,11},{4,12},{5,13},{6,14},{7,15},{8,0},{9,1},... | collective-permute-start | bytes 638984 | tf_op jit(solution)/shard_map/ppermute | solution.py:1135
  34.5 14.7 %collective-permute-start.19 = (bf16[8,112,128]{2,1,0:T(8,128)(2,1)S(1)}, bf16[8,112,128]{2,1,0:T(8,128)(2,1)S(1)}, u32[]{:S(2)}, u32[]{:S(2)}) collective-permute-start(bf16[8,112,128]{2,1,0:T(8,128)(2,1)S(1)} %pad_maximum_fusion.4), channel_id=1, source_target_pairs={{0,16},{1,17},{2,18},{3,19},{4,20},{5,21},{6,22},{7,23},{8,24},{9,... | collective-permute-start | bytes 688136 | tf_op jit(solution)/shard_map/ppermute | solution.py:1135
  35.1 13.3 %collective-permute-start.21 = (bf16[8,112,128]{2,1,0:T(8,128)(2,1)S(1)}, bf16[8,112,128]{2,1,0:T(8,128)(2,1)S(1)}, u32[]{:S(2)}, u32[]{:S(2)}) collective-permute-start(bf16[8,112,128]{2,1,0:T(8,128)(2,1)S(1)} %pad_maximum_fusion.5), channel_id=1, source_target_pairs={{0,8},{1,9},{2,10},{3,11},{4,12},{5,13},{6,14},{7,15},{8,0},{9,1},... | collective-permute-start | bytes 688136 | tf_op jit(solution)/shard_map/ppermute | solution.py:1135
  38.0 10.4 %collective-permute-start.10 = (bf16[4,184,128]{2,1,0:T(8,128)(2,1)S(1)}, bf16[4,184,128]{2,1,0:T(8,128)(2,1)S(1)}, u32[]{:S(2)}, u32[]{:S(2)}) collective-permute-start(bf16[4,184,128]{2,1,0:T(8,128)(2,1)S(1)} %get-tuple-element.148), channel_id=1, source_target_pairs={{0,8},{1,9},{2,10},{3,11},{4,12},{5,13},{6,14},{7,15},{8,0},{9,1},... | collective-permute-start | bytes 565256 | tf_op jit(solution)/shard_map/ppermute | solution.py:1135
  42.3 13.9 %collective-permute-start.7 = (bf16[16,208,128]{2,1,0:T(8,128)(2,1)S(1)}, bf16[16,208,128]{2,1,0:T(8,128)(2,1)S(1)}, u32[]{:S(2)}, u32[]{:S(2)}) collective-permute-start(bf16[16,208,128]{2,1,0:T(8,128)(2,1)S(1)} %maximum_maximum_fusion.2.low), channel_id=1, source_target_pairs={{0,1},{1,0},{2,3},{3,2},{4,5},{5,4},{6,7},{7,6},{8,9},{9,8},{10,11... | collective-permute-start | bytes 2555912 | tf_op jit(solution)/shard_map/ppermute | solution.py:1135
  49.2 17.1 %collective-permute-start.22 = (bf16[16,224,128]{2,1,0:T(8,128)(2,1)S(1)}, bf16[16,224,128]{2,1,0:T(8,128)(2,1)S(1)}, u32[]{:S(2)}, u32[]{:S(2)}) collective-permute-start(bf16[16,224,128]{2,1,0:T(8,128)(2,1)S(1)} %maximum_maximum_fusion.1.low), channel_id=1, source_target_pairs={{0,1},{1,0},{2,3},{3,2},{4,5},{5,4},{6,7},{7,6},{8,9},{9,8},{10,11... | collective-permute-start | bytes 2752520 | tf_op jit(solution)/shard_map/ppermute | solution.py:1135
  56.2 24.9 %collective-permute-start.14 = (bf16[16,368,128]{2,1,0:T(8,128)(2,1)S(1)}, bf16[16,368,128]{2,1,0:T(8,128)(2,1)S(1)}, u32[]{:S(2)}, u32[]{:S(2)}) collective-permute-start(bf16[16,368,128]{2,1,0:T(8,128)(2,1)S(1)} %maximum_maximum_fusion.c_low), channel_id=1, source_target_pairs={{0,1},{1,0},{2,3},{3,2},{4,5},{5,4},{6,7},{7,6},{8,9},{9,8},{10,11... | collective-permute-start | bytes 4521992 | tf_op jit(solution)/shard_map/ppermute | solution.py:1135
  130.0 31.6 %collective-permute-start.39 = (bf16[16,368,128]{2,1,0:T(8,128)(2,1)S(1)}, bf16[16,368,128]{2,1,0:T(8,128)(2,1)S(1)}, u32[]{:S(2)}, u32[]{:S(2)}) collective-permute-start(bf16[16,368,128]{2,1,0:T(8,128)(2,1)S(1)} %get-tuple-element.145), channel_id=1, source_target_pairs={{0,1},{1,0},{2,3},{3,2},{4,5},{5,4},{6,7},{7,6},{8,9},{9,8},{10,11... | collective-permute-start | bytes 4521992 | tf_op jit(solution)/shard_map/ppermute | solution.py:1135
  135.7 8.2 %collective-permute-start.24 = (bf16[8,104,128]{2,1,0:T(8,128)(2,1)S(1)}, bf16[8,104,128]{2,1,0:T(8,128)(2,1)S(1)}, u32[]{:S(2)}, u32[]{:S(2)}) collective-permute-start(bf16[8,104,128]{2,1,0:T(8,128)(2,1)S(1)} %slice.245), channel_id=1, source_target_pairs={{0,16},{1,17},{2,18},{3,19},{4,20},{5,21},{6,22},{7,23},{8,24},{9,... | collective-permute-start | bytes 638984 | tf_op jit(solution)/shard_map/ppermute | solution.py:1135
  136.5 8.3 %collective-permute-start.26 = (bf16[2,4,104,128]{3,2,1,0:T(8,128)(2,1)S(1)}, bf16[2,4,104,128]{3,2,1,0:T(8,128)(2,1)S(1)}, u32[]{:S(2)}, u32[]{:S(2)}) collective-permute-start(bf16[2,4,104,128]{3,2,1,0:T(8,128)(2,1)S(1)} %slice_bitcast_fusion.4), channel_id=1, source_target_pairs={{0,8},{1,9},{2,10},{3,11},{4,12},{5,13},{6,14},{7,15},{8,0},{9,1},... | collective-permute-start | bytes 638984 | tf_op jit(solution)/shard_map/ppermute | solution.py:1135
  138.1 10.8 %collective-permute-start.32 = (bf16[8,112,128]{2,1,0:T(8,128)(2,1)S(1)}, bf16[8,112,128]{2,1,0:T(8,128)(2,1)S(1)}, u32[]{:S(2)}, u32[]{:S(2)}) collective-permute-start(bf16[8,112,128]{2,1,0:T(8,128)(2,1)S(1)} %slice.260), channel_id=1, source_target_pairs={{0,16},{1,17},{2,18},{3,19},{4,20},{5,21},{6,22},{7,23},{8,24},{9,... | collective-permute-start | bytes 688136 | tf_op jit(solution)/shard_map/ppermute | solution.py:1135
  139.0 10.7 %collective-permute-start.34 = (bf16[2,4,112,128]{3,2,1,0:T(8,128)(2,1)S(1)}, bf16[2,4,112,128]{3,2,1,0:T(8,128)(2,1)S(1)}, u32[]{:S(2)}, u32[]{:S(2)}) collective-permute-start(bf16[2,4,112,128]{3,2,1,0:T(8,128)(2,1)S(1)} %slice_bitcast_fusion.2), channel_id=1, source_target_pairs={{0,8},{1,9},{2,10},{3,11},{4,12},{5,13},{6,14},{7,15},{8,0},{9,1},... | collective-permute-start | bytes 688136 | tf_op jit(solution)/shard_map/ppermute | solution.py:1135
  148.9 14.4 %collective-permute-start.33 = (bf16[4,112,128]{2,1,0:T(8,128)(2,1)S(1)}, bf16[4,112,128]{2,1,0:T(8,128)(2,1)S(1)}, u32[]{:S(2)}, u32[]{:S(2)}) collective-permute-start(bf16[4,112,128]{2,1,0:T(8,128)(2,1)S(1)} %slice.262), channel_id=1, source_target_pairs={{0,8},{1,9},{2,10},{3,11},{4,12},{5,13},{6,14},{7,15},{8,0},{9,1},... | collective-permute-start | bytes 344072 | tf_op jit(solution)/shard_map/ppermute | solution.py:1135
  155.8 22.6 %collective-permute-start.35 = (bf16[4,112,128]{2,1,0:T(8,128)(2,1)S(1)}, bf16[4,112,128]{2,1,0:T(8,128)(2,1)S(1)}, u32[]{:S(2)}, u32[]{:S(2)}) collective-permute-start(bf16[4,112,128]{2,1,0:T(8,128)(2,1)S(1)} %slice_bitcast_fusion.8), channel_id=1, source_target_pairs={{0,16},{1,17},{2,18},{3,19},{4,20},{5,21},{6,22},{7,23},{8,24},{9,... | collective-permute-start | bytes 344072 | tf_op jit(solution)/shard_map/ppermute | solution.py:1135
  162.8 9.7 %collective-permute-start.42 = (bf16[2,4,184,128]{3,2,1,0:T(8,128)(2,1)S(1)}, bf16[2,4,184,128]{3,2,1,0:T(8,128)(2,1)S(1)}, u32[]{:S(2)}, u32[]{:S(2)}) collective-permute-start(bf16[2,4,184,128]{3,2,1,0:T(8,128)(2,1)S(1)} %slice_bitcast_fusion), channel_id=1, source_target_pairs={{0,8},{1,9},{2,10},{3,11},{4,12},{5,13},{6,14},{7,15},{8,0},{9,1},... | collective-permute-start | bytes 1130504 | tf_op jit(solution)/shard_map/ppermute | solution.py:1135
  178.5 8.7 %collective-permute-start.36 = (bf16[1,224,128]{2,1,0:T(8,128)(2,1)S(1)}, bf16[1,224,128]{2,1,0:T(8,128)(2,1)S(1)}, u32[]{:S(2)}, u32[]{:S(2)}) collective-permute-start(bf16[1,224,128]{2,1,0:T(8,128)(2,1)S(1)} %get-tuple-element.152), channel_id=1, source_target_pairs={{0,2},{1,3},{2,0},{3,1},{4,6},{5,7},{6,4},{7,5},{8,10},{9,11},{10,... | collective-permute-start | bytes 172040 | tf_op jit(solution)/shard_map/ppermute | solution.py:1135
  (40 other events, 240.9 us)
